TPU v7x, 512 devices: a whole 4x8x8 slice. The times are simulated.
512 devices in a mesh: atoms: 64 (over x, z, core), width: 8 (over y).
Axes of the slice: x: 4, y: 8, z: 8, core: 2. Of those that a mesh axis runs over, the one named last changes fastest.
Arguments:
- tokens: bfloat16 [8192, 8192], P('atoms', 'width'), may hold values from -6 to 6
- dec_bias: float32 [8192], P('width'), may hold values from -3 to 3
- encoder: bfloat16 [8192, 8192], P('atoms', 'width'), may hold values from -1.5 to 1.5
- enc_bias: float32 [8192], P('atoms'), may hold values from -24 to 24
- decoder: bfloat16 [8192, 8192], P('atoms', 'width'), may hold values from -0.25 to 0.25
- atom_ids: int32 [8192, 16], P('atoms'), may hold values from 0 to 8191, as said below
- block_count: int32 [64], P('atoms'), may hold values from 1 to 2, as said below
Outputs:
- residual: bfloat16 [8192, 8192], P('atoms', 'width')
- encoder_grad: bfloat16 [8192, 8192], P('atoms', 'width')
- decoder_grad: bfloat16 [8192, 8192], P('atoms', 'width')
- bias_grad: float32 [8192], P('atoms')
Inputs may be any that keep to these rules, and one draw needn't show every extreme that they name: atom_ids[t, 2g] and atom_ids[t, 2g + 1] are two different atom slots of one owner o (slot // 128 = o), both below o * 128 + 64 block_count[o]; the 8 owners of one token differ. Of the 128 tokens of one index of atoms, at most 24 use any one owner, and in every draw some owner is used by exactly 24 tokens of every index of atoms. `block_count`: every draw has an owner with 2 live blocks and one with a single live block.
All inputs are finite; a program needn't handle non-finite values.
Results may differ from a plain program's by a relative error of at most 0.018.
Values may be sent and summed in bfloat16 or wider, within the bound.
No kernel may reach another device: no remote copies, remote signals or barrier semaphores. Data moves between devices by JAX's collectives and lax.ppermute only.
A program may use at most 64 MiB of HBM per device.

v0:
```python
import jax
import jax.numpy as jnp
from jax import lax
from jax.sharding import PartitionSpec as P

BLOCK = 64


coherence = 128.0
loss_grad = 1.0 / 32.0
epsilon = 1e-06


def coherence_weights(raw_rows, norm_rows, norm_all, alive_rows, alive_all):
    row_total, extent = raw_rows.shape
    row_ids = jnp.arange(row_total)[:, None]
    col_ids = jnp.arange(extent)[None, :]
    norm_pair = norm_rows[:, None] * norm_all[None, :]
    cosine = raw_rows / norm_pair
    on_diagonal = row_ids == col_ids
    coupled = jnp.where(on_diagonal, 0.0, alive_rows[:, None] * alive_all[None, :] * cosine)
    spread = jnp.sum(coupled * cosine, axis=1)
    diag_term = jnp.where(on_diagonal, (spread / (norm_rows * norm_rows))[:, None], 0.0)
    return (4.0 * coherence * (coupled / norm_pair - diag_term)).astype(jnp.bfloat16)


def picked_pair(table, hit_a, hit_b):
    first_pick = jnp.sum(jnp.where(hit_a, table, 0.0), axis=1)
    second_pick = jnp.sum(jnp.where(hit_b, table, 0.0), axis=1)
    return (first_pick, second_pick)


def per_device(tokens, dec_bias, encoder, enc_bias, decoder, atom_ids, block_count):
    tok_dev, width_shard = tokens.shape
    atom_dev = encoder.shape[0]
    owner_total = lax.axis_size("atoms")
    pair_total = atom_ids.shape[1] // 2
    capacity = 3 * tok_dev * pair_total // (2 * owner_total)
    slot_total = owner_total * capacity
    contract = (((1,), (1,)), ((), ()))
    contract_rows = (((0,), (0,)), ((), ()))
    centered = (tokens.astype(jnp.float32) - dec_bias).astype(jnp.bfloat16)
    pair_ids = atom_ids.reshape(tok_dev * pair_total, 2)
    owner_of = pair_ids[:, 0] // atom_dev
    local_atom = pair_ids % atom_dev
    member = (owner_of[:, None] == jnp.arange(owner_total)[None, :]).astype(jnp.int32)
    before = jnp.cumsum(member, axis=0) - member
    slot_of = owner_of * capacity + jnp.sum(before * member, axis=1)
    source_tok = jnp.arange(tok_dev * pair_total) // pair_total
    outgoing = (
        jnp.zeros((slot_total, width_shard), jnp.bfloat16).at[slot_of].set(centered[source_tok])
    )
    slot_tags = jnp.concatenate([local_atom, source_tok[:, None]], axis=1)
    tag_out = jnp.full((slot_total, 3), -1, jnp.int32).at[slot_of].set(slot_tags)
    incoming = lax.all_to_all(outgoing, "atoms", split_axis=0, concat_axis=0, tiled=True)
    tag_in = lax.all_to_all(tag_out, "atoms", split_axis=0, concat_axis=0, tiled=True)
    columns = jnp.arange(atom_dev)[None, :]
    hit_a = tag_in[:, 0:1] == columns
    hit_b = tag_in[:, 1:2] == columns
    scores = lax.dot_general(incoming, encoder, contract, preferred_element_type=jnp.float32)
    scores = lax.psum(scores.astype(jnp.bfloat16), "width").astype(jnp.float32)
    pre_a, pre_b = picked_pair(scores, hit_a, hit_b)
    bias_a, bias_b = picked_pair(enc_bias[None, :], hit_a, hit_b)
    act_a = (pre_a + bias_a).astype(jnp.bfloat16)
    act_b = (pre_b + bias_b).astype(jnp.bfloat16)
    zero_low = jnp.zeros((), jnp.bfloat16)
    act_table = jnp.where(hit_a, act_a[:, None], zero_low) + jnp.where(
        hit_b, act_b[:, None], zero_low
    )
    decoded = jnp.dot(act_table, decoder, preferred_element_type=jnp.float32).astype(jnp.bfloat16)
    returned = lax.all_to_all(decoded, "atoms", split_axis=0, concat_axis=0, tiled=True)
    own_terms = returned[slot_of].reshape(tok_dev, pair_total, width_shard).astype(jnp.float32)
    residual = (jnp.sum(own_terms, axis=1) + dec_bias - tokens.astype(jnp.float32)).astype(
        jnp.bfloat16
    )
    error_out = (
        jnp.zeros((slot_total, width_shard), jnp.bfloat16).at[slot_of].set(residual[source_tok])
    )
    errors = lax.all_to_all(error_out, "atoms", split_axis=0, concat_axis=0, tiled=True)
    back_scores = lax.dot_general(errors, decoder, contract, preferred_element_type=jnp.float32)
    back_scores = lax.psum(back_scores.astype(jnp.bfloat16), "width").astype(jnp.float32)
    grad_a, grad_b = picked_pair(back_scores, hit_a, hit_b)
    dact_a = grad_a * loss_grad
    dact_b = grad_b * loss_grad
    dact_table = jnp.where(hit_a, dact_a[:, None], 0.0) + jnp.where(hit_b, dact_b[:, None], 0.0)
    bias_grad = jnp.sum(dact_table, axis=0)
    encoder_grad = lax.dot_general(
        dact_table.astype(jnp.bfloat16), incoming, contract_rows, preferred_element_type=jnp.float32
    ).astype(jnp.bfloat16)
    fitted = (
        lax.dot_general(act_table, errors, contract_rows, preferred_element_type=jnp.float32)
        * loss_grad
    )
    raw_gram = lax.dot_general(decoder, decoder, contract, preferred_element_type=jnp.float32)
    alive = (jnp.arange(atom_dev) < block_count[0] * BLOCK).astype(jnp.float32)
    summed = lax.psum(raw_gram, "width")
    norms = jnp.sqrt(jnp.diagonal(summed) + epsilon)
    weights = coherence_weights(summed, norms, norms, alive, alive)
    penalty = jnp.dot(weights, decoder, preferred_element_type=jnp.float32)
    decoder_grad = (fitted + penalty).astype(jnp.bfloat16)
    return (residual, encoder_grad, decoder_grad, bias_grad)


def solution(mesh):
    in_specs = (
        P("atoms", "width"),
        P("width"),
        P("atoms", "width"),
        P("atoms"),
        P("atoms", "width"),
        P("atoms", None),
        P("atoms"),
    )
    out_specs = (P("atoms", "width"), P("atoms", "width"), P("atoms", "width"), P("atoms"))
    return jax.shard_map(
        per_device, mesh=mesh, in_specs=in_specs, out_specs=out_specs, check_vma=False
    )
```

profile of v0, /device:TPU:6, one launch (start us, length us, event | category | flops | bytes accessed | tf_op | source)
XLA Modules:
  0.0 508.2 jit_solution(8681748230388222543)
XLA Ops:
  8.9 18.0 %reduce-window.6 = s32[64,8,128]{2,1,0:T(8,128)S(1)} reduce-window(s32[64,8,128]{2,1,0:T(8,128)S(1)} %fusion.41, s32[]{:T(128)} %constant.61.clone.1), window={size=1x1x128 pad=0_0x0_0x127_0}, to_apply=%region_0.1 | reduce-window | flops 8323072 | bytes 524292 | tf_op jit(solution)/shard_map/reduce-window
  29.8 15.7 %scatter_custom_fusion.1 = bf16[1536,1024]{1,0:T(8,128)(2,1)S(1)} fusion(s32[1024]{0:T(1024)S(1)} %get-tuple-element.13, bf16[128,1024]{1,0:T(8,128)(2,1)} %fusion.16, s32[1024]{0:T(1024)S(1)} %broadcast_clamp_fusion.1, bf16[]{:T(256)} %constant.68.clone.1), kind=kCustom, calls=%fused_computation.13 | custom fusion | bytes 3146240 | tf_op jit(solution)/shard_map/scatter | solution.py:51
  45.5 86.2 %all_to_all.48 = bf16[64,24,1024]{2,1,0:T(8,128)(2,1)S(1)} all-to-all(bf16[64,24,1024]{2,1,0:T(8,128)(2,1)S(1)} %bitcast.47), channel_id=1, replica_groups=mesh['atoms'=64,'width'=8] {'atoms'}, dimensions={0} | all-to-all | bytes 6291456 | tf_op jit(solution)/shard_map/all_to_all | solution.py:55
  131.8 1.7 copy-done.4
  133.4 1.7 convolution_convert_fusion.2
  135.4 3.5 scatter_custom_fusion
  139.4 16.0 %all_to_all.49 = s32[64,24,3]{1,2,0:T(4,128)S(1)} all-to-all(s32[64,24,3]{1,2,0:T(4,128)S(1)} %copy.33), channel_id=1, replica_groups=mesh['atoms'=64,'width'=8] {'atoms'}, dimensions={0} | all-to-all | bytes 36864 | tf_op jit(solution)/shard_map/all_to_all | solution.py:56
  155.6 56.2 %all-reduce.4.cloned.1.call-done = bf16[1536,128]{1,0:T(8,128)(2,1)} async-done(((bf16[1536,128]{1,0:T(8,128)(2,1)}), bf16[1536,128]{1,0:T(8,128)(2,1)}) %all-reduce.4.cloned.1.call-update) | async-done | bytes 393232 | tf_op jit(solution)/shard_map/psum | solution.py:61
  211.8 2.5 fusion.8
  214.3 3.1 convolution_convert_fusion
  217.5 11.1 %all-to-all-start.2 = ((bf16[64,24,1024]{2,1,0:T(8,128)(2,1)}), bf16[64,24,1024]{2,1,0:T(8,128)(2,1)S(1)}, u32[]{:S(2)}, u32[]{:S(2)}) async-start(bf16[64,24,1024]{2,1,0:T(8,128)(2,1)} %bitcast.46), calls=%async_computation.2 | async-start | bytes 6291456 | tf_op jit(solution)/shard_map/all_to_all | solution.py:71
  228.6 70.9 %all-to-all-done.2 = bf16[64,24,1024]{2,1,0:T(8,128)(2,1)S(1)} async-done(((bf16[64,24,1024]{2,1,0:T(8,128)(2,1)}), bf16[64,24,1024]{2,1,0:T(8,128)(2,1)S(1)}, u32[]{:S(2)}, u32[]{:S(2)}) %all-to-all-start.2) | async-done | bytes 3145760 | tf_op jit(solution)/shard_map/all_to_all | solution.py:71
  299.5 5.4 %gather_fusion = bf16[1024,1024]{1,0:T(8,128)(2,1)} fusion(bf16[1536,1024]{1,0:T(8,128)(2,1)S(1)} %bitcast.45, s32[1024]{0:T(1024)S(1)} %broadcast_clamp_fusion), kind=kCustom, calls=%fused_computation.1 | custom fusion | bytes 4198400 | tf_op jit(solution)/shard_map/gather | solution.py:72
  304.9 3.0 convert_reduce_fusion
  308.9 14.8 %scatter_custom_fusion.2 = bf16[1536,1024]{1,0:T(8,128)(2,1)} fusion(s32[1024]{0:T(1024)S(1)} %get-tuple-element.13, bf16[128,1024]{1,0:T(8,128)(2,1)S(1)} %fusion.17, s32[1024]{0:T(1024)S(1)} %broadcast_clamp_fusion.1, bf16[]{:T(256)} %constant.68.clone.1), kind=kCustom, calls=%fused_computation.11 | custom fusion | bytes 3145730 | tf_op jit(solution)/shard_map/scatter | solution.py:77
  323.7 8.5 %all-to-all-start.3 = ((bf16[64,24,1024]{2,1,0:T(8,128)(2,1)}), bf16[64,24,1024]{2,1,0:T(8,128)(2,1)}, u32[]{:S(2)}, u32[]{:S(2)}) async-start(bf16[64,24,1024]{2,1,0:T(8,128)(2,1)} %bitcast.9), calls=%async_computation.3 | async-start | bytes 6291456 | tf_op jit(solution)/shard_map/all_to_all | solution.py:79
  334.1 77.2 %all-reduce.8.cloned.1.call-done = f32[128,128]{1,0:T(8,128)} async-done(((f32[128,128]{1,0:T(8,128)}), f32[128,128]{1,0:T(8,128)}) %all-reduce.8.cloned.1.call-update) | async-done | bytes 65552 | tf_op jit(solution)/shard_map/psum | solution.py:96
  411.3 1.9 gather_fusion.1
  414.4 3.6 convolution_convert_fusion.1
  418.4 5.2 %fusion.7 = bf16[128,1024]{1,0:T(8,128)(2,1)} fusion(f32[128,1024]{1,0:T(8,128)S(1)} %fusion.47, bf16[1536,1024]{1,0:T(8,128)(2,1)} %bitcast.10, s32[1536]{0:T(1024)S(1)} %get-tuple-element.9, s32[1536]{0:T(1024)S(1)} %get-tuple-element.8, bf16[1536]{0:T(1024)(128)(2,1)S(1)} %add_convert_fusion, bf16[1536]{0:T(1024)(128)(2,1)S(1)} %add_convert_fusion.1), kind=kOutput, calls=%fused_computation.21 | convolution fusion | flops 404619264 | bytes 3950592 | tf_op jit(solution)/shard_map/dot_general | solution.py:91
  423.6 71.9 %all-reduce.6.cloned.1.call-done = bf16[1536,128]{1,0:T(8,128)(2,1)} async-done(((bf16[1536,128]{1,0:T(8,128)(2,1)}), bf16[1536,128]{1,0:T(8,128)(2,1)}) %all-reduce.6.cloned.1.call-update) | async-done | bytes 393232 | tf_op jit(solution)/shard_map/psum | solution.py:81
  495.5 2.1 fusion.10
  497.6 1.8 fusion.12
  499.4 2.3 convolution_convert_fusion.3
  (64 shorter events, 9.0 us)
Async XLA Ops:
  7.2 207.2 %copy-start = (bf16[128,1024]{1,0:T(8,128)(2,1)S(1)}, bf16[128,1024]{1,0:T(8,128)(2,1)}, u32[]{:S(2)}) copy-start(bf16[128,1024]{1,0:T(8,128)(2,1)} %param.11) | copy-start | bytes 786436
  7.2 21.8 %copy-start.7 = (bf16[128,1024]{1,0:T(8,128)(2,1)S(1)}, bf16[128,1024]{1,0:T(8,128)(2,1)}, u32[]{:S(2)}) copy-start(bf16[128,1024]{1,0:T(8,128)(2,1)} %param.7) | copy-start | bytes 786436
  7.2 21.8 %copy-start.9 = (f32[1024]{0:T(1024)S(1)}, f32[1024]{0:T(1024)}, u32[]{:S(2)}) copy-start(f32[1024]{0:T(1024)} %param.8) | copy-start | bytes 12292
  7.2 204.6 %all-reduce.4.cloned.1.call-start = ((), (), s32[]{:S(2)}) async-start(), calls=%async_computation.4 | async-start | bytes 786432 | tf_op jit(solution)/shard_map/psum | solution.py:61
  8.5 21.3 %copy-start.1 = (s32[1024,2]{1,0:T(8,128)}, s32[1024,2]{1,0:T(8,128)S(1)}, u32[]{:S(2)}) copy-start(s32[1024,2]{1,0:T(8,128)S(1)} %reshape.129) | copy-start | bytes 24580
  45.5 87.9 %copy-start.11 = (bf16[128,1024]{1,0:T(8,128)(2,1)S(1)}, bf16[128,1024]{1,0:T(8,128)(2,1)}, u32[]{:S(2)}) copy-start(bf16[128,1024]{1,0:T(8,128)(2,1)} %param.9) | copy-start | bytes 786436
  131.8 1.7 copy-start.4
  131.8 3.4 copy-start.2
  133.4 2.0 copy-start.6
  135.2 76.6 %copy-start.10 = (f32[128]{0:T(128)S(1)}, f32[128]{0:T(128)}, u32[]{:S(2)}) copy-start(f32[128]{0:T(128)} %param.10) | copy-start | bytes 1540
  217.5 82.0 %all-to-all-start.2 = ((bf16[64,24,1024]{2,1,0:T(8,128)(2,1)}), bf16[64,24,1024]{2,1,0:T(8,128)(2,1)S(1)}, u32[]{:S(2)}, u32[]{:S(2)}) async-start(bf16[64,24,1024]{2,1,0:T(8,128)(2,1)} %bitcast.46), calls=%async_computation.2 | async-start | bytes 6291456 | tf_op jit(solution)/shard_map/all_to_all | solution.py:71
  308.9 14.8 %copy-start.8 = (bf16[128,1024]{1,0:T(8,128)(2,1)}, bf16[128,1024]{1,0:T(8,128)(2,1)S(1)}, u32[]{:S(2)}) copy-start(bf16[128,1024]{1,0:T(8,128)(2,1)S(1)} %fusion.17) | copy-start | bytes 786436
  323.7 90.7 %all-to-all-start.3 = ((bf16[64,24,1024]{2,1,0:T(8,128)(2,1)}), bf16[64,24,1024]{2,1,0:T(8,128)(2,1)}, u32[]{:S(2)}, u32[]{:S(2)}) async-start(bf16[64,24,1024]{2,1,0:T(8,128)(2,1)} %bitcast.9), calls=%async_computation.3 | async-start | bytes 6291456 | tf_op jit(solution)/shard_map/all_to_all | solution.py:79
  332.2 79.1 %all-reduce.8.cloned.1.call-start = ((), (), s32[]{:S(2)}) async-start(), calls=%async_computation.6 | async-start | bytes 131072 | tf_op jit(solution)/shard_map/psum | solution.py:96
  333.1 162.4 %all-reduce.6.cloned.1.call-start = ((), (), s32[]{:S(2)}) async-start(), calls=%async_computation.5 | async-start | bytes 786432 | tf_op jit(solution)/shard_map/psum | solution.py:81
  413.3 4.8 copy-start.3
  418.0 81.4 %copy-start.5 = (bf16[64,24,1024]{2,1,0:T(8,128)(2,1)S(1)}, bf16[64,24,1024]{2,1,0:T(8,128)(2,1)}, u32[]{:S(2)}) copy-start(bf16[64,24,1024]{2,1,0:T(8,128)(2,1)} %copy-done.4) | copy-start | bytes 9437188
Sparse Core Ops, SparseCore 0:
  135.3 76.4 all-reduce.3
  335.9 75.4 all-reduce.7
  418.2 77.2 all-reduce.5
where the time goes:
time: 509 us; the launch traced here: 508 us
  waiting for transfers between devices  276 us (54%)
  blocking collectives  102 us (20%)
  local copies, waits for them, and re-layouts  41.7 us (8%)
  other arithmetic  36.1 us (7%)
  starting transfers between devices  19.9 us (4%)
  matrix products  17.1 us (3%)
  between operations  14.7 us (3%)
    all_to_all x1, blocking collectives, per_device(): lax.all_to_all(outgoing, 'atoms', split_axis=0, concat_axis=0, tiled=True)  86.2 us
    psum x1, waiting for transfers between devices, per_device(): summed = lax.psum(raw_gram, 'width')  77.2 us
    psum x1, waiting for transfers between devices, per_device(): lax.psum(back_scores.astype(jnp.bfloat16), 'width').astype(jnp.float32)  71.9 us
    all_to_all x1, waiting for transfers between devices, per_device(): lax.all_to_all(decoded, 'atoms', split_axis=0, concat_axis=0, tiled=True)  70.9 us
    psum x1, waiting for transfers between devices, per_device(): scores = lax.psum(scores.astype(jnp.bfloat16), 'width').astype(jnp.float32)  56.2 us
    scatter x2, local copies, waits for them, and re-layouts, per_device(): jnp.zeros((slot_total, width_shard), jnp.bfloat16).at[slot_of]  30.5 us
    another operation x3, other arithmetic  18.2 us
    all_to_all x1, blocking collectives, per_device(): lax.all_to_all(tag_out, 'atoms', split_axis=0, concat_axis=0, tiled=True)  16 us
  transfers between devices with their start and end apart: 5, of which 4 were waited for; matrix products, arithmetic and copies ran while one was open for 3% of the time, Pallas kernels for 0%

commit v1 on v0

v1 whole, which is shorter than its diff:
```python
import jax
import jax.numpy as jnp
from jax import lax
from jax.experimental import pallas as pl
from jax.experimental.pallas import tpu as pltpu
from jax.sharding import PartitionSpec as P

NX, NZ, NC, NY = 4, 8, 2, 8
BLOCK = 64
R = 128
COHERENCE = 128.0
LOSS_GRAD = 1.0 / 32.0
EPSILON = 1e-06
BF, F32, I32 = jnp.bfloat16, jnp.float32, jnp.int32
VMEM = 48 * 1024 * 1024


def _place(x, z, c):
    return ((x % NX) * NZ + z % NZ) * NC + c % NC


def _perm(dx=0, dz=0, dc=0):
    return [
        (_place(x, z, c), _place(x + dx, z + dz, c + dc))
        for x in range(NX)
        for z in range(NZ)
        for c in range(NC)
    ]


def move(value, **shift):
    return lax.ppermute(value, "atoms", _perm(**shift))


def call(body, outs, *args, scratch=(), specs=None, name):
    return pl.pallas_call(
        body,
        out_shape=outs,
        in_specs=specs,
        scratch_shapes=scratch,
        compiler_params=pltpu.CompilerParams(vmem_limit_bytes=VMEM),
        name=name,
    )(*args)


def sds(shape, dtype):
    return jax.ShapeDtypeStruct(shape, dtype)


def whole(n):
    return [pl.BlockSpec(memory_space=pltpu.VMEM)] * n


SMEM_SPEC = pl.BlockSpec(memory_space=pltpu.SMEM)
ANY_SPEC = pl.BlockSpec(memory_space=pl.ANY)

NT = (((1,), (1,)), ((), ()))
NN = (((1,), (0,)), ((), ()))


def dot(a, b, dims):
    return lax.dot_general(a, b, dims, preferred_element_type=F32)


def rows_iota(shape):
    return lax.broadcasted_iota(I32, shape, 0)


def lanes_iota(shape):
    return lax.broadcasted_iota(I32, shape, 1)


def center_body(tokens, dec_bias, atom_ids, out):
    out[0:R, :] = (tokens[...].astype(F32) - dec_bias[...]).astype(BF)
    ids = atom_ids[...]
    owner = (ids >> 7).astype(F32).astype(BF)
    local = (ids & 127).astype(F32).astype(BF)
    row, col = rows_iota((8, 16)), lanes_iota((8, 16))
    even = (col == 2 * row).astype(F32).astype(BF)
    odd = (col == 2 * row + 1).astype(F32).astype(BF)
    out[R : R + 8, 0:128] = dot(even, owner, NT).astype(BF)
    out[R : R + 8, 128:256] = dot(even, local, NT).astype(BF)
    out[R : R + 8, 256:384] = dot(odd, local, NT).astype(BF)
    out[R : R + 8, 384:1024] = jnp.zeros((8, 640), BF)


def pack_body(encoder, decoder, enc_bias, out, gram):
    out[0:R, :] = encoder[...]
    out[R : 2 * R, :] = decoder[...]
    bias = jnp.broadcast_to(enc_bias[...], (8, 128))
    high = bias.astype(BF)
    rest = bias - high.astype(F32)
    mid = rest.astype(BF)
    low = (rest - mid.astype(F32)).astype(BF)
    out[2 * R : 2 * R + 8, 0:128] = high
    out[2 * R : 2 * R + 8, 128:256] = mid
    out[2 * R : 2 * R + 8, 256:384] = low
    out[2 * R : 2 * R + 8, 384:1024] = jnp.zeros((8, 640), BF)
    gram[...] = dot(decoder[...], decoder[...], NT)


def locate(ext, pos):
    x, z, c = pos[0], pos[1], pos[2]
    owner = ext[:, 0:128].astype(I32)
    first, second = ext[:, 128:256].astype(I32), ext[:, 256:384].astype(I32)
    dx = (((owner >> 4) - x) + NX) & 3
    b = jnp.where(dx == 0, 0, jnp.where(dx == 3, 1, jnp.where(dx == 1, 2, 3)))
    b = b + jnp.where((owner & 1) == c, 0, 4)
    b = jnp.where(((owner >> 1) & 7) == z, b, -1)
    slot = rows_iota((8, 128))
    at_a = jnp.full((8, 128), -1, I32)
    at_b = jnp.full((8, 128), -1, I32)
    for g in range(8):
        hit = jnp.broadcast_to(b[g : g + 1, :], (8, 128)) == slot
        at_a = jnp.where(hit, jnp.broadcast_to(first[g : g + 1, :], (8, 128)), at_a)
        at_b = jnp.where(hit, jnp.broadcast_to(second[g : g + 1, :], (8, 128)), at_b)
    return at_a, at_b


def pick_into(out, tables, tok, places):
    n = len(places)
    atom = rows_iota((R, 128))
    for h, table in enumerate(tables):
        scores = dot(table[0 : 4 * R, :], tok, NT)
        for i in range(n):
            at_a, at_b = places[i]
            for q in range(4):
                b = 4 * h + q
                part = scores[q * R : (q + 1) * R, i * 128 : (i + 1) * 128]
                for s, at in ((0, at_a), (1, at_b)):
                    row = jnp.broadcast_to(at[b : b + 1, :], (R, 128))
                    got = jnp.sum(jnp.where(atom == row, part, 0.0), axis=0, keepdims=True)
                    out[16 * i + 8 * s + b : 16 * i + 8 * s + b + 1, :] = got


def score_body(split, n):
    def body(pos, own, other, *refs):
        chunks, (picks, where) = refs[:-2], refs[-2:]
        if split:
            toks = [jnp.concatenate([chunks[0][...], chunks[1][0:64, :]], axis=0)]
            exts = [chunks[1][64:72, 0:384].astype(F32)]
        else:
            toks = [c[0:R, :] for c in chunks]
            exts = [c[R : R + 8, 0:384].astype(F32) for c in chunks]
        places = [locate(ext, pos) for ext in exts]
        for i, (at_a, at_b) in enumerate(places):
            where[16 * i : 16 * i + 8, :] = at_a
            where[16 * i + 8 : 16 * i + 16, :] = at_b
        tok = toks[0] if n == 1 else jnp.concatenate(toks, axis=0)
        pick_into(picks, (own, other), tok, places)

    return body


def back_body(split, n, first):
    def body(own, other, where, *refs):
        chunks, picks = refs[:-1], refs[-1]
        toks = [c[...] for c in chunks]
        places = []
        for i in range(n):
            at = 16 * (first + i)
            places.append((where[at : at + 8, :], where[at + 8 : at + 16, :]))
        tok = toks[0] if len(toks) == 1 else jnp.concatenate(toks, axis=0)
        pick_into(picks, (own, other), tok, places)

    return body


def send_body(p0, p1, p2, p3, gram, out):
    picks = jnp.concatenate([p0[...], p1[...], p2[...], p3[...]], axis=0).astype(BF)
    high = gram[...].astype(BF)
    low = (gram[...] - high.astype(F32)).astype(BF)
    for d in range(NY):
        out[d, 0:128, :] = picks
        out[d, 128:144, :] = high[16 * d : 16 * d + 16, :]
        out[d, 144:160, :] = low[16 * d : 16 * d + 16, :]


def resend_body(p0, p1, p2, p3, rows, out):
    picks = jnp.concatenate([p0[...], p1[...], p2[...], p3[...]], axis=0).astype(BF)
    for d in range(NY):
        out[d, 0:128, :] = picks
        out[d, 128:160, :] = rows[...]


def total(got, lo, hi):
    acc = got[0, lo:hi, :].astype(F32)
    for d in range(1, NY):
        acc = acc + got[d, lo:hi, :].astype(F32)
    return acc


def table_rows(at_t, val_t, m, half):
    lane = lanes_iota((R, 128))
    parts = []
    for q in range(4):
        k = 16 * m + 4 * half + q
        first = jnp.where(lane == at_t[:, k : k + 1], val_t[:, k : k + 1], 0.0)
        second = jnp.where(lane == at_t[:, k + 8 : k + 9], val_t[:, k + 8 : k + 9], 0.0)
        parts.append((first + second).astype(BF))
    return jnp.concatenate(parts, axis=1)


def decode(at_t, val_t, own, other, ms):
    halves = []
    for half, table in enumerate((own, other)):
        rows = [table_rows(at_t, val_t, m, half) for m in ms]
        rows = rows[0] if len(ms) == 1 else jnp.concatenate(rows, axis=0)
        halves.append(dot(rows, table[0 : 4 * R, :], NN))
    return halves[0] + halves[1]


def act_body(got, own, other, w0, w1, w2, w3, act, where, at_t, act_t, gram_rows, out):
    pre = total(got, 0, 128)
    bias = []
    for table in (own, other):
        for q in range(4):
            ext = table[4 * R + 8 * q : 4 * R + 8 * q + 8, 0:384].astype(F32)
            bias.append((ext[0:1, 0:128] + ext[0:1, 128:256]) + ext[0:1, 256:384])
    bias = jnp.concatenate(bias, axis=0)
    at = jnp.concatenate([w0[...], w1[...], w2[...], w3[...]], axis=0)
    shift = [
        jnp.take_along_axis(bias, jnp.maximum(at[8 * k : 8 * k + 8, :], 0), axis=1, mode="promise_in_bounds")
        for k in range(16)
    ]
    pre = pre + jnp.concatenate(shift, axis=0)
    value = jnp.where(at >= 0, pre.astype(BF).astype(F32), 0.0)
    act[...] = value
    where[...] = at
    turned = at.astype(F32).T.astype(I32)
    value_t = value.T
    at_t[...] = turned
    act_t[...] = value_t
    rows = total(got, 128, 144) + total(got, 144, 160)
    high = rows.astype(BF)
    gram_rows[0:16, :] = high
    gram_rows[16:32, :] = (rows - high.astype(F32)).astype(BF)
    out[...] = decode(turned, value_t, own, other, (7,)).astype(BF)


def decode_body(ms):
    def body(at_t, act_t, own, other, *outs):
        got = decode(at_t[...], act_t[...], own, other, ms)
        for i, out in enumerate(outs):
            out[...] = got[i * R : (i + 1) * R, :].astype(out.dtype)

    return body


def turned_table(at, val, b):
    atom = rows_iota((R, 128))
    parts = []
    for m in range(8):
        k = 16 * m + b
        first = jnp.where(atom == at[k : k + 1, :], val[k : k + 1, :], 0.0)
        second = jnp.where(atom == at[k + 8 : k + 9, :], val[k + 8 : k + 9, :], 0.0)
        parts.append(first + second)
    return parts


def load_rows(refs, rows, sem):
    copies, at = [], 0
    for i, ref in enumerate(refs):
        n = min(ref.shape[0], R)
        if ref.shape[0] == 72:
            n = 64
        copies.append(pltpu.make_async_copy(ref.at[pl.ds(0, n)], rows.at[pl.ds(at, n)], sem.at[i]))
        at += n
    for copy in copies:
        copy.start()
    return copies


def fitted_body(at, act, *refs):
    chunks, (own, other, rows, sem) = refs[:9], refs[9:]
    copies = load_rows(chunks, rows, sem)
    tables = []
    for half in (1, 0):
        parts = []
        for q in range(4):
            parts.append(jnp.concatenate(turned_table(at, act, 4 * half + q), axis=1).astype(BF))
        tables.append(jnp.concatenate(parts, axis=0))
    for copy in copies:
        copy.wait()
    other[...] = (dot(tables[0], rows[...], NN) * LOSS_GRAD).astype(BF)
    own[...] = (dot(tables[1], rows[...], NN) * LOSS_GRAD).astype(BF)


def encgrad_body(got, at, *refs):
    chunks, (own, other, gram, rows, sem) = refs[:9], refs[9:]
    copies = load_rows(chunks, rows, sem)
    grad = jnp.where(at[...] >= 0, total(got, 0, 128) * LOSS_GRAD, 0.0)
    for d in range(NY):
        gram[16 * d : 16 * d + 16, :] = got[d, 128:144, :].astype(F32) + got[d, 144:160, :].astype(F32)
    tables, sums = [], []
    ones = jnp.ones((8, 128), F32)
    for half in (1, 0):
        parts = []
        for q in range(4):
            pieces = turned_table(at, grad, 4 * half + q)
            acc = pieces[0]
            for piece in pieces[1:]:
                acc = acc + piece
            sums.append(lax.dot_general(ones, acc, NT, precision=lax.Precision.HIGHEST, preferred_element_type=F32))
            parts.append(jnp.concatenate(pieces, axis=1).astype(BF))
        tables.append(jnp.concatenate(parts, axis=0))
    for copy in copies:
        copy.wait()
    for k, out in ((0, other), (1, own)):
        part = dot(tables[k], rows[...], NN).astype(BF)
        for q in range(4):
            out[q, 0:R, :] = part[q * R : (q + 1) * R, :]
            out[q, R : R + 8, 0:128] = sums[4 * k + q].astype(BF)
            out[q, R : R + 8, 128:1024] = jnp.zeros((8, 896), BF)


def penalty_body(count, gram_ref, decoder, out):
    gram = gram_ref[...]
    row, col = rows_iota((R, R)), lanes_iota((R, R))
    diagonal = row == col
    kept = jnp.where(diagonal, gram, 0.0)
    norm_c = jnp.sqrt(jnp.sum(kept, axis=1, keepdims=True) + EPSILON)
    norm_r = jnp.sqrt(jnp.sum(kept, axis=0, keepdims=True) + EPSILON)
    live = count[0] * BLOCK
    pair = norm_c * norm_r
    cosine = gram / pair
    alive = (row < live) & (col < live) & jnp.logical_not(diagonal)
    coupled = jnp.where(alive, cosine, 0.0)
    spread = jnp.sum(coupled * cosine, axis=1, keepdims=True)
    diag_term = jnp.where(diagonal, spread / (norm_c * norm_c), 0.0)
    weights = (4.0 * COHERENCE * (coupled / pair - diag_term)).astype(BF)
    out[...] = dot(weights, decoder[...], NN)


def add(a, b):
    return (a.astype(F32) + b.astype(F32)).astype(BF)


def gather_z(own, cut):
    f1, b1 = move(own, dz=1), move(own, dz=-1)
    f2, b2 = move(f1, dz=1), move(b1, dz=-1)
    f3, b3 = move(f2, dz=1), move(b2, dz=-1)
    f4, b4 = move(f3[:cut], dz=1), move(b3[cut:], dz=-1)
    return [own, f1, b1, f2, b2, f3, b3, f4, b4]


def scatter_x(own, other):
    theirs = move(other, dc=1)
    blocks = [add(own[i], theirs[i]) for i in range(4)]
    cut = 64
    f = move(blocks[3][:cut], dx=1)
    b = move(blocks[3][cut:], dx=-1)
    to_next = jnp.concatenate([add(blocks[2][:cut], f), blocks[2][cut:]], axis=0)
    to_prev = jnp.concatenate([blocks[1][:cut], add(blocks[1][cut:], b)], axis=0)
    return blocks[0], move(to_next, dx=1), move(to_prev, dx=-1)


def per_device(tokens, dec_bias, encoder, enc_bias, decoder, atom_ids, block_count):
    place = lax.axis_index("atoms")
    pos = jnp.stack([place // (NZ * NC), (place // NC) % NZ, place % NC]).astype(I32)
    bias_row = dec_bias.reshape(1, -1)

    sent = call(center_body, sds((R + 8, 1024), BF), tokens, bias_row, atom_ids, specs=whole(3), name="center")
    packed, gram_part = call(
        pack_body,
        (sds((2 * R + 8, 1024), BF), sds((R, R), F32)),
        encoder, decoder, enc_bias.reshape(1, -1), specs=whole(3), name="pack",
    )
    tok = gather_z(sent, 64)

    x1, x2 = move(packed, dx=1), move(packed, dx=-1)
    x3e, x3d = move(x1[:R], dx=1), move(x2[R:], dx=-1)
    enc_own = jnp.concatenate([encoder, x1[:R], x2[:R], x3e], axis=0)
    dec_own = jnp.concatenate(
        [decoder, x1[R : 2 * R], x2[R : 2 * R], x3d[:R], packed[2 * R :], x1[2 * R :], x2[2 * R :], x3d[R:]], axis=0
    )
    enc_other = move(enc_own, dc=1)
    dec_other = move(dec_own, dc=1)

    def score(chunks, split=False):
        n = 1 if split else len(chunks)
        return call(
            score_body(split, n),
            (sds((16 * n, 128), F32), sds((16 * n, 128), I32)),
            pos, enc_own, enc_other, *chunks,
            specs=[SMEM_SPEC] + whole(2 + len(chunks)), name="score",
        )

    picks, wheres = zip(score(tok[0:3]), score(tok[3:5]), score(tok[5:7]), score(tok[7:9], True))
    out = call(send_body, sds((NY, 160, 128), BF), *picks, gram_part, specs=whole(5), name="send")
    got = lax.all_to_all(out, "width", split_axis=0, concat_axis=0, tiled=True)

    act, where, at_t, act_t, gram_rows, d7 = call(
        act_body,
        (sds((R, R), F32), sds((R, R), I32), sds((R, R), I32), sds((R, R), F32), sds((32, 128), BF), sds((R, 1024), BF)),
        got, dec_own, dec_other, *wheres, specs=whole(7), name="act",
    )

    def decoded(ms, dtype=BF):
        return call(
            decode_body(ms), tuple(sds((R, 1024), dtype) for _ in ms),
            at_t, act_t, dec_own, dec_other, specs=whole(4), name="decode",
        )

    d5, d6 = decoded((5, 6))
    d3, d4 = decoded((3, 4))
    d1, d2 = decoded((1, 2))
    (d0,) = decoded((0,), F32)
    f = move(d7[:64], dz=1)
    b = move(d7[64:], dz=-1)
    f = move(jnp.concatenate([add(d6[:64], f), d6[64:]], axis=0), dz=1)
    b = move(jnp.concatenate([d5[:64], add(d5[64:], b)], axis=0), dz=-1)
    f, b = move(add(d4, f), dz=1), move(add(d3, b), dz=-1)
    f, b = move(add(d2, f), dz=1), move(add(d1, b), dz=-1)
    summed = d0 + f.astype(F32) + b.astype(F32)
    residual = (summed + bias_row - tokens.astype(F32)).astype(BF)

    res = gather_z(residual, 64)

    def back(chunks, first, split=False):
        n = 1 if split else len(chunks)
        return call(
            back_body(split, n, first), sds((16 * n, 128), F32),
            dec_own, dec_other, where, *chunks, specs=whole(3 + len(chunks)), name="back",
        )

    backs = (back(res[0:3], 0), back(res[3:5], 3), back(res[5:7], 5), back(res[7:9], 7, True))
    out2 = call(resend_body, sds((NY, 160, 128), BF), *backs, gram_rows, specs=whole(5), name="resend")
    got2 = lax.all_to_all(out2, "width", split_axis=0, concat_axis=0, tiled=True)

    scratch = [pltpu.VMEM((8 * R, 1024), BF), pltpu.SemaphoreType.DMA((9,))]
    fit_own, fit_other = call(
        fitted_body, (sds((4 * R, 1024), BF), sds((4 * R, 1024), BF)),
        where, act, *res, specs=whole(2) + [ANY_SPEC] * 9, scratch=scratch, name="fitted",
    )
    fit = scatter_x(fit_own.reshape(4, R, 1024), fit_other.reshape(4, R, 1024))

    eg_own, eg_other, gram = call(
        encgrad_body, (sds((4, R + 8, 1024), BF), sds((4, R + 8, 1024), BF), sds((R, R), F32)),
        got2, where, *tok, specs=whole(2) + [ANY_SPEC] * 9, scratch=scratch, name="encgrad",
    )
    eg = scatter_x(eg_own, eg_other)
    eg_sum = eg[0].astype(F32) + eg[1].astype(F32) + eg[2].astype(F32)
    encoder_grad = eg_sum[:R].astype(BF)
    bias_grad = eg_sum[R, 0:R]

    penalty = call(
        penalty_body, sds((R, 1024), F32), block_count, gram, decoder, specs=[SMEM_SPEC] + whole(2), name="penalty"
    )
    decoder_grad = (fit[0].astype(F32) + fit[1].astype(F32) + fit[2].astype(F32) + penalty).astype(BF)
    return (residual, encoder_grad, decoder_grad, bias_grad)


def solution(mesh):
    in_specs = (
        P("atoms", "width"),
        P("width"),
        P("atoms", "width"),
        P("atoms"),
        P("atoms", "width"),
        P("atoms", None),
        P("atoms"),
    )
    out_specs = (P("atoms", "width"), P("atoms", "width"), P("atoms", "width"), P("atoms"))
    return jax.shard_map(per_device, mesh=mesh, in_specs=in_specs, out_specs=out_specs, check_vma=False)
```

time: 509 us -> 270 us (0.53)
  waiting for transfers between devices: 276 us -> 56.3 us
  starting transfers between devices: 19.9 us -> 143 us
  blocking collectives: 102 us -> 16.7 us
  other arithmetic: 36.1 us -> 2.59 us
  Pallas kernels: 0 us -> 31.8 us
  local copies, waits for them, and re-layouts: 41.7 us -> 15.9 us
  matrix products: 17.1 us -> 0 us
  between operations: 14.7 us -> 2.55 us
    psum x3 -> x0, waiting for transfers between devices: 205 us -> none  [the longest x1 77.2 us: per_device(): summed = lax.psum(raw_gram, 'width')]
    ppermute x0 -> x40, starting transfers between devices: none -> 135 us  [move(): return lax.ppermute(value, 'atoms', _perm(**shift))]
    all_to_all x2 -> x1, blocking collectives: 102 us -> 16.7 us  [per_device(): lax.all_to_all(out2, 'width', split_axis=0, concat_axis=0, tiled=True)]
    all_to_all x2 -> x1, waiting for transfers between devices: 70.9 us -> 12.8 us  [per_device(): got = lax.all_to_all(out, 'width', split_axis=0, concat_axis=0, tiled=True)]
    ppermute x0 -> x40, waiting for transfers between devices: none -> 43.5 us  [move(): return lax.ppermute(value, 'atoms', _perm(**shift))]
    pallas_call x0 -> x20, Pallas kernels: none -> 31.8 us  [call(): pl.pallas_call(body, out_shape=outs, in_specs=specs, scratch_shapes=scrat...]
    scatter x2 -> x0, local copies, waits for them, and re-layouts: 30.5 us -> none  [per_device(): jnp.zeros((slot_total, width_shard), jnp.bfloat16).at[slot_of]]
    another operation x3 -> x1, other arithmetic: 18.2 us -> 0.08 us  [per_device(): jnp.stack([place // (NZ * NC), place // NC % NZ, place % NC]).astype(I32)]
  transfers between devices with their start and end apart: 5 -> 41, of which waited for: 4 -> 17; matrix products, arithmetic and copies ran while one was open for 3% -> 2% of each run, Pallas kernels for 0% -> 10%
where the time goes in v1:
time: 270 us; the launch traced here: 268 us
  starting transfers between devices  143 us (53%)
  waiting for transfers between devices  56.3 us (21%)
  Pallas kernels  31.8 us (12%)
  blocking collectives  16.7 us (6%)
  local copies, waits for them, and re-layouts  15.9 us (6%)
    ppermute x40, starting transfers between devices, move(): return lax.ppermute(value, 'atoms', _perm(**shift))  135 us
    ppermute x40, waiting for transfers between devices, move(): return lax.ppermute(value, 'atoms', _perm(**shift))  43.5 us
    pallas_call x20, Pallas kernels, call(): pl.pallas_call(body, out_shape=outs, in_specs=specs, scratch_shapes=scrat...  31.8 us
    all_to_all x1, blocking collectives, per_device(): lax.all_to_all(out2, 'width', split_axis=0, concat_axis=0, tiled=True)  16.7 us
    unnamed x90, local copies, waits for them, and re-layouts  13.1 us
    all_to_all x1, waiting for transfers between devices, per_device(): got = lax.all_to_all(out, 'width', split_axis=0, concat_axis=0, tiled=True)  12.8 us
    all_to_all x1, starting transfers between devices, per_device(): got = lax.all_to_all(out, 'width', split_axis=0, concat_axis=0, tiled=True)  7.11 us
  transfers between devices with their start and end apart: 41, of which 17 were waited for; matrix products, arithmetic and copies ran while one was open for 2% of the time, Pallas kernels for 10%

profile of v1, /device:TPU:6, one launch (start us, length us, event | category | flops | bytes accessed | tf_op | source)
XLA Modules:
  0.0 268.4 jit_solution(5666876472479093941)
XLA Ops:
  4.1 7.7 %collective-permute-start = (bf16[264,1024]{1,0:T(8,128)(2,1)S(1)}, bf16[264,1024]{1,0:T(8,128)(2,1)S(1)}, u32[]{:S(2)}, u32[]{:S(2)}) collective-permute-start(bf16[264,1024]{1,0:T(8,128)(2,1)S(1)} %get-tuple-element.31), channel_id=1, source_target_pairs={{0,128},{8,136},{16,144},{24,152},{32,160},{40,168},{48,176},{56,1... | collective-permute-start | bytes 1622024 | tf_op jit(solution)/shard_map/ppermute | solution.py:32
  16.4 7.1 %collective-permute-start.5 = (bf16[136,1024]{1,0:T(8,128)(2,1)S(1)}, bf16[136,1024]{1,0:T(8,128)(2,1)S(1)}, u32[]{:S(2)}, u32[]{:S(2)}) collective-permute-start(bf16[136,1024]{1,0:T(8,128)(2,1)S(1)} %center.1.refs_0_), channel_id=1, source_target_pairs={{0,112},{8,120},{16,0},{24,8},{32,16},{40,24},{48,32},{56,40},{64,... | collective-permute-start | bytes 835592 | tf_op jit(solution)/shard_map/ppermute | solution.py:32
  29.3 5.3 %collective-permute-start.7 = (bf16[136,1024]{1,0:T(8,128)(2,1)S(1)}, bf16[136,1024]{1,0:T(8,128)(2,1)S(1)}, u32[]{:S(2)}, u32[]{:S(2)}) collective-permute-start(bf16[136,1024]{1,0:T(8,128)(2,1)S(1)} %collective-permute-done.5.refs_2_), channel_id=1, source_target_pairs={{0,112},{8,120},{16,0},{24,8},{32,16},{40,24},{48,32},{56,40},{64,... | collective-permute-start | bytes 835592 | tf_op jit(solution)/shard_map/ppermute | solution.py:32
  41.3 5.4 %collective-permute-done.12 = bf16[136,1024]{1,0:T(8,128)(2,1)S(1)} collective-permute-done((bf16[136,1024]{1,0:T(8,128)(2,1)S(1)}, bf16[136,1024]{1,0:T(8,128)(2,1)S(1)}, u32[]{:S(2)}, u32[]{:S(2)}) %collective-permute-start.12) | collective-permute-done | bytes 278560 | tf_op jit(solution)/shard_map/ppermute | solution.py:32
  50.1 4.9 %collective-permute-start.9 = (bf16[136,1024]{1,0:T(8,128)(2,1)S(1)}, bf16[136,1024]{1,0:T(8,128)(2,1)S(1)}, u32[]{:S(2)}, u32[]{:S(2)}) collective-permute-start(bf16[136,1024]{1,0:T(8,128)(2,1)S(1)} %collective-permute-done.7.refs_1_.refs_4_), channel_id=1, source_target_pairs={{0,112},{8,120},{16,0},{24,8},{32,16},{40,24},{48,32},{56,40},{64,... | collective-permute-start | bytes 835592 | tf_op jit(solution)/shard_map/ppermute | solution.py:32
  62.9 5.6 %collective-permute-start.11 = (bf16[72,1024]{1,0:T(8,128)(2,1)}, bf16[72,1024]{1,0:T(8,128)(2,1)}, u32[]{:S(2)}, u32[]{:S(2)}) collective-permute-start(bf16[72,1024]{1,0:T(8,128)(2,1)} %slice.227), channel_id=1, source_target_pairs={{0,112},{8,120},{16,0},{24,8},{32,16},{40,24},{48,32},{56,40},{64,... | collective-permute-start | bytes 442376 | tf_op jit(solution)/shard_map/ppermute | solution.py:32
  85.7 7.1 %all-to-all-start = ((bf16[8,160,128]{2,1,0:T(8,128)(2,1)}), bf16[8,160,128]{2,1,0:T(8,128)(2,1)S(1)}, u32[]{:S(2)}, u32[]{:S(2)}) async-start(bf16[8,160,128]{2,1,0:T(8,128)(2,1)} %send.1), calls=%async_computation | async-start | bytes 655360 | tf_op jit(solution)/shard_map/all_to_all | solution.py:391
  92.8 12.8 %all-to-all-done.got = bf16[8,160,128]{2,1,0:T(8,128)(2,1)S(1)} async-done(((bf16[8,160,128]{2,1,0:T(8,128)(2,1)}), bf16[8,160,128]{2,1,0:T(8,128)(2,1)S(1)}, u32[]{:S(2)}, u32[]{:S(2)}) %all-to-all-start) | async-done | bytes 327712 | tf_op jit(solution)/shard_map/all_to_all | solution.py:391
  106.8 4.9 %collective-permute-start.18 = (bf16[64,1024]{1,0:T(8,128)(2,1)S(1)}, bf16[64,1024]{1,0:T(8,128)(2,1)S(1)}, u32[]{:S(2)}, u32[]{:S(2)}) collective-permute-start(bf16[64,1024]{1,0:T(8,128)(2,1)S(1)} %get-tuple-element.71), channel_id=1, source_target_pairs={{0,112},{8,120},{16,0},{24,8},{32,16},{40,24},{48,32},{56,40},{64,... | collective-permute-start | bytes 393224 | tf_op jit(solution)/shard_map/ppermute | solution.py:32
  115.6 5.1 %collective-permute-start.19 = (bf16[128,1024]{1,0:T(8,128)(2,1)S(1)}, bf16[128,1024]{1,0:T(8,128)(2,1)S(1)}, u32[]{:S(2)}, u32[]{:S(2)}) collective-permute-start(bf16[128,1024]{1,0:T(8,128)(2,1)S(1)} %pad_maximum_fusion.4), channel_id=1, source_target_pairs={{0,112},{8,120},{16,0},{24,8},{32,16},{40,24},{48,32},{56,40},{64,... | collective-permute-start | bytes 786440 | tf_op jit(solution)/shard_map/ppermute | solution.py:32
  124.8 5.5 %collective-permute-start.20 = (bf16[128,1024]{1,0:T(8,128)(2,1)S(1)}, bf16[128,1024]{1,0:T(8,128)(2,1)S(1)}, u32[]{:S(2)}, u32[]{:S(2)}) collective-permute-start(bf16[128,1024]{1,0:T(8,128)(2,1)S(1)} %add_convert_fusion.6), channel_id=1, source_target_pairs={{0,112},{8,120},{16,0},{24,8},{32,16},{40,24},{48,32},{56,40},{64,... | collective-permute-start | bytes 786440 | tf_op jit(solution)/shard_map/ppermute | solution.py:32
  134.5 5.3 %collective-permute-start.21 = (bf16[128,1024]{1,0:T(8,128)(2,1)S(1)}, bf16[128,1024]{1,0:T(8,128)(2,1)S(1)}, u32[]{:S(2)}, u32[]{:S(2)}) collective-permute-start(bf16[128,1024]{1,0:T(8,128)(2,1)S(1)} %add_convert_fusion.5), channel_id=1, source_target_pairs={{0,112},{8,120},{16,0},{24,8},{32,16},{40,24},{48,32},{56,40},{64,... | collective-permute-start | bytes 786440 | tf_op jit(solution)/shard_map/ppermute | solution.py:32
  143.7 5.8 %collective-permute-done.17 = bf16[128,1024]{1,0:T(8,128)(2,1)S(1)} collective-permute-done((bf16[128,1024]{1,0:T(8,128)(2,1)S(1)}, bf16[128,1024]{1,0:T(8,128)(2,1)S(1)}, u32[]{:S(2)}, u32[]{:S(2)}) %collective-permute-start.17) | collective-permute-done | bytes 262176 | tf_op jit(solution)/shard_map/ppermute | solution.py:32
  155.6 5.2 %collective-permute-done.23.refs_2_ = bf16[128,1024]{1,0:T(8,128)(2,1)S(1)} collective-permute-done((bf16[128,1024]{1,0:T(8,128)(2,1)S(1)}, bf16[128,1024]{1,0:T(8,128)(2,1)S(1)}, u32[]{:S(2)}, u32[]{:S(2)}) %collective-permute-start.23) | collective-permute-done | bytes 262176 | tf_op jit(solution)/shard_map/ppermute | solution.py:32
  166.6 4.3 %collective-permute-done.25.refs_1_.refs_4_ = bf16[128,1024]{1,0:T(8,128)(2,1)S(1)} collective-permute-done((bf16[128,1024]{1,0:T(8,128)(2,1)S(1)}, bf16[128,1024]{1,0:T(8,128)(2,1)S(1)}, u32[]{:S(2)}, u32[]{:S(2)}) %collective-permute-start.25) | collective-permute-done | bytes 262176 | tf_op jit(solution)/shard_map/ppermute | solution.py:32
  179.3 5.6 %collective-permute-start.29 = (bf16[64,1024]{1,0:T(8,128)(2,1)S(1)}, bf16[64,1024]{1,0:T(8,128)(2,1)S(1)}, u32[]{:S(2)}, u32[]{:S(2)}) collective-permute-start(bf16[64,1024]{1,0:T(8,128)(2,1)S(1)} %slice.236), channel_id=1, source_target_pairs={{0,112},{8,120},{16,0},{24,8},{32,16},{40,24},{48,32},{56,40},{64,... | collective-permute-start | bytes 393224 | tf_op jit(solution)/shard_map/ppermute | solution.py:32
  187.4 5.7 %collective-permute-done.28.refs_0_.refs_7_ = bf16[64,1024]{1,0:T(8,128)(2,1)S(1)} collective-permute-done((bf16[64,1024]{1,0:T(8,128)(2,1)S(1)}, bf16[64,1024]{1,0:T(8,128)(2,1)S(1)}, u32[]{:S(2)}, u32[]{:S(2)}) %collective-permute-start.28) | collective-permute-done | bytes 131104 | tf_op jit(solution)/shard_map/ppermute | solution.py:32
  203.2 16.7 %all_to_all.10.got = bf16[8,160,128]{2,1,0:T(8,128)(2,1)S(1)} all-to-all(bf16[8,160,128]{2,1,0:T(8,128)(2,1)S(1)} %resend.1), channel_id=1, replica_groups=mesh['atoms'=64,'width'=8] {'width'}, dimensions={0} | all-to-all | bytes 655360 | tf_op jit(solution)/shard_map/all_to_all | solution.py:429
  220.0 5.0 %encgrad.1 = (bf16[4,136,1024]{2,1,0:T(8,128)(2,1)S(1)}, bf16[4,136,1024]{2,1,0:T(8,128)(2,1)S(1)}, f32[128,128]{1,0:T(8,128)S(1)}) custom-call(bf16[8,160,128]{2,1,0:T(8,128)(2,1)S(1)} %all_to_all.10.got, s32[128,128]{1,0:T(8,128)S(1)} %get-tuple-element.50.where.at, bf16[136,1024]{1,0:T(8,128)(2,1)S(1)} %center.1.refs_0_, ...), custom_call_target="tpu_custom_call" | custom-call | tf_op jit(solution)/shard_map/encgrad/pallas_call | solution.py:36
  229.2 5.1 %collective-permute-start.36 = (bf16[64,1024]{1,0:T(8,128)(2,1)S(1)}, bf16[64,1024]{1,0:T(8,128)(2,1)S(1)}, u32[]{:S(2)}, u32[]{:S(2)}) collective-permute-start(bf16[64,1024]{1,0:T(8,128)(2,1)S(1)} %get-tuple-element.68), channel_id=1, source_target_pairs={{0,128},{8,136},{16,144},{24,152},{32,160},{40,168},{48,176},{56,1... | collective-permute-start | bytes 393224 | tf_op jit(solution)/shard_map/ppermute | solution.py:32
  238.3 5.1 %collective-permute-start.37 = (bf16[128,1024]{1,0:T(8,128)(2,1)S(1)}, bf16[128,1024]{1,0:T(8,128)(2,1)S(1)}, u32[]{:S(2)}, u32[]{:S(2)}) collective-permute-start(bf16[128,1024]{1,0:T(8,128)(2,1)S(1)} %pad_maximum_fusion.5), channel_id=1, source_target_pairs={{0,128},{8,136},{16,144},{24,152},{32,160},{40,168},{48,176},{56,1... | collective-permute-start | bytes 786440 | tf_op jit(solution)/shard_map/ppermute | solution.py:32
  245.8 4.1 %collective-permute-start.33 = (bf16[72,1024]{1,0:T(8,128)(2,1)S(1)}, bf16[72,1024]{1,0:T(8,128)(2,1)S(1)}, u32[]{:S(2)}, u32[]{:S(2)}) collective-permute-start(bf16[72,1024]{1,0:T(8,128)(2,1)S(1)} %slice_bitcast_fusion.4), channel_id=1, source_target_pairs={{0,384},{8,392},{16,400},{24,408},{32,416},{40,424},{48,432},{56,4... | collective-permute-start | bytes 442376 | tf_op jit(solution)/shard_map/ppermute | solution.py:32
  251.4 5.6 %collective-permute-start.32 = (bf16[136,1024]{1,0:T(8,128)(2,1)S(1)}, bf16[136,1024]{1,0:T(8,128)(2,1)S(1)}, u32[]{:S(2)}, u32[]{:S(2)}) collective-permute-start(bf16[136,1024]{1,0:T(8,128)(2,1)S(1)} %pad_maximum_fusion.1), channel_id=1, source_target_pairs={{0,128},{8,136},{16,144},{24,152},{32,160},{40,168},{48,176},{56,1... | collective-permute-start | bytes 835592 | tf_op jit(solution)/shard_map/ppermute | solution.py:32
  261.6 5.4 %collective-permute-done.34 = bf16[136,1024]{1,0:T(8,128)(2,1)S(1)} collective-permute-done((bf16[136,1024]{1,0:T(8,128)(2,1)S(1)}, bf16[136,1024]{1,0:T(8,128)(2,1)S(1)}, u32[]{:S(2)}, u32[]{:S(2)}) %collective-permute-start.34) | collective-permute-done | bytes 278560 | tf_op jit(solution)/shard_map/ppermute | solution.py:32
  (210 shorter events, 115.6 us)
Async XLA Ops:
  4.1 21.4 %collective-permute-start = (bf16[264,1024]{1,0:T(8,128)(2,1)S(1)}, bf16[264,1024]{1,0:T(8,128)(2,1)S(1)}, u32[]{:S(2)}, u32[]{:S(2)}) collective-permute-start(bf16[264,1024]{1,0:T(8,128)(2,1)S(1)} %get-tuple-element.31), channel_id=1, source_target_pairs={{0,128},{8,136},{16,144},{24,152},{32,160},{40,168},{48,176},{56,1... | collective-permute-start | bytes 1622024 | tf_op jit(solution)/shard_map/ppermute | solution.py:32
  11.8 24.7 %collective-permute-start.1 = (bf16[264,1024]{1,0:T(8,128)(2,1)S(1)}, bf16[264,1024]{1,0:T(8,128)(2,1)S(1)}, u32[]{:S(2)}, u32[]{:S(2)}) collective-permute-start(bf16[264,1024]{1,0:T(8,128)(2,1)S(1)} %get-tuple-element.31), channel_id=1, source_target_pairs={{0,384},{8,392},{16,400},{24,408},{32,416},{40,424},{48,432},{56,4... | collective-permute-start | bytes 1622024 | tf_op jit(solution)/shard_map/ppermute | solution.py:32
  16.4 12.9 %collective-permute-start.5 = (bf16[136,1024]{1,0:T(8,128)(2,1)S(1)}, bf16[136,1024]{1,0:T(8,128)(2,1)S(1)}, u32[]{:S(2)}, u32[]{:S(2)}) collective-permute-start(bf16[136,1024]{1,0:T(8,128)(2,1)S(1)} %center.1.refs_0_), channel_id=1, source_target_pairs={{0,112},{8,120},{16,0},{24,8},{32,16},{40,24},{48,32},{56,40},{64,... | collective-permute-start | bytes 835592 | tf_op jit(solution)/shard_map/ppermute | solution.py:32
  23.5 11.1 %collective-permute-start.4 = (bf16[136,1024]{1,0:T(8,128)(2,1)S(1)}, bf16[136,1024]{1,0:T(8,128)(2,1)S(1)}, u32[]{:S(2)}, u32[]{:S(2)}) collective-permute-start(bf16[136,1024]{1,0:T(8,128)(2,1)S(1)} %center.1.refs_0_), channel_id=1, source_target_pairs={{0,16},{8,24},{16,32},{24,40},{32,48},{40,56},{48,64},{56,72},{64,... | collective-permute-start | bytes 835592 | tf_op jit(solution)/shard_map/ppermute | solution.py:32
  25.6 13.7 %collective-permute-start.2 = (bf16[128,1024]{1,0:T(8,128)(2,1)S(1)}, bf16[128,1024]{1,0:T(8,128)(2,1)S(1)}, u32[]{:S(2)}, u32[]{:S(2)}) collective-permute-start(bf16[128,1024]{1,0:T(8,128)(2,1)S(1)} %get-tuple-element.67), channel_id=1, source_target_pairs={{0,128},{8,136},{16,144},{24,152},{32,160},{40,168},{48,176},{56,1... | collective-permute-start | bytes 786440 | tf_op jit(solution)/shard_map/ppermute | solution.py:32
  29.3 20.8 %collective-permute-start.7 = (bf16[136,1024]{1,0:T(8,128)(2,1)S(1)}, bf16[136,1024]{1,0:T(8,128)(2,1)S(1)}, u32[]{:S(2)}, u32[]{:S(2)}) collective-permute-start(bf16[136,1024]{1,0:T(8,128)(2,1)S(1)} %collective-permute-done.5.refs_2_), channel_id=1, source_target_pairs={{0,112},{8,120},{16,0},{24,8},{32,16},{40,24},{48,32},{56,40},{64,... | collective-permute-start | bytes 835592 | tf_op jit(solution)/shard_map/ppermute | solution.py:32
  34.6 20.3 %collective-permute-start.6 = (bf16[136,1024]{1,0:T(8,128)(2,1)S(1)}, bf16[136,1024]{1,0:T(8,128)(2,1)S(1)}, u32[]{:S(2)}, u32[]{:S(2)}) collective-permute-start(bf16[136,1024]{1,0:T(8,128)(2,1)S(1)} %collective-permute-done.4.refs_1_), channel_id=1, source_target_pairs={{0,16},{8,24},{16,32},{24,40},{32,48},{40,56},{48,64},{56,72},{64,... | collective-permute-start | bytes 835592 | tf_op jit(solution)/shard_map/ppermute | solution.py:32
  39.4 32.5 %collective-permute-start.3 = (bf16[512,1024]{1,0:T(8,128)(2,1)S(1)}, bf16[512,1024]{1,0:T(8,128)(2,1)}, u32[]{:S(2)}, u32[]{:S(2)}) collective-permute-start(bf16[512,1024]{1,0:T(8,128)(2,1)S(1)} %pad_maximum_fusion.own), channel_id=1, source_target_pairs={{0,8},{8,0},{16,24},{24,16},{32,40},{40,32},{48,56},{56,48},{64,72... | collective-permute-start | bytes 3145736 | tf_op jit(solution)/shard_map/ppermute | solution.py:32
  48.2 44.7 %collective-permute-start.13 = (bf16[544,1024]{1,0:T(8,128)(2,1)S(1)}, bf16[544,1024]{1,0:T(8,128)(2,1)S(1)}, u32[]{:S(2)}, u32[]{:S(2)}) collective-permute-start(bf16[544,1024]{1,0:T(8,128)(2,1)S(1)} %constant_dynamic-update-slice_fusion.own), channel_id=1, source_target_pairs={{0,8},{8,0},{16,24},{24,16},{32,40},{40,32},{48,56},{56,48},{64,72... | collective-permute-start | bytes 3342344 | tf_op jit(solution)/shard_map/ppermute | solution.py:32
  50.1 11.4 %collective-permute-start.9 = (bf16[136,1024]{1,0:T(8,128)(2,1)S(1)}, bf16[136,1024]{1,0:T(8,128)(2,1)S(1)}, u32[]{:S(2)}, u32[]{:S(2)}) collective-permute-start(bf16[136,1024]{1,0:T(8,128)(2,1)S(1)} %collective-permute-done.7.refs_1_.refs_4_), channel_id=1, source_target_pairs={{0,112},{8,120},{16,0},{24,8},{32,16},{40,24},{48,32},{56,40},{64,... | collective-permute-start | bytes 835592 | tf_op jit(solution)/shard_map/ppermute | solution.py:32
  55.0 13.5 %collective-permute-start.8 = (bf16[136,1024]{1,0:T(8,128)(2,1)S(1)}, bf16[136,1024]{1,0:T(8,128)(2,1)S(1)}, u32[]{:S(2)}, u32[]{:S(2)}) collective-permute-start(bf16[136,1024]{1,0:T(8,128)(2,1)S(1)} %collective-permute-done.6.refs_0_.refs_3_), channel_id=1, source_target_pairs={{0,16},{8,24},{16,32},{24,40},{32,48},{40,56},{48,64},{56,72},{64,... | collective-permute-start | bytes 835592 | tf_op jit(solution)/shard_map/ppermute | solution.py:32
  62.9 19.4 %collective-permute-start.11 = (bf16[72,1024]{1,0:T(8,128)(2,1)}, bf16[72,1024]{1,0:T(8,128)(2,1)}, u32[]{:S(2)}, u32[]{:S(2)}) collective-permute-start(bf16[72,1024]{1,0:T(8,128)(2,1)} %slice.227), channel_id=1, source_target_pairs={{0,112},{8,120},{16,0},{24,8},{32,16},{40,24},{48,32},{56,40},{64,... | collective-permute-start | bytes 442376 | tf_op jit(solution)/shard_map/ppermute | solution.py:32
  69.9 12.4 %collective-permute-start.10 = (bf16[64,1024]{1,0:T(8,128)(2,1)}, bf16[64,1024]{1,0:T(8,128)(2,1)}, u32[]{:S(2)}, u32[]{:S(2)}) collective-permute-start(bf16[64,1024]{1,0:T(8,128)(2,1)} %slice.226), channel_id=1, source_target_pairs={{0,16},{8,24},{16,32},{24,40},{32,48},{40,56},{48,64},{56,72},{64,... | collective-permute-start | bytes 393224 | tf_op jit(solution)/shard_map/ppermute | solution.py:32
  85.7 19.9 %all-to-all-start = ((bf16[8,160,128]{2,1,0:T(8,128)(2,1)}), bf16[8,160,128]{2,1,0:T(8,128)(2,1)S(1)}, u32[]{:S(2)}, u32[]{:S(2)}) async-start(bf16[8,160,128]{2,1,0:T(8,128)(2,1)} %send.1), calls=%async_computation | async-start | bytes 655360 | tf_op jit(solution)/shard_map/all_to_all | solution.py:391
  149.7 11.0 %collective-permute-start.23 = (bf16[128,1024]{1,0:T(8,128)(2,1)S(1)}, bf16[128,1024]{1,0:T(8,128)(2,1)S(1)}, u32[]{:S(2)}, u32[]{:S(2)}) collective-permute-start(bf16[128,1024]{1,0:T(8,128)(2,1)S(1)} %subtract_convert_fusion.refs_0_), channel_id=1, source_target_pairs={{0,112},{8,120},{16,0},{24,8},{32,16},{40,24},{48,32},{56,40},{64,... | collective-permute-start | bytes 786440 | tf_op jit(solution)/shard_map/ppermute | solution.py:32
  151.7 11.1 %collective-permute-start.22 = (bf16[128,1024]{1,0:T(8,128)(2,1)S(1)}, bf16[128,1024]{1,0:T(8,128)(2,1)S(1)}, u32[]{:S(2)}, u32[]{:S(2)}) collective-permute-start(bf16[128,1024]{1,0:T(8,128)(2,1)S(1)} %subtract_convert_fusion.refs_0_), channel_id=1, source_target_pairs={{0,16},{8,24},{16,32},{24,40},{32,48},{40,56},{48,64},{56,72},{64,... | collective-permute-start | bytes 786440 | tf_op jit(solution)/shard_map/ppermute | solution.py:32
  160.8 10.2 %collective-permute-start.25 = (bf16[128,1024]{1,0:T(8,128)(2,1)S(1)}, bf16[128,1024]{1,0:T(8,128)(2,1)S(1)}, u32[]{:S(2)}, u32[]{:S(2)}) collective-permute-start(bf16[128,1024]{1,0:T(8,128)(2,1)S(1)} %collective-permute-done.23.refs_2_), channel_id=1, source_target_pairs={{0,112},{8,120},{16,0},{24,8},{32,16},{40,24},{48,32},{56,40},{64,... | collective-permute-start | bytes 786440 | tf_op jit(solution)/shard_map/ppermute | solution.py:32
  162.8 12.2 %collective-permute-start.24 = (bf16[128,1024]{1,0:T(8,128)(2,1)S(1)}, bf16[128,1024]{1,0:T(8,128)(2,1)S(1)}, u32[]{:S(2)}, u32[]{:S(2)}) collective-permute-start(bf16[128,1024]{1,0:T(8,128)(2,1)S(1)} %collective-permute-done.22.refs_1_), channel_id=1, source_target_pairs={{0,16},{8,24},{16,32},{24,40},{32,48},{40,56},{48,64},{56,72},{64,... | collective-permute-start | bytes 786440 | tf_op jit(solution)/shard_map/ppermute | solution.py:32
  197.1 29.8 %collective-permute-start.35 = (bf16[4,128,1024]{2,1,0:T(8,128)(2,1)S(1)}, bf16[4,128,1024]{2,1,0:T(8,128)(2,1)S(1)}, u32[]{:S(2)}, u32[]{:S(2)}) collective-permute-start(bf16[4,128,1024]{2,1,0:T(8,128)(2,1)S(1)} %bitcast.53), channel_id=1, source_target_pairs={{0,8},{8,0},{16,24},{24,16},{32,40},{40,32},{48,56},{56,48},{64,72... | collective-permute-start | bytes 3145736 | tf_op jit(solution)/shard_map/ppermute | solution.py:32
  225.0 18.5 %collective-permute-start.30 = (bf16[4,136,1024]{2,1,0:T(8,128)(2,1)S(1)}, bf16[4,136,1024]{2,1,0:T(8,128)(2,1)S(1)}, u32[]{:S(2)}, u32[]{:S(2)}) collective-permute-start(bf16[4,136,1024]{2,1,0:T(8,128)(2,1)S(1)} %get-tuple-element.53), channel_id=1, source_target_pairs={{0,8},{8,0},{16,24},{24,16},{32,40},{40,32},{48,56},{56,48},{64,72... | collective-permute-start | bytes 3342344 | tf_op jit(solution)/shard_map/ppermute | solution.py:32
  236.3 23.8 %collective-permute-start.39 = (bf16[128,1024]{1,0:T(8,128)(2,1)S(1)}, bf16[128,1024]{1,0:T(8,128)(2,1)S(1)}, u32[]{:S(2)}, u32[]{:S(2)}) collective-permute-start(bf16[128,1024]{1,0:T(8,128)(2,1)S(1)} %pad_maximum_fusion.6), channel_id=1, source_target_pairs={{0,384},{8,392},{16,400},{24,408},{32,416},{40,424},{48,432},{56,4... | collective-permute-start | bytes 786440 | tf_op jit(solution)/shard_map/ppermute | solution.py:32
  238.3 21.8 %collective-permute-start.37 = (bf16[128,1024]{1,0:T(8,128)(2,1)S(1)}, bf16[128,1024]{1,0:T(8,128)(2,1)S(1)}, u32[]{:S(2)}, u32[]{:S(2)}) collective-permute-start(bf16[128,1024]{1,0:T(8,128)(2,1)S(1)} %pad_maximum_fusion.5), channel_id=1, source_target_pairs={{0,128},{8,136},{16,144},{24,152},{32,160},{40,168},{48,176},{56,1... | collective-permute-start | bytes 786440 | tf_op jit(solution)/shard_map/ppermute | solution.py:32
  245.8 11.2 %collective-permute-start.33 = (bf16[72,1024]{1,0:T(8,128)(2,1)S(1)}, bf16[72,1024]{1,0:T(8,128)(2,1)S(1)}, u32[]{:S(2)}, u32[]{:S(2)}) collective-permute-start(bf16[72,1024]{1,0:T(8,128)(2,1)S(1)} %slice_bitcast_fusion.4), channel_id=1, source_target_pairs={{0,384},{8,392},{16,400},{24,408},{32,416},{40,424},{48,432},{56,4... | collective-permute-start | bytes 442376 | tf_op jit(solution)/shard_map/ppermute | solution.py:32
  251.4 10.2 %collective-permute-start.32 = (bf16[136,1024]{1,0:T(8,128)(2,1)S(1)}, bf16[136,1024]{1,0:T(8,128)(2,1)S(1)}, u32[]{:S(2)}, u32[]{:S(2)}) collective-permute-start(bf16[136,1024]{1,0:T(8,128)(2,1)S(1)} %pad_maximum_fusion.1), channel_id=1, source_target_pairs={{0,128},{8,136},{16,144},{24,152},{32,160},{40,168},{48,176},{56,1... | collective-permute-start | bytes 835592 | tf_op jit(solution)/shard_map/ppermute | solution.py:32
  (58 other events, 535.4 us)

commit v2 on v1

v2 whole, which is shorter than its diff:
```python
import jax
import jax.numpy as jnp
from jax import lax
from jax.experimental import pallas as pl
from jax.experimental.pallas import tpu as pltpu
from jax.sharding import PartitionSpec as P

NX, NZ, NC, NY = 4, 8, 2, 8
BLOCK = 64
R = 128
COHERENCE = 128.0
LOSS_GRAD = 1.0 / 32.0
EPSILON = 1e-06
BF, F32, I32 = jnp.bfloat16, jnp.float32, jnp.int32
VMEM = 20 * 1024 * 1024
CAP = 24


def _place(x, z, c):
    return ((x % NX) * NZ + z % NZ) * NC + c % NC


def _perm(dx=0, dz=0, dc=0):
    return [
        (_place(x, z, c), _place(x + (dx if c == 0 else -dx), z + (dz if c == 0 else -dz), c + dc))
        for x in range(NX)
        for z in range(NZ)
        for c in range(NC)
    ]


def move(value, **shift):
    return lax.ppermute(value, "atoms", _perm(**shift))


def call(body, outs, *args, scratch=(), specs=None, name):
    return pl.pallas_call(
        body,
        out_shape=outs,
        in_specs=specs,
        scratch_shapes=scratch,
        compiler_params=pltpu.CompilerParams(vmem_limit_bytes=VMEM),
        name=name,
    )(*args)


def sds(shape, dtype):
    return jax.ShapeDtypeStruct(shape, dtype)


def whole(n):
    return [pl.BlockSpec(memory_space=pltpu.VMEM)] * n


SMEM_SPEC = pl.BlockSpec(memory_space=pltpu.SMEM)
ANY_SPEC = pl.BlockSpec(memory_space=pl.ANY)

NT = (((1,), (1,)), ((), ()))
NN = (((1,), (0,)), ((), ()))


def dot(a, b, dims):
    return lax.dot_general(a, b, dims, preferred_element_type=F32)


def rows_iota(shape):
    return lax.broadcasted_iota(I32, shape, 0)


def lanes_iota(shape):
    return lax.broadcasted_iota(I32, shape, 1)


def center_body(tokens, dec_bias, atom_ids, out):
    out[0:R, :] = (tokens[...].astype(F32) - dec_bias[...]).astype(BF)
    ids = atom_ids[...]
    owner = (ids >> 7).astype(F32).astype(BF)
    local = (ids & 127).astype(F32).astype(BF)
    row, col = rows_iota((8, 16)), lanes_iota((8, 16))
    even = (col == 2 * row).astype(F32).astype(BF)
    odd = (col == 2 * row + 1).astype(F32).astype(BF)
    out[R : R + 8, 0:128] = dot(even, owner, NT).astype(BF)
    out[R : R + 8, 128:256] = dot(even, local, NT).astype(BF)
    out[R : R + 8, 256:384] = dot(odd, local, NT).astype(BF)
    out[R : R + 8, 384:1024] = jnp.zeros((8, 640), BF)


def pack_body(encoder, decoder, enc_bias, after, out, gram):
    out[0:R, :] = encoder[...]
    out[R : 2 * R, :] = decoder[...]
    bias = jnp.broadcast_to(enc_bias[...], (8, 128))
    high = bias.astype(BF)
    rest = bias - high.astype(F32)
    mid = rest.astype(BF)
    low = (rest - mid.astype(F32)).astype(BF)
    out[2 * R : 2 * R + 8, 0:128] = high
    out[2 * R : 2 * R + 8, 128:256] = mid
    out[2 * R : 2 * R + 8, 256:384] = low
    out[2 * R : 2 * R + 8, 384:1024] = jnp.zeros((8, 640), BF)
    gram[...] = dot(decoder[...], decoder[...], NT)


def locate(ext, pos):
    x, z, c = pos[0], pos[1], pos[2]
    owner = ext[:, 0:128].astype(I32)
    first, second = ext[:, 128:256].astype(I32), ext[:, 256:384].astype(I32)
    dx = (((owner >> 4) - x) * (1 - 2 * (owner & 1)) + NX) & 3
    b = jnp.where(dx == 0, 0, jnp.where(dx == 3, 1, jnp.where(dx == 1, 2, 3)))
    b = b + jnp.where((owner & 1) == c, 0, 4)
    b = jnp.where(((owner >> 1) & 7) == z, b, -1)
    slot = rows_iota((8, 128))
    at_a = jnp.full((8, 128), -1, I32)
    at_b = jnp.full((8, 128), -1, I32)
    for g in range(8):
        hit = jnp.broadcast_to(b[g : g + 1, :], (8, 128)) == slot
        at_a = jnp.where(hit, jnp.broadcast_to(first[g : g + 1, :], (8, 128)), at_a)
        at_b = jnp.where(hit, jnp.broadcast_to(second[g : g + 1, :], (8, 128)), at_b)
    return at_a, at_b


def pick_into(out, tables, tok, places):
    n = len(places)
    atom = rows_iota((R, 128))
    for h, table in enumerate(tables):
        scores = dot(table[0 : 4 * R, :], tok, NT)
        for i in range(n):
            at_a, at_b = places[i]
            for q in range(4):
                b = 4 * h + q
                part = scores[q * R : (q + 1) * R, i * 128 : (i + 1) * 128]
                for s, at in ((0, at_a), (1, at_b)):
                    row = jnp.broadcast_to(at[b : b + 1, :], (R, 128))
                    got = jnp.sum(jnp.where(atom == row, part, 0.0), axis=0, keepdims=True)
                    out[16 * i + 8 * s + b : 16 * i + 8 * s + b + 1, :] = got


def score_body(pos, own, other, *refs):
    chunks, (picks, where) = refs[:-2], refs[-2:]
    places = [locate(c[R : R + 8, 0:384].astype(F32), pos) for c in chunks]
    for i, (at_a, at_b) in enumerate(places):
        where[16 * i : 16 * i + 8, :] = at_a
        where[16 * i + 8 : 16 * i + 16, :] = at_b
    toks = [c[0:R, :] for c in chunks]
    tok = toks[0] if len(toks) == 1 else jnp.concatenate(toks, axis=0)
    pick_into(picks, (own, other), tok, places)


def back_body(first):
    def body(own, other, where, *refs):
        chunks, picks = refs[:-1], refs[-1]
        toks = [c[...] for c in chunks]
        places = []
        for i in range(len(chunks)):
            at = 16 * (first + i)
            places.append((where[at : at + 8, :], where[at + 8 : at + 16, :]))
        tok = toks[0] if len(toks) == 1 else jnp.concatenate(toks, axis=0)
        pick_into(picks, (own, other), tok, places)

    return body


def halves_of(packed):
    first = jnp.concatenate([packed[16 * m : 16 * m + 8, :] for m in range(8)], axis=0)
    second = jnp.concatenate([packed[16 * m + 8 : 16 * m + 16, :] for m in range(8)], axis=0)
    return first, second


def squeeze(picks, live, rank):
    first, second = halves_of(picks)
    lane = lanes_iota((64, 128))
    left = jnp.where(live, lane - rank, 0)
    for k in range(7):
        step = 128 - (1 << k)
        left_in = pltpu.roll(left, step, 1)
        hit = ((left_in >> k) & 1) == 1
        first = jnp.where(hit, pltpu.roll(first, step, 1), first)
        second = jnp.where(hit, pltpu.roll(second, step, 1), second)
        left = jnp.where(hit, left_in, jnp.where(((left >> k) & 1) == 1, 0, left))
    lane = lanes_iota((32, 128))
    out = jnp.zeros((32, 128), F32)
    for q, part in enumerate((first[0:32], first[32:64], second[0:32], second[32:64])):
        moved = part if q == 0 else pltpu.roll(part, 32 * q, 1)
        out = jnp.where((lane >> 5) == q, moved, out)
    return out


def unsqueeze(got, rank):
    parts = [got] + [pltpu.roll(got, 128 - 32 * q, 1) for q in (1, 2, 3)]
    first = jnp.concatenate(parts[0:2], axis=0)
    second = jnp.concatenate(parts[2:4], axis=0)
    index = jnp.minimum(rank, CAP - 1)
    out = []
    for m in range(8):
        for half in (first, second):
            out.append(
                jnp.take_along_axis(
                    half[8 * m : 8 * m + 8, :], index[8 * m : 8 * m + 8, :], axis=1, mode="promise_in_bounds"
                )
            )
    return jnp.concatenate(out, axis=0)


def send_body(p0, p1, w0, w1, gram, out, where, ranks):
    picks = jnp.concatenate([p0[...], p1[...]], axis=0)
    at = jnp.concatenate([w0[...], w1[...]], axis=0)
    where[...] = at
    live = halves_of(at)[0] >= 0
    before = (rows_iota((128, 128)) < lanes_iota((128, 128))).astype(F32).astype(BF)
    rank = dot(jnp.where(live, 1.0, 0.0).astype(BF), before, NN).astype(I32)
    ranks[...] = rank
    sent = squeeze(picks, live, rank).astype(BF)
    high = gram[...].astype(BF)
    low = (gram[...] - high.astype(F32)).astype(BF)
    for d in range(NY):
        out[d, 0:32, :] = sent
        out[d, 32:48, :] = high[16 * d : 16 * d + 16, :]
        out[d, 48:64, :] = low[16 * d : 16 * d + 16, :]


def resend_body(p0, p1, where, ranks, rows, out):
    picks = jnp.concatenate([p0[...], p1[...]], axis=0)
    live = halves_of(where[...])[0] >= 0
    sent = squeeze(picks, live, ranks[...]).astype(BF)
    for d in range(NY):
        out[d, 0:32, :] = sent
        out[d, 32:64, :] = rows[...]


def total(got, lo, hi):
    acc = got[0, lo:hi, :].astype(F32)
    for d in range(1, NY):
        acc = acc + got[d, lo:hi, :].astype(F32)
    return acc


def table_rows(at_t, val_t, m, half):
    lane = lanes_iota((R, 128))
    parts = []
    for q in range(4):
        k = 16 * m + 4 * half + q
        first = jnp.where(lane == at_t[:, k : k + 1], val_t[:, k : k + 1], 0.0)
        second = jnp.where(lane == at_t[:, k + 8 : k + 9], val_t[:, k + 8 : k + 9], 0.0)
        parts.append((first + second).astype(BF))
    return jnp.concatenate(parts, axis=1)


def decode(at_t, val_t, own, other, ms):
    halves = []
    for half, table in enumerate((own, other)):
        rows = [table_rows(at_t, val_t, m, half) for m in ms]
        rows = rows[0] if len(ms) == 1 else jnp.concatenate(rows, axis=0)
        halves.append(dot(rows, table[0 : 4 * R, :], NN))
    return halves[0] + halves[1]


def act_body(got, own, other, where, ranks, act, at_t, act_t, gram_rows, out):
    pre = unsqueeze(total(got, 0, 32), ranks[...])
    bias = []
    for table in (own, other):
        for q in range(4):
            ext = table[4 * R + 8 * q : 4 * R + 8 * q + 8, 0:384].astype(F32)
            bias.append((ext[0:1, 0:128] + ext[0:1, 128:256]) + ext[0:1, 256:384])
    bias = jnp.concatenate(bias, axis=0)
    at = where[...]
    shift = [
        jnp.take_along_axis(bias, jnp.maximum(at[8 * k : 8 * k + 8, :], 0), axis=1, mode="promise_in_bounds")
        for k in range(16)
    ]
    pre = pre + jnp.concatenate(shift, axis=0)
    value = jnp.where(at >= 0, pre.astype(BF).astype(F32), 0.0)
    act[...] = value
    turned = at.astype(F32).T.astype(I32)
    value_t = value.T
    at_t[...] = turned
    act_t[...] = value_t
    rows = total(got, 32, 48) + total(got, 48, 64)
    high = rows.astype(BF)
    gram_rows[0:16, :] = high
    gram_rows[16:32, :] = (rows - high.astype(F32)).astype(BF)
    out[...] = decode(turned, value_t, own, other, (7,)).astype(BF)


def decode_body(ms):
    def body(at_t, act_t, own, other, *outs):
        got = decode(at_t[...], act_t[...], own, other, ms)
        for i, out in enumerate(outs):
            out[...] = got[i * R : (i + 1) * R, :].astype(out.dtype)

    return body


def turned_table(at, val, b):
    atom = rows_iota((R, 128))
    parts = []
    for m in range(8):
        k = 16 * m + b
        first = jnp.where(atom == at[k : k + 1, :], val[k : k + 1, :], 0.0)
        second = jnp.where(atom == at[k + 8 : k + 9, :], val[k + 8 : k + 9, :], 0.0)
        parts.append(first + second)
    return parts


def load_rows(refs, rows, sem):
    copies = [
        pltpu.make_async_copy(ref.at[pl.ds(0, R)], rows.at[pl.ds(i * R, R)], sem.at[i]) for i, ref in enumerate(refs)
    ]
    for copy in copies:
        copy.start()
    return copies


def fitted_body(half):
    def body(at, act, after, *refs):
        chunks, (out, rows, sem) = refs[:8], refs[8:]
        copies = load_rows(chunks, rows, sem)
        parts = [jnp.concatenate(turned_table(at, act, 4 * half + q), axis=1).astype(BF) for q in range(4)]
        table = jnp.concatenate(parts, axis=0)
        for copy in copies:
            copy.wait()
        out[...] = (dot(table, rows[...], NN) * LOSS_GRAD).astype(BF)

    return body


def encgrad_body(half):
    def body(got, at, ranks, *refs):
        chunks, rest = refs[:8], refs[8:]
        out, (rows, sem) = rest[0], rest[-2:]
        copies = load_rows(chunks, rows, sem)
        grad = jnp.where(at[...] >= 0, unsqueeze(total(got, 0, 32), ranks[...]) * LOSS_GRAD, 0.0)
        if half == 0:
            gram = rest[1]
            for d in range(NY):
                gram[16 * d : 16 * d + 16, :] = got[d, 32:48, :].astype(F32) + got[d, 48:64, :].astype(F32)
        parts, ones = [], jnp.ones((8, 128), F32)
        for q in range(4):
            pieces = turned_table(at, grad, 4 * half + q)
            acc = pieces[0]
            for piece in pieces[1:]:
                acc = acc + piece
            sums = lax.dot_general(ones, acc, NT, precision=lax.Precision.HIGHEST, preferred_element_type=F32)
            out[q, R : R + 8, 0:128] = sums.astype(BF)
            out[q, R : R + 8, 128:1024] = jnp.zeros((8, 896), BF)
            parts.append(jnp.concatenate(pieces, axis=1).astype(BF))
        table = jnp.concatenate(parts, axis=0)
        for copy in copies:
            copy.wait()
        part = dot(table, rows[...], NN).astype(BF)
        for q in range(4):
            out[q, 0:R, :] = part[q * R : (q + 1) * R, :]

    return body


def penalty_body(count, gram_ref, decoder, out):
    gram = gram_ref[...]
    row, col = rows_iota((R, R)), lanes_iota((R, R))
    diagonal = row == col
    kept = jnp.where(diagonal, gram, 0.0)
    norm_c = jnp.sqrt(jnp.sum(kept, axis=1, keepdims=True) + EPSILON)
    norm_r = jnp.sqrt(jnp.sum(kept, axis=0, keepdims=True) + EPSILON)
    live = count[0] * BLOCK
    pair = norm_c * norm_r
    cosine = gram / pair
    alive = (row < live) & (col < live) & jnp.logical_not(diagonal)
    coupled = jnp.where(alive, cosine, 0.0)
    spread = jnp.sum(coupled * cosine, axis=1, keepdims=True)
    diag_term = jnp.where(diagonal, spread / (norm_c * norm_c), 0.0)
    weights = (4.0 * COHERENCE * (coupled / pair - diag_term)).astype(BF)
    out[...] = dot(weights, decoder[...], NN)


def add(a, b):
    return (a.astype(F32) + b.astype(F32)).astype(BF)


def gather_z(own):
    f1, b1 = move(own, dz=1), move(own, dz=-1)
    f2, b2 = move(f1, dz=1), move(b1, dz=-1)
    f3, b3 = move(f2, dz=1), move(b2, dz=-1)
    return [own, f1, b1, f2, b2, f3, b3, move(f3, dz=1)]


def scatter_x(own, theirs):
    blocks = [add(own[i], theirs[i]) for i in range(4)]
    to_next = add(blocks[2], move(blocks[3], dx=1))
    return blocks[0], move(blocks[1], dx=-1), move(to_next, dx=1)


def per_device(tokens, dec_bias, encoder, enc_bias, decoder, atom_ids, block_count):
    place = lax.axis_index("atoms")
    pos = jnp.stack([place >> 4, (place >> 1) & 7, place & 1]).astype(I32)
    bias_row = dec_bias.reshape(1, -1)

    sent = call(center_body, sds((R + 8, 1024), BF), tokens, bias_row, atom_ids, specs=whole(3), name="center")
    packed, gram_part = call(
        pack_body,
        (sds((2 * R + 8, 1024), BF), sds((R, R), F32)),
        encoder, decoder, enc_bias.reshape(1, -1), sent, specs=whole(3) + [ANY_SPEC], name="pack",
    )
    tok = gather_z(sent)

    x1, x2 = move(packed, dx=1), move(packed, dx=-1)
    x3 = move(x1, dx=1)
    enc_own = jnp.concatenate([encoder, x1[:R], x2[:R], x3[:R]], axis=0)
    dec_own = jnp.concatenate(
        [decoder, x1[R : 2 * R], x2[R : 2 * R], x3[R : 2 * R], packed[2 * R :], x1[2 * R :], x2[2 * R :], x3[2 * R :]],
        axis=0,
    )
    enc_other = move(enc_own, dc=1)
    dec_other = move(dec_own, dc=1)

    def score(chunks):
        n = len(chunks)
        return call(
            score_body,
            (sds((16 * n, 128), F32), sds((16 * n, 128), I32)),
            pos, enc_own, enc_other, *chunks,
            specs=[SMEM_SPEC] + whole(2 + n), name="score",
        )

    picks, wheres = zip(score(tok[0:7]), score(tok[7:8]))
    out, where, ranks = call(
        send_body, (sds((NY, 64, 128), BF), sds((R, R), I32), sds((64, R), I32)),
        *picks, *wheres, gram_part, specs=whole(5), name="send",
    )
    got = lax.all_to_all(out, "width", split_axis=0, concat_axis=0, tiled=True)

    act, at_t, act_t, gram_rows, d7 = call(
        act_body,
        (sds((R, R), F32), sds((R, R), I32), sds((R, R), F32), sds((32, 128), BF), sds((R, 1024), BF)),
        got, dec_own, dec_other, where, ranks, specs=whole(5), name="act",
    )

    def decoded(ms, dtype=BF):
        return call(
            decode_body(ms), tuple(sds((R, 1024), dtype) for _ in ms),
            at_t, act_t, dec_own, dec_other, specs=whole(4), name="decode",
        )

    d5, d6 = decoded((5, 6))
    d3, d4 = decoded((3, 4))
    d1, d2 = decoded((1, 2))
    (d0,) = decoded((0,), F32)
    f = move(d7, dz=1)
    b = move(d5, dz=-1)
    f = move(add(d6, f), dz=1)
    b = move(add(d3, b), dz=-1)
    f = move(add(d4, f), dz=1)
    b = move(add(d1, b), dz=-1)
    f = move(add(d2, f), dz=1)
    summed = d0 + f.astype(F32) + b.astype(F32)
    residual = (summed + bias_row - tokens.astype(F32)).astype(BF)

    res = gather_z(residual)

    def back(chunks, first):
        n = len(chunks)
        return call(
            back_body(first), sds((16 * n, 128), F32),
            dec_own, dec_other, where, *chunks, specs=whole(3 + n), name="back",
        )

    backs = (back(res[0:7], 0), back(res[7:8], 7))
    out2 = call(
        resend_body, sds((NY, 64, 128), BF), *backs, where, ranks, gram_rows, specs=whole(5), name="resend"
    )
    got2 = lax.all_to_all(out2, "width", split_axis=0, concat_axis=0, tiled=True)

    scratch = [pltpu.VMEM((8 * R, 1024), BF), pltpu.SemaphoreType.DMA((8,))]

    def fitted(half, after):
        return call(
            fitted_body(half), sds((4 * R, 1024), BF), where, act, after, *res,
            specs=whole(2) + [ANY_SPEC] * 9, scratch=scratch, name="fitted",
        )

    fit_other = fitted(1, out2)
    fit_theirs = move(fit_other, dc=1)
    fit_own = fitted(0, fit_other)
    fit = scatter_x(fit_own.reshape(4, R, 1024), fit_theirs.reshape(4, R, 1024))

    def encgrad(half):
        outs = [sds((4, R + 8, 1024), BF)] + ([sds((R, R), F32)] if half == 0 else [])
        return call(
            encgrad_body(half), tuple(outs), got2, where, ranks, *tok,
            specs=whole(3) + [ANY_SPEC] * 8, scratch=scratch, name="encgrad",
        )

    (eg_other,) = encgrad(1)
    eg_theirs = move(eg_other, dc=1)
    eg_own, gram = encgrad(0)
    eg = scatter_x(eg_own, eg_theirs)
    eg_sum = eg[0].astype(F32) + eg[1].astype(F32) + eg[2].astype(F32)
    encoder_grad = eg_sum[:R].astype(BF)
    bias_grad = eg_sum[R, 0:R]

    penalty = call(
        penalty_body, sds((R, 1024), F32), block_count, gram, decoder, specs=[SMEM_SPEC] + whole(2), name="penalty"
    )
    decoder_grad = (fit[0].astype(F32) + fit[1].astype(F32) + fit[2].astype(F32) + penalty).astype(BF)
    return (residual, encoder_grad, decoder_grad, bias_grad)


def solution(mesh):
    in_specs = (
        P("atoms", "width"),
        P("width"),
        P("atoms", "width"),
        P("atoms"),
        P("atoms", "width"),
        P("atoms", None),
        P("atoms"),
    )
    out_specs = (P("atoms", "width"), P("atoms", "width"), P("atoms", "width"), P("atoms"))
    return jax.shard_map(per_device, mesh=mesh, in_specs=in_specs, out_specs=out_specs, check_vma=False)
```

time: 270 us -> 246 us (0.911)
  the two profiles are of different devices: /device:TPU:6 before, /device:TPU:8 now
where the time goes in v2:
time: 246 us; the launch traced here: 244 us
  starting transfers between devices  131 us (53%)
  waiting for transfers between devices  55.2 us (22%)
  Pallas kernels  31 us (13%)
  local copies, waits for them, and re-layouts  19.9 us (8%)
  other arithmetic  5.27 us (2%)
    ppermute x34, starting transfers between devices, move(): return lax.ppermute(value, 'atoms', _perm(**shift))  119 us
    ppermute x34, waiting for transfers between devices, move(): return lax.ppermute(value, 'atoms', _perm(**shift))  47.6 us
    pallas_call x18, Pallas kernels, call(): pl.pallas_call(body, out_shape=outs, in_specs=specs, scratch_shapes=scrat...  31 us
    unnamed x96, local copies, waits for them, and re-layouts  18.6 us
    all_to_all x1, waiting for transfers between devices, per_device(): got = lax.all_to_all(out, 'width', split_axis=0, concat_axis=0, tiled=True)  7.62 us
    all_to_all x1, starting transfers between devices, per_device(): got = lax.all_to_all(out, 'width', split_axis=0, concat_axis=0, tiled=True)  7.58 us
  transfers between devices with their start and end apart: 36, of which 22 were waited for; matrix products, arithmetic and copies ran while one was open for 2% of the time, Pallas kernels for 11%

profile of v2, /device:TPU:8, one launch (start us, length us, event | category | flops | bytes accessed | tf_op | source)
XLA Modules:
  0.0 244.5 jit_solution(11221670947185838542)
XLA Ops:
  9.5 3.7 %collective-permute-start.1 = (bf16[264,1024]{1,0:T(8,128)(2,1)S(1)}, bf16[264,1024]{1,0:T(8,128)(2,1)S(1)}, u32[]{:S(2)}, u32[]{:S(2)}) collective-permute-start(bf16[264,1024]{1,0:T(8,128)(2,1)S(1)} %get-tuple-element.26), channel_id=1, source_target_pairs={{0,384},{8,136},{16,400},{24,152},{32,416},{40,168},{48,432},{56,1... | collective-permute-start | bytes 1622024 | tf_op jit(solution)/shard_map/ppermute | solution.py:33
  13.2 4.3 %collective-permute-start.4 = (bf16[136,1024]{1,0:T(8,128)(2,1)S(1)}, bf16[136,1024]{1,0:T(8,128)(2,1)S(1)}, u32[]{:S(2)}, u32[]{:S(2)}) collective-permute-start(bf16[136,1024]{1,0:T(8,128)(2,1)S(1)} %center.1.after.refs_0_), channel_id=1, source_target_pairs={{0,16},{8,120},{16,32},{24,8},{32,48},{40,24},{48,64},{56,40},{64,... | collective-permute-start | bytes 835592 | tf_op jit(solution)/shard_map/ppermute | solution.py:33
  17.5 3.6 %collective-permute-done = bf16[264,1024]{1,0:T(8,128)(2,1)S(1)} collective-permute-done((bf16[264,1024]{1,0:T(8,128)(2,1)S(1)}, bf16[264,1024]{1,0:T(8,128)(2,1)S(1)}, u32[]{:S(2)}, u32[]{:S(2)}) %collective-permute-start) | collective-permute-done | bytes 540704 | tf_op jit(solution)/shard_map/ppermute | solution.py:33
  24.7 9.1 %collective-permute-done.2 = bf16[264,1024]{1,0:T(8,128)(2,1)S(1)} collective-permute-done((bf16[264,1024]{1,0:T(8,128)(2,1)S(1)}, bf16[264,1024]{1,0:T(8,128)(2,1)S(1)}, u32[]{:S(2)}, u32[]{:S(2)}) %collective-permute-start.2) | collective-permute-done | bytes 540704 | tf_op jit(solution)/shard_map/ppermute | solution.py:33
  38.3 4.3 %collective-permute-start.6 = (bf16[136,1024]{1,0:T(8,128)(2,1)S(1)}, bf16[136,1024]{1,0:T(8,128)(2,1)S(1)}, u32[]{:S(2)}, u32[]{:S(2)}) collective-permute-start(bf16[136,1024]{1,0:T(8,128)(2,1)S(1)} %collective-permute-done.4.refs_1_), channel_id=1, source_target_pairs={{0,16},{8,120},{16,32},{24,8},{32,48},{40,24},{48,64},{56,40},{64,... | collective-permute-start | bytes 835592 | tf_op jit(solution)/shard_map/ppermute | solution.py:33
  43.3 8.6 %collective-permute-start.5 = (bf16[136,1024]{1,0:T(8,128)(2,1)S(1)}, bf16[136,1024]{1,0:T(8,128)(2,1)S(1)}, u32[]{:S(2)}, u32[]{:S(2)}) collective-permute-start(bf16[136,1024]{1,0:T(8,128)(2,1)S(1)} %center.1.after.refs_0_), channel_id=1, source_target_pairs={{0,112},{8,24},{16,0},{24,40},{32,16},{40,56},{48,32},{56,72},{64,... | collective-permute-start | bytes 835592 | tf_op jit(solution)/shard_map/ppermute | solution.py:33
  56.4 5.1 %collective-permute-start.7 = (bf16[136,1024]{1,0:T(8,128)(2,1)S(1)}, bf16[136,1024]{1,0:T(8,128)(2,1)}, u32[]{:S(2)}, u32[]{:S(2)}) collective-permute-start(bf16[136,1024]{1,0:T(8,128)(2,1)S(1)} %collective-permute-done.5.refs_2_), channel_id=1, source_target_pairs={{0,112},{8,24},{16,0},{24,40},{32,16},{40,56},{48,32},{56,72},{64,... | collective-permute-start | bytes 835592 | tf_op jit(solution)/shard_map/ppermute | solution.py:33
  65.6 5.7 %collective-permute-start.9 = (bf16[136,1024]{1,0:T(8,128)(2,1)}, bf16[136,1024]{1,0:T(8,128)(2,1)}, u32[]{:S(2)}, u32[]{:S(2)}) collective-permute-start(bf16[136,1024]{1,0:T(8,128)(2,1)} %collective-permute-done.7.refs_4_), channel_id=1, source_target_pairs={{0,112},{8,24},{16,0},{24,40},{32,16},{40,56},{48,32},{56,72},{64,... | collective-permute-start | bytes 835592 | tf_op jit(solution)/shard_map/ppermute | solution.py:33
  71.4 3.9 %collective-permute-done.10.refs_0_.refs_7_ = bf16[136,1024]{1,0:T(8,128)(2,1)} collective-permute-done((bf16[136,1024]{1,0:T(8,128)(2,1)}, bf16[136,1024]{1,0:T(8,128)(2,1)}, u32[]{:S(2)}, u32[]{:S(2)}) %collective-permute-start.10) | collective-permute-done | bytes 278560 | tf_op jit(solution)/shard_map/ppermute | solution.py:33
  77.4 4.5 %score.2 = (f32[112,128]{1,0:T(8,128)S(1)}, s32[112,128]{1,0:T(8,128)S(1)}) custom-call(s32[3]{0:T(128)S(1)} %pad_add_fusion.pos, bf16[512,1024]{1,0:T(8,128)(2,1)S(1)} %pad_maximum_fusion.own, bf16[512,1024]{1,0:T(8,128)(2,1)} %collective-permute-done.3.other, bf16[136,1024]{1,0:T(8,128)(2,1)S(1)} %center.1.after.refs_0_, bf16[136,1024]{1,0:T(8,128)(2,1)S(1)} %copy-done.2, ...), custom_call_target="tpu_custom_call" | custom-call | tf_op jit(solution)/shard_map/score/pallas_call | solution.py:37
  83.2 7.6 %all-to-all-start = ((bf16[8,64,128]{2,1,0:T(8,128)(2,1)}), bf16[8,64,128]{2,1,0:T(8,128)(2,1)S(1)}, u32[]{:S(2)}, u32[]{:S(2)}) async-start(bf16[8,64,128]{2,1,0:T(8,128)(2,1)} %get-tuple-element.32), calls=%async_computation | async-start | bytes 262144 | tf_op jit(solution)/shard_map/all_to_all | solution.py:427
  90.8 7.6 %all-to-all-done.got = bf16[8,64,128]{2,1,0:T(8,128)(2,1)S(1)} async-done(((bf16[8,64,128]{2,1,0:T(8,128)(2,1)}), bf16[8,64,128]{2,1,0:T(8,128)(2,1)S(1)}, u32[]{:S(2)}, u32[]{:S(2)}) %all-to-all-start) | async-done | bytes 131104 | tf_op jit(solution)/shard_map/all_to_all | solution.py:427
  103.9 5.1 %collective-permute-start.16 = (bf16[128,1024]{1,0:T(8,128)(2,1)S(1)}, bf16[128,1024]{1,0:T(8,128)(2,1)S(1)}, u32[]{:S(2)}, u32[]{:S(2)}) collective-permute-start(bf16[128,1024]{1,0:T(8,128)(2,1)S(1)} %get-tuple-element.43), channel_id=1, source_target_pairs={{0,112},{8,24},{16,0},{24,40},{32,16},{40,56},{48,32},{56,72},{64,... | collective-permute-start | bytes 786440 | tf_op jit(solution)/shard_map/ppermute | solution.py:33
  109.5 3.7 %collective-permute-start.13 = (bf16[128,1024]{1,0:T(8,128)(2,1)S(1)}, bf16[128,1024]{1,0:T(8,128)(2,1)S(1)}, u32[]{:S(2)}, u32[]{:S(2)}) collective-permute-start(bf16[128,1024]{1,0:T(8,128)(2,1)S(1)} %add_convert_fusion.14), channel_id=1, source_target_pairs={{0,16},{8,120},{16,32},{24,8},{32,48},{40,24},{48,64},{56,40},{64,... | collective-permute-start | bytes 786440 | tf_op jit(solution)/shard_map/ppermute | solution.py:33
  115.8 4.9 %collective-permute-start.17 = (bf16[128,1024]{1,0:T(8,128)(2,1)S(1)}, bf16[128,1024]{1,0:T(8,128)(2,1)S(1)}, u32[]{:S(2)}, u32[]{:S(2)}) collective-permute-start(bf16[128,1024]{1,0:T(8,128)(2,1)S(1)} %add_convert_fusion.11), channel_id=1, source_target_pairs={{0,112},{8,24},{16,0},{24,40},{32,16},{40,56},{48,32},{56,72},{64,... | collective-permute-start | bytes 786440 | tf_op jit(solution)/shard_map/ppermute | solution.py:33
  127.1 5.5 %collective-permute-start.18 = (bf16[128,1024]{1,0:T(8,128)(2,1)S(1)}, bf16[128,1024]{1,0:T(8,128)(2,1)S(1)}, u32[]{:S(2)}, u32[]{:S(2)}) collective-permute-start(bf16[128,1024]{1,0:T(8,128)(2,1)S(1)} %add_convert_fusion.10), channel_id=1, source_target_pairs={{0,112},{8,24},{16,0},{24,40},{32,16},{40,56},{48,32},{56,72},{64,... | collective-permute-start | bytes 786440 | tf_op jit(solution)/shard_map/ppermute | solution.py:33
  137.9 6.4 %collective-permute-done.15 = bf16[128,1024]{1,0:T(8,128)(2,1)S(1)} collective-permute-done((bf16[128,1024]{1,0:T(8,128)(2,1)S(1)}, bf16[128,1024]{1,0:T(8,128)(2,1)S(1)}, u32[]{:S(2)}, u32[]{:S(2)}) %collective-permute-start.15) | collective-permute-done | bytes 262176 | tf_op jit(solution)/shard_map/ppermute | solution.py:33
  146.4 5.1 %collective-permute-start.20 = (bf16[128,1024]{1,0:T(8,128)(2,1)S(1)}, bf16[128,1024]{1,0:T(8,128)(2,1)S(1)}, u32[]{:S(2)}, u32[]{:S(2)}) collective-permute-start(bf16[128,1024]{1,0:T(8,128)(2,1)S(1)} %subtract_convert_fusion.refs_0_), channel_id=1, source_target_pairs={{0,112},{8,24},{16,0},{24,40},{32,16},{40,56},{48,32},{56,72},{64,... | collective-permute-start | bytes 786440 | tf_op jit(solution)/shard_map/ppermute | solution.py:33
  156.5 5.6 %collective-permute-start.22 = (bf16[128,1024]{1,0:T(8,128)(2,1)S(1)}, bf16[128,1024]{1,0:T(8,128)(2,1)S(1)}, u32[]{:S(2)}, u32[]{:S(2)}) collective-permute-start(bf16[128,1024]{1,0:T(8,128)(2,1)S(1)} %collective-permute-done.20.refs_2_), channel_id=1, source_target_pairs={{0,112},{8,24},{16,0},{24,40},{32,16},{40,56},{48,32},{56,72},{64,... | collective-permute-start | bytes 786440 | tf_op jit(solution)/shard_map/ppermute | solution.py:33
  166.3 5.6 %collective-permute-start.24 = (bf16[128,1024]{1,0:T(8,128)(2,1)S(1)}, bf16[128,1024]{1,0:T(8,128)(2,1)S(1)}, u32[]{:S(2)}, u32[]{:S(2)}) collective-permute-start(bf16[128,1024]{1,0:T(8,128)(2,1)S(1)} %collective-permute-done.22.refs_4_), channel_id=1, source_target_pairs={{0,112},{8,24},{16,0},{24,40},{32,16},{40,56},{48,32},{56,72},{64,... | collective-permute-start | bytes 786440 | tf_op jit(solution)/shard_map/ppermute | solution.py:33
  184.3 4.6 %all-to-all-start.1 = ((bf16[8,64,128]{2,1,0:T(8,128)(2,1)}), bf16[8,64,128]{2,1,0:T(8,128)(2,1)S(1)}, u32[]{:S(2)}, u32[]{:S(2)}) async-start(bf16[8,64,128]{2,1,0:T(8,128)(2,1)} %resend.1.after), calls=%async_computation.1 | async-start | bytes 262144 | tf_op jit(solution)/shard_map/all_to_all | solution.py:468
  217.8 4.5 %collective-permute-start.28 = (bf16[136,1024]{1,0:T(8,128)(2,1)S(1)}, bf16[136,1024]{1,0:T(8,128)(2,1)S(1)}, u32[]{:S(2)}, u32[]{:S(2)}) collective-permute-start(bf16[136,1024]{1,0:T(8,128)(2,1)S(1)} %get-tuple-element.49), channel_id=1, source_target_pairs={{0,128},{8,392},{16,144},{24,408},{32,160},{40,424},{48,176},{56,4... | collective-permute-start | bytes 835592 | tf_op jit(solution)/shard_map/ppermute | solution.py:33
  229.2 4.0 %collective-permute-start.27 = (bf16[136,1024]{1,0:T(8,128)(2,1)S(1)}, bf16[136,1024]{1,0:T(8,128)(2,1)S(1)}, u32[]{:S(2)}, u32[]{:S(2)}) collective-permute-start(bf16[136,1024]{1,0:T(8,128)(2,1)S(1)} %get-tuple-element.48), channel_id=1, source_target_pairs={{0,384},{8,136},{16,400},{24,152},{32,416},{40,168},{48,432},{56,1... | collective-permute-start | bytes 835592 | tf_op jit(solution)/shard_map/ppermute | solution.py:33
  238.9 4.2 %collective-permute-done.29 = bf16[136,1024]{1,0:T(8,128)(2,1)S(1)} collective-permute-done((bf16[136,1024]{1,0:T(8,128)(2,1)S(1)}, bf16[136,1024]{1,0:T(8,128)(2,1)S(1)}, u32[]{:S(2)}, u32[]{:S(2)}) %collective-permute-start.29) | collective-permute-done | bytes 278560 | tf_op jit(solution)/shard_map/ppermute | solution.py:33
  (179 shorter events, 115.1 us)
Async XLA Ops:
  6.1 15.0 %collective-permute-start = (bf16[264,1024]{1,0:T(8,128)(2,1)S(1)}, bf16[264,1024]{1,0:T(8,128)(2,1)S(1)}, u32[]{:S(2)}, u32[]{:S(2)}) collective-permute-start(bf16[264,1024]{1,0:T(8,128)(2,1)S(1)} %get-tuple-element.26), channel_id=1, source_target_pairs={{0,128},{8,392},{16,144},{24,408},{32,160},{40,424},{48,176},{56,4... | collective-permute-start | bytes 1622024 | tf_op jit(solution)/shard_map/ppermute | solution.py:33
  9.5 15.1 %collective-permute-start.1 = (bf16[264,1024]{1,0:T(8,128)(2,1)S(1)}, bf16[264,1024]{1,0:T(8,128)(2,1)S(1)}, u32[]{:S(2)}, u32[]{:S(2)}) collective-permute-start(bf16[264,1024]{1,0:T(8,128)(2,1)S(1)} %get-tuple-element.26), channel_id=1, source_target_pairs={{0,384},{8,136},{16,400},{24,152},{32,416},{40,168},{48,432},{56,1... | collective-permute-start | bytes 1622024 | tf_op jit(solution)/shard_map/ppermute | solution.py:33
  13.2 25.1 %collective-permute-start.4 = (bf16[136,1024]{1,0:T(8,128)(2,1)S(1)}, bf16[136,1024]{1,0:T(8,128)(2,1)S(1)}, u32[]{:S(2)}, u32[]{:S(2)}) collective-permute-start(bf16[136,1024]{1,0:T(8,128)(2,1)S(1)} %center.1.after.refs_0_), channel_id=1, source_target_pairs={{0,16},{8,120},{16,32},{24,8},{32,48},{40,24},{48,64},{56,40},{64,... | collective-permute-start | bytes 835592 | tf_op jit(solution)/shard_map/ppermute | solution.py:33
  21.1 12.7 %collective-permute-start.2 = (bf16[264,1024]{1,0:T(8,128)(2,1)S(1)}, bf16[264,1024]{1,0:T(8,128)(2,1)S(1)}, u32[]{:S(2)}, u32[]{:S(2)}) collective-permute-start(bf16[264,1024]{1,0:T(8,128)(2,1)S(1)} %collective-permute-done), channel_id=1, source_target_pairs={{0,128},{8,392},{16,144},{24,408},{32,160},{40,424},{48,176},{56,4... | collective-permute-start | bytes 1622024 | tf_op jit(solution)/shard_map/ppermute | solution.py:33
  33.9 41.4 %collective-permute-start.3 = (bf16[512,1024]{1,0:T(8,128)(2,1)S(1)}, bf16[512,1024]{1,0:T(8,128)(2,1)}, u32[]{:S(2)}, u32[]{:S(2)}) collective-permute-start(bf16[512,1024]{1,0:T(8,128)(2,1)S(1)} %pad_maximum_fusion.own), channel_id=1, source_target_pairs={{0,8},{8,0},{16,24},{24,16},{32,40},{40,32},{48,56},{56,48},{64,72... | collective-permute-start | bytes 3145736 | tf_op jit(solution)/shard_map/ppermute | solution.py:33
  35.9 54.9 %collective-permute-start.11 = (bf16[544,1024]{1,0:T(8,128)(2,1)S(1)}, bf16[544,1024]{1,0:T(8,128)(2,1)S(1)}, u32[]{:S(2)}, u32[]{:S(2)}) collective-permute-start(bf16[544,1024]{1,0:T(8,128)(2,1)S(1)} %constant_dynamic-update-slice_fusion.own), channel_id=1, source_target_pairs={{0,8},{8,0},{16,24},{24,16},{32,40},{40,32},{48,56},{56,48},{64,72... | collective-permute-start | bytes 3342344 | tf_op jit(solution)/shard_map/ppermute | solution.py:33
  38.3 15.5 %collective-permute-start.6 = (bf16[136,1024]{1,0:T(8,128)(2,1)S(1)}, bf16[136,1024]{1,0:T(8,128)(2,1)S(1)}, u32[]{:S(2)}, u32[]{:S(2)}) collective-permute-start(bf16[136,1024]{1,0:T(8,128)(2,1)S(1)} %collective-permute-done.4.refs_1_), channel_id=1, source_target_pairs={{0,16},{8,120},{16,32},{24,8},{32,48},{40,24},{48,64},{56,40},{64,... | collective-permute-start | bytes 835592 | tf_op jit(solution)/shard_map/ppermute | solution.py:33
  43.3 13.1 %collective-permute-start.5 = (bf16[136,1024]{1,0:T(8,128)(2,1)S(1)}, bf16[136,1024]{1,0:T(8,128)(2,1)S(1)}, u32[]{:S(2)}, u32[]{:S(2)}) collective-permute-start(bf16[136,1024]{1,0:T(8,128)(2,1)S(1)} %center.1.after.refs_0_), channel_id=1, source_target_pairs={{0,112},{8,24},{16,0},{24,40},{32,16},{40,56},{48,32},{56,72},{64,... | collective-permute-start | bytes 835592 | tf_op jit(solution)/shard_map/ppermute | solution.py:33
  63.5 11.8 %collective-permute-start.10 = (bf16[136,1024]{1,0:T(8,128)(2,1)}, bf16[136,1024]{1,0:T(8,128)(2,1)}, u32[]{:S(2)}, u32[]{:S(2)}) collective-permute-start(bf16[136,1024]{1,0:T(8,128)(2,1)} %collective-permute-done.8.refs_5_), channel_id=1, source_target_pairs={{0,16},{8,120},{16,32},{24,8},{32,48},{40,24},{48,64},{56,40},{64,... | collective-permute-start | bytes 835592 | tf_op jit(solution)/shard_map/ppermute | solution.py:33
  65.6 11.7 %collective-permute-start.9 = (bf16[136,1024]{1,0:T(8,128)(2,1)}, bf16[136,1024]{1,0:T(8,128)(2,1)}, u32[]{:S(2)}, u32[]{:S(2)}) collective-permute-start(bf16[136,1024]{1,0:T(8,128)(2,1)} %collective-permute-done.7.refs_4_), channel_id=1, source_target_pairs={{0,112},{8,24},{16,0},{24,40},{32,16},{40,56},{48,32},{56,72},{64,... | collective-permute-start | bytes 835592 | tf_op jit(solution)/shard_map/ppermute | solution.py:33
  83.2 15.2 %all-to-all-start = ((bf16[8,64,128]{2,1,0:T(8,128)(2,1)}), bf16[8,64,128]{2,1,0:T(8,128)(2,1)S(1)}, u32[]{:S(2)}, u32[]{:S(2)}) async-start(bf16[8,64,128]{2,1,0:T(8,128)(2,1)} %get-tuple-element.32), calls=%async_computation | async-start | bytes 262144 | tf_op jit(solution)/shard_map/all_to_all | solution.py:427
  99.6 9.9 %collective-permute-start.12 = (bf16[128,1024]{1,0:T(8,128)(2,1)S(1)}, bf16[128,1024]{1,0:T(8,128)(2,1)S(1)}, u32[]{:S(2)}, u32[]{:S(2)}) collective-permute-start(bf16[128,1024]{1,0:T(8,128)(2,1)S(1)} %get-tuple-element.40), channel_id=1, source_target_pairs={{0,16},{8,120},{16,32},{24,8},{32,48},{40,24},{48,64},{56,40},{64,... | collective-permute-start | bytes 786440 | tf_op jit(solution)/shard_map/ppermute | solution.py:33
  103.9 11.8 %collective-permute-start.16 = (bf16[128,1024]{1,0:T(8,128)(2,1)S(1)}, bf16[128,1024]{1,0:T(8,128)(2,1)S(1)}, u32[]{:S(2)}, u32[]{:S(2)}) collective-permute-start(bf16[128,1024]{1,0:T(8,128)(2,1)S(1)} %get-tuple-element.43), channel_id=1, source_target_pairs={{0,112},{8,24},{16,0},{24,40},{32,16},{40,56},{48,32},{56,72},{64,... | collective-permute-start | bytes 786440 | tf_op jit(solution)/shard_map/ppermute | solution.py:33
  109.5 13.6 %collective-permute-start.13 = (bf16[128,1024]{1,0:T(8,128)(2,1)S(1)}, bf16[128,1024]{1,0:T(8,128)(2,1)S(1)}, u32[]{:S(2)}, u32[]{:S(2)}) collective-permute-start(bf16[128,1024]{1,0:T(8,128)(2,1)S(1)} %add_convert_fusion.14), channel_id=1, source_target_pairs={{0,16},{8,120},{16,32},{24,8},{32,48},{40,24},{48,64},{56,40},{64,... | collective-permute-start | bytes 786440 | tf_op jit(solution)/shard_map/ppermute | solution.py:33
  115.8 11.3 %collective-permute-start.17 = (bf16[128,1024]{1,0:T(8,128)(2,1)S(1)}, bf16[128,1024]{1,0:T(8,128)(2,1)S(1)}, u32[]{:S(2)}, u32[]{:S(2)}) collective-permute-start(bf16[128,1024]{1,0:T(8,128)(2,1)S(1)} %add_convert_fusion.11), channel_id=1, source_target_pairs={{0,112},{8,24},{16,0},{24,40},{32,16},{40,56},{48,32},{56,72},{64,... | collective-permute-start | bytes 786440 | tf_op jit(solution)/shard_map/ppermute | solution.py:33
  123.2 11.4 %collective-permute-start.14 = (bf16[128,1024]{1,0:T(8,128)(2,1)S(1)}, bf16[128,1024]{1,0:T(8,128)(2,1)S(1)}, u32[]{:S(2)}, u32[]{:S(2)}) collective-permute-start(bf16[128,1024]{1,0:T(8,128)(2,1)S(1)} %add_convert_fusion.13), channel_id=1, source_target_pairs={{0,16},{8,120},{16,32},{24,8},{32,48},{40,24},{48,64},{56,40},{64,... | collective-permute-start | bytes 786440 | tf_op jit(solution)/shard_map/ppermute | solution.py:33
  127.1 10.8 %collective-permute-start.18 = (bf16[128,1024]{1,0:T(8,128)(2,1)S(1)}, bf16[128,1024]{1,0:T(8,128)(2,1)S(1)}, u32[]{:S(2)}, u32[]{:S(2)}) collective-permute-start(bf16[128,1024]{1,0:T(8,128)(2,1)S(1)} %add_convert_fusion.10), channel_id=1, source_target_pairs={{0,112},{8,24},{16,0},{24,40},{32,16},{40,56},{48,32},{56,72},{64,... | collective-permute-start | bytes 786440 | tf_op jit(solution)/shard_map/ppermute | solution.py:33
  146.4 10.1 %collective-permute-start.20 = (bf16[128,1024]{1,0:T(8,128)(2,1)S(1)}, bf16[128,1024]{1,0:T(8,128)(2,1)S(1)}, u32[]{:S(2)}, u32[]{:S(2)}) collective-permute-start(bf16[128,1024]{1,0:T(8,128)(2,1)S(1)} %subtract_convert_fusion.refs_0_), channel_id=1, source_target_pairs={{0,112},{8,24},{16,0},{24,40},{32,16},{40,56},{48,32},{56,72},{64,... | collective-permute-start | bytes 786440 | tf_op jit(solution)/shard_map/ppermute | solution.py:33
  184.3 16.2 %all-to-all-start.1 = ((bf16[8,64,128]{2,1,0:T(8,128)(2,1)}), bf16[8,64,128]{2,1,0:T(8,128)(2,1)S(1)}, u32[]{:S(2)}, u32[]{:S(2)}) async-start(bf16[8,64,128]{2,1,0:T(8,128)(2,1)} %resend.1.after), calls=%async_computation.1 | async-start | bytes 262144 | tf_op jit(solution)/shard_map/all_to_all | solution.py:468
  198.5 15.9 %collective-permute-start.30 = (bf16[512,1024]{1,0:T(8,128)(2,1)S(1)}, bf16[512,1024]{1,0:T(8,128)(2,1)}, u32[]{:S(2)}, u32[]{:S(2)}) collective-permute-start(bf16[512,1024]{1,0:T(8,128)(2,1)S(1)} %fitted.2.after), channel_id=1, source_target_pairs={{0,8},{8,0},{16,24},{24,16},{32,40},{40,32},{48,56},{56,48},{64,72... | collective-permute-start | bytes 3145736 | tf_op jit(solution)/shard_map/ppermute | solution.py:33
  203.2 14.3 %collective-permute-start.26 = (bf16[4,136,1024]{2,1,0:T(8,128)(2,1)S(1)}, bf16[4,136,1024]{2,1,0:T(8,128)(2,1)S(1)}, u32[]{:S(2)}, u32[]{:S(2)}) collective-permute-start(bf16[4,136,1024]{2,1,0:T(8,128)(2,1)S(1)} %encgrad.3), channel_id=1, source_target_pairs={{0,8},{8,0},{16,24},{24,16},{32,40},{40,32},{48,56},{56,48},{64,72... | collective-permute-start | bytes 3342344 | tf_op jit(solution)/shard_map/ppermute | solution.py:33
  217.8 15.5 %collective-permute-start.28 = (bf16[136,1024]{1,0:T(8,128)(2,1)S(1)}, bf16[136,1024]{1,0:T(8,128)(2,1)S(1)}, u32[]{:S(2)}, u32[]{:S(2)}) collective-permute-start(bf16[136,1024]{1,0:T(8,128)(2,1)S(1)} %get-tuple-element.49), channel_id=1, source_target_pairs={{0,128},{8,392},{16,144},{24,408},{32,160},{40,424},{48,176},{56,4... | collective-permute-start | bytes 835592 | tf_op jit(solution)/shard_map/ppermute | solution.py:33
  222.3 14.1 %collective-permute-start.31 = (bf16[128,1024]{1,0:T(8,128)(2,1)S(1)}, bf16[128,1024]{1,0:T(8,128)(2,1)S(1)}, u32[]{:S(2)}, u32[]{:S(2)}) collective-permute-start(bf16[128,1024]{1,0:T(8,128)(2,1)S(1)} %get-tuple-element.50), channel_id=1, source_target_pairs={{0,384},{8,136},{16,400},{24,152},{32,416},{40,168},{48,432},{56,1... | collective-permute-start | bytes 786440 | tf_op jit(solution)/shard_map/ppermute | solution.py:33
  226.2 10.2 %collective-permute-start.33 = (bf16[128,1024]{1,0:T(8,128)(2,1)S(1)}, bf16[128,1024]{1,0:T(8,128)(2,1)S(1)}, u32[]{:S(2)}, u32[]{:S(2)}) collective-permute-start(bf16[128,1024]{1,0:T(8,128)(2,1)S(1)} %add_convert_fusion.5), channel_id=1, source_target_pairs={{0,128},{8,392},{16,144},{24,408},{32,160},{40,424},{48,176},{56,4... | collective-permute-start | bytes 786440 | tf_op jit(solution)/shard_map/ppermute | solution.py:33
  (56 other events, 402.7 us)

commit v3 on v2

--- a/solution.py
+++ b/solution.py
@@ -20,17 +20,27 @@
     return ((x % NX) * NZ + z % NZ) * NC + c % NC
 
 
-def _perm(dx=0, dz=0, dc=0):
-    return [
-        (_place(x, z, c), _place(x + (dx if c == 0 else -dx), z + (dz if c == 0 else -dz), c + dc))
-        for x in range(NX)
-        for z in range(NZ)
-        for c in range(NC)
-    ]
-
-
-def move(value, **shift):
-    return lax.ppermute(value, "atoms", _perm(**shift))
+def _side(place, core):
+    return 1 if (place + core) % 2 == 0 else -1
+
+
+def _swap(axis, partner):
+    pairs = []
+    for x in range(NX):
+        for z in range(NZ):
+            for c in range(NC):
+                if axis == "x":
+                    to = _place(x + partner * _side(x, c), z, c)
+                elif axis == "z":
+                    to = _place(x, z + partner * _side(z, c), c)
+                else:
+                    to = _place(x, z, c + 1)
+                pairs.append((_place(x, z, c), to))
+    return pairs
+
+
+def swap(value, axis, partner=1):
+    return lax.ppermute(value, "atoms", _swap(axis, partner))
 
 
 def call(body, outs, *args, scratch=(), specs=None, name):
@@ -104,8 +114,9 @@
     x, z, c = pos[0], pos[1], pos[2]
     owner = ext[:, 0:128].astype(I32)
     first, second = ext[:, 128:256].astype(I32), ext[:, 256:384].astype(I32)
-    dx = (((owner >> 4) - x) * (1 - 2 * (owner & 1)) + NX) & 3
-    b = jnp.where(dx == 0, 0, jnp.where(dx == 3, 1, jnp.where(dx == 1, 2, 3)))
+    side = (1 - 2 * (owner & 1)) * (1 - 2 * (x & 1))
+    dx = (((owner >> 4) - x) * side + NX) & 3
+    b = jnp.where(dx == 3, 2, jnp.where(dx == 2, 3, dx))
     b = b + jnp.where((owner & 1) == c, 0, 4)
     b = jnp.where(((owner >> 1) & 7) == z, b, -1)
     slot = rows_iota((8, 128))
@@ -134,29 +145,52 @@
                     out[16 * i + 8 * s + b : 16 * i + 8 * s + b + 1, :] = got
 
 
+def rows_of(pairs):
+    parts = [p[0 : 2 * R, :] for p in pairs]
+    return parts[0] if len(parts) == 1 else jnp.concatenate(parts, axis=0)
+
+
 def score_body(pos, own, other, *refs):
-    chunks, (picks, where) = refs[:-2], refs[-2:]
-    places = [locate(c[R : R + 8, 0:384].astype(F32), pos) for c in chunks]
+    pairs, (picks, where) = refs[:-2], refs[-2:]
+    places = []
+    for p in pairs:
+        for i in range(2):
+            ext = p[2 * R : 2 * R + 16, 0:384].astype(F32)
+            places.append(locate(ext[8 * i : 8 * i + 8, :], pos))
     for i, (at_a, at_b) in enumerate(places):
         where[16 * i : 16 * i + 8, :] = at_a
         where[16 * i + 8 : 16 * i + 16, :] = at_b
-    toks = [c[0:R, :] for c in chunks]
-    tok = toks[0] if len(toks) == 1 else jnp.concatenate(toks, axis=0)
-    pick_into(picks, (own, other), tok, places)
+    pick_into(picks, (own, other), rows_of(pairs), places)
 
 
 def back_body(first):
     def body(own, other, where, *refs):
-        chunks, picks = refs[:-1], refs[-1]
-        toks = [c[...] for c in chunks]
+        pairs, picks = refs[:-1], refs[-1]
         places = []
-        for i in range(len(chunks)):
+        for i in range(2 * len(pairs)):
             at = 16 * (first + i)
             places.append((where[at : at + 8, :], where[at + 8 : at + 16, :]))
-        tok = toks[0] if len(toks) == 1 else jnp.concatenate(toks, axis=0)
-        pick_into(picks, (own, other), tok, places)
+        pick_into(picks, (own, other), rows_of(pairs), places)
 
     return body
+
+
+def join_body(cuts):
+    def body(first, second, *refs):
+        out, at, to = refs[-1], 0, 0
+        for n in cuts:
+            out[to : to + n, :] = first[at : at + n, :]
+            out[to + n : to + 2 * n, :] = second[at : at + n, :]
+            at, to = at + n, to + 2 * n
+
+    return body
+
+
+def tables_body(near, far, after, enc, dec):
+    for i, ref in enumerate((near, far)):
+        enc[2 * R * i : 2 * R * (i + 1), :] = ref[0 : 2 * R, :]
+        dec[2 * R * i : 2 * R * (i + 1), :] = ref[2 * R : 4 * R, :]
+        dec[4 * R + 16 * i : 4 * R + 16 * i + 16, :] = ref[4 * R : 4 * R + 16, :]
 
 
 def halves_of(packed):
@@ -277,14 +311,12 @@
     high = rows.astype(BF)
     gram_rows[0:16, :] = high
     gram_rows[16:32, :] = (rows - high.astype(F32)).astype(BF)
-    out[...] = decode(turned, value_t, own, other, (7,)).astype(BF)
+    out[...] = decode(turned, value_t, own, other, (6, 7)).astype(BF)
 
 
 def decode_body(ms):
-    def body(at_t, act_t, own, other, *outs):
-        got = decode(at_t[...], act_t[...], own, other, ms)
-        for i, out in enumerate(outs):
-            out[...] = got[i * R : (i + 1) * R, :].astype(out.dtype)
+    def body(at_t, act_t, own, other, out):
+        out[...] = decode(at_t[...], act_t[...], own, other, ms).astype(out.dtype)
 
     return body
 
@@ -300,33 +332,20 @@
     return parts
 
 
-def load_rows(refs, rows, sem):
-    copies = [
-        pltpu.make_async_copy(ref.at[pl.ds(0, R)], rows.at[pl.ds(i * R, R)], sem.at[i]) for i, ref in enumerate(refs)
-    ]
-    for copy in copies:
-        copy.start()
-    return copies
-
-
 def fitted_body(half):
     def body(at, act, after, *refs):
-        chunks, (out, rows, sem) = refs[:8], refs[8:]
-        copies = load_rows(chunks, rows, sem)
+        pairs, out = refs[:4], refs[4]
         parts = [jnp.concatenate(turned_table(at, act, 4 * half + q), axis=1).astype(BF) for q in range(4)]
         table = jnp.concatenate(parts, axis=0)
-        for copy in copies:
-            copy.wait()
-        out[...] = (dot(table, rows[...], NN) * LOSS_GRAD).astype(BF)
+        out[...] = (dot(table, rows_of(pairs), NN) * LOSS_GRAD).astype(BF)
 
     return body
 
 
 def encgrad_body(half):
     def body(got, at, ranks, *refs):
-        chunks, rest = refs[:8], refs[8:]
-        out, (rows, sem) = rest[0], rest[-2:]
-        copies = load_rows(chunks, rows, sem)
+        pairs, rest = refs[:4], refs[4:]
+        out = rest[0]
         grad = jnp.where(at[...] >= 0, unsqueeze(total(got, 0, 32), ranks[...]) * LOSS_GRAD, 0.0)
         if half == 0:
             gram = rest[1]
@@ -339,15 +358,12 @@
             for piece in pieces[1:]:
                 acc = acc + piece
             sums = lax.dot_general(ones, acc, NT, precision=lax.Precision.HIGHEST, preferred_element_type=F32)
-            out[q, R : R + 8, 0:128] = sums.astype(BF)
-            out[q, R : R + 8, 128:1024] = jnp.zeros((8, 896), BF)
+            low = 4 * R + 8 * q
+            out[low : low + 8, 0:128] = sums.astype(BF)
+            out[low : low + 8, 128:1024] = jnp.zeros((8, 896), BF)
             parts.append(jnp.concatenate(pieces, axis=1).astype(BF))
         table = jnp.concatenate(parts, axis=0)
-        for copy in copies:
-            copy.wait()
-        part = dot(table, rows[...], NN).astype(BF)
-        for q in range(4):
-            out[q, 0:R, :] = part[q * R : (q + 1) * R, :]
+        out[0 : 4 * R, :] = dot(table, rows_of(pairs), NN).astype(BF)
 
     return body
 
@@ -374,17 +390,36 @@
     return (a.astype(F32) + b.astype(F32)).astype(BF)
 
 
-def gather_z(own):
-    f1, b1 = move(own, dz=1), move(own, dz=-1)
-    f2, b2 = move(f1, dz=1), move(b1, dz=-1)
-    f3, b3 = move(f2, dz=1), move(b2, dz=-1)
-    return [own, f1, b1, f2, b2, f3, b3, move(f3, dz=1)]
-
-
-def scatter_x(own, theirs):
-    blocks = [add(own[i], theirs[i]) for i in range(4)]
-    to_next = add(blocks[2], move(blocks[3], dx=1))
-    return blocks[0], move(blocks[1], dx=-1), move(to_next, dx=1)
+def join(first, second, cuts, *after, name):
+    n = first.shape[0]
+    return call(
+        join_body(cuts), sds((2 * n, 1024), BF), first, second, *after,
+        specs=whole(2) + [ANY_SPEC] * len(after), name=name,
+    )
+
+
+def gather_z(own, cuts, name):
+    near = swap(own, "z", 1)
+    pairs = [join(own, near, cuts, name=name)]
+    for partner in (-1, 1, -1):
+        pairs.append(swap(pairs[-1], "z", partner))
+    return pairs
+
+
+def scatter_x(own, theirs, ext):
+    a, b = 2 * R, 4 * R
+    if ext:
+        both = [add(own[i:j], theirs[i:j]) for i, j in ((0, a), (a, b), (b, b + 2 * ext), (b + 2 * ext, b + 4 * ext))]
+        far = swap(jnp.concatenate([both[1], both[3]], axis=0), "x", -1)
+        keep = jnp.concatenate([both[0][:R], both[2][:ext]], axis=0)
+        give = jnp.concatenate([both[0][R:], both[2][ext:]], axis=0)
+        far_keep = jnp.concatenate([far[:R], far[a : a + ext]], axis=0)
+        far_give = jnp.concatenate([far[R:a], far[a + ext :]], axis=0)
+    else:
+        keep, give = add(own[:R], theirs[:R]), add(own[R:a], theirs[R:a])
+        far = swap(add(own[a:], theirs[a:]), "x", -1)
+        far_keep, far_give = far[:R], far[R:]
+    return keep, far_keep, swap(add(give, far_give), "x", 1)
 
 
 def per_device(tokens, dec_bias, encoder, enc_bias, decoder, atom_ids, block_count):
@@ -398,99 +433,88 @@
         (sds((2 * R + 8, 1024), BF), sds((R, R), F32)),
         encoder, decoder, enc_bias.reshape(1, -1), sent, specs=whole(3) + [ANY_SPEC], name="pack",
     )
-    tok = gather_z(sent)
-
-    x1, x2 = move(packed, dx=1), move(packed, dx=-1)
-    x3 = move(x1, dx=1)
-    enc_own = jnp.concatenate([encoder, x1[:R], x2[:R], x3[:R]], axis=0)
-    dec_own = jnp.concatenate(
-        [decoder, x1[R : 2 * R], x2[R : 2 * R], x3[R : 2 * R], packed[2 * R :], x1[2 * R :], x2[2 * R :], x3[2 * R :]],
-        axis=0,
-    )
-    enc_other = move(enc_own, dc=1)
-    dec_other = move(dec_own, dc=1)
-
-    def score(chunks):
-        n = len(chunks)
+    tok = gather_z(sent, (R, 8), "join")
+    x_near = swap(packed, "x", 1)
+    x_pair = join(packed, x_near, (R, R, 8), tok[0], name="xjoin")
+    x_far = swap(x_pair, "x", -1)
+    enc_own, dec_own = call(
+        tables_body, (sds((4 * R, 1024), BF), sds((4 * R + 32, 1024), BF)), x_pair, x_far, tok[2],
+        specs=whole(2) + [ANY_SPEC], name="tables",
+    )
+    enc_other = swap(enc_own, "core")
+    dec_other = swap(dec_own, "core")
+
+    def score(pairs):
+        n = 2 * len(pairs)
         return call(
             score_body,
             (sds((16 * n, 128), F32), sds((16 * n, 128), I32)),
-            pos, enc_own, enc_other, *chunks,
-            specs=[SMEM_SPEC] + whole(2 + n), name="score",
+            pos, enc_own, enc_other, *pairs,
+            specs=[SMEM_SPEC] + whole(2 + len(pairs)), name="score",
         )
 
-    picks, wheres = zip(score(tok[0:7]), score(tok[7:8]))
+    picks, wheres = zip(score(tok[0:3]), score(tok[3:4]))
     out, where, ranks = call(
         send_body, (sds((NY, 64, 128), BF), sds((R, R), I32), sds((64, R), I32)),
         *picks, *wheres, gram_part, specs=whole(5), name="send",
     )
     got = lax.all_to_all(out, "width", split_axis=0, concat_axis=0, tiled=True)
 
-    act, at_t, act_t, gram_rows, d7 = call(
+    act, at_t, act_t, gram_rows, d67 = call(
         act_body,
-        (sds((R, R), F32), sds((R, R), I32), sds((R, R), F32), sds((32, 128), BF), sds((R, 1024), BF)),
+        (sds((R, R), F32), sds((R, R), I32), sds((R, R), F32), sds((32, 128), BF), sds((2 * R, 1024), BF)),
         got, dec_own, dec_other, where, ranks, specs=whole(5), name="act",
     )
 
     def decoded(ms, dtype=BF):
         return call(
-            decode_body(ms), tuple(sds((R, 1024), dtype) for _ in ms),
-            at_t, act_t, dec_own, dec_other, specs=whole(4), name="decode",
+            decode_body(ms), sds((2 * R, 1024), dtype), at_t, act_t, dec_own, dec_other, specs=whole(4), name="decode"
         )
 
-    d5, d6 = decoded((5, 6))
-    d3, d4 = decoded((3, 4))
-    d1, d2 = decoded((1, 2))
-    (d0,) = decoded((0,), F32)
-    f = move(d7, dz=1)
-    b = move(d5, dz=-1)
-    f = move(add(d6, f), dz=1)
-    b = move(add(d3, b), dz=-1)
-    f = move(add(d4, f), dz=1)
-    b = move(add(d1, b), dz=-1)
-    f = move(add(d2, f), dz=1)
-    summed = d0 + f.astype(F32) + b.astype(F32)
+    d45, d23, d01 = decoded((4, 5)), decoded((2, 3)), decoded((0, 1), F32)
+    part = swap(d67, "z", -1)
+    part = swap(add(d45, part), "z", 1)
+    far = swap(add(d23, part), "z", -1)
+    near = swap(add(d01[R:], far[R:]), "z", 1)
+    summed = d01[:R] + far[:R].astype(F32) + near.astype(F32)
     residual = (summed + bias_row - tokens.astype(F32)).astype(BF)
 
-    res = gather_z(residual)
-
-    def back(chunks, first):
-        n = len(chunks)
+    res = gather_z(residual, (R,), "rjoin")
+
+    def back(pairs, first):
+        n = 2 * len(pairs)
         return call(
             back_body(first), sds((16 * n, 128), F32),
-            dec_own, dec_other, where, *chunks, specs=whole(3 + n), name="back",
+            dec_own, dec_other, where, *pairs, specs=whole(3 + len(pairs)), name="back",
         )
 
-    backs = (back(res[0:7], 0), back(res[7:8], 7))
+    backs = (back(res[0:3], 0), back(res[3:4], 6))
     out2 = call(
         resend_body, sds((NY, 64, 128), BF), *backs, where, ranks, gram_rows, specs=whole(5), name="resend"
     )
     got2 = lax.all_to_all(out2, "width", split_axis=0, concat_axis=0, tiled=True)
-
-    scratch = [pltpu.VMEM((8 * R, 1024), BF), pltpu.SemaphoreType.DMA((8,))]
 
     def fitted(half, after):
         return call(
             fitted_body(half), sds((4 * R, 1024), BF), where, act, after, *res,
-            specs=whole(2) + [ANY_SPEC] * 9, scratch=scratch, name="fitted",
+            specs=whole(2) + [ANY_SPEC] + whole(4), name="fitted",
         )
 
     fit_other = fitted(1, out2)
-    fit_theirs = move(fit_other, dc=1)
+    fit_theirs = swap(fit_other, "core")
     fit_own = fitted(0, fit_other)
-    fit = scatter_x(fit_own.reshape(4, R, 1024), fit_theirs.reshape(4, R, 1024))
+    fit = scatter_x(fit_own, fit_theirs, 0)
 
     def encgrad(half):
-        outs = [sds((4, R + 8, 1024), BF)] + ([sds((R, R), F32)] if half == 0 else [])
+        outs = [sds((4 * R + 32, 1024), BF)] + ([sds((R, R), F32)] if half == 0 else [])
         return call(
-            encgrad_body(half), tuple(outs), got2, where, ranks, *tok,
-            specs=whole(3) + [ANY_SPEC] * 8, scratch=scratch, name="encgrad",
+            encgrad_body(half), tuple(outs), got2, where, ranks, *tok, specs=whole(7), name="encgrad"
         )
 
     (eg_other,) = encgrad(1)
-    eg_theirs = move(eg_other, dc=1)
+    eg_theirs = swap(eg_other, "core")
     eg_own, gram = encgrad(0)
-    eg = scatter_x(eg_own, eg_theirs)
+    eg = scatter_x(eg_own, eg_theirs, 8)
     eg_sum = eg[0].astype(F32) + eg[1].astype(F32) + eg[2].astype(F32)
     encoder_grad = eg_sum[:R].astype(BF)
     bias_grad = eg_sum[R, 0:R]

time: 246 us -> 253 us (1.028)
  the two profiles are of different devices: /device:TPU:8 before, /device:TPU:6 now
where the time goes in v3:
time: 253 us; the launch traced here: 250 us
  waiting for transfers between devices  108 us (43%)
  starting transfers between devices  87.8 us (35%)
  Pallas kernels  32.6 us (13%)
  local copies, waits for them, and re-layouts  14.6 us (6%)
  other arithmetic  5.47 us (2%)
    ppermute x22, waiting for transfers between devices, swap(): return lax.ppermute(value, 'atoms', _swap(axis, partner))  98.5 us
    ppermute x22, starting transfers between devices, swap(): return lax.ppermute(value, 'atoms', _swap(axis, partner))  77.3 us
    pallas_call x21, Pallas kernels, call(): pl.pallas_call(body, out_shape=outs, in_specs=specs, scratch_shapes=scrat...  32.6 us
    unnamed x61, local copies, waits for them, and re-layouts  13.3 us
    all_to_all x1, waiting for transfers between devices, per_device(): got = lax.all_to_all(out, 'width', split_axis=0, concat_axis=0, tiled=True)  9.18 us
    all_to_all x1, starting transfers between devices, per_device(): got = lax.all_to_all(out, 'width', split_axis=0, concat_axis=0, tiled=True)  7.1 us
  transfers between devices with their start and end apart: 24, of which 16 were waited for; matrix products, arithmetic and copies ran while one was open for 2% of the time, Pallas kernels for 10%

profile of v3, /device:TPU:6, one launch (start us, length us, event | category | flops | bytes accessed | tf_op | source)
XLA Modules:
  0.0 250.1 jit_solution(7661660414195746939)
XLA Ops:
  8.8 4.3 %collective-permute-start.1 = (bf16[136,1024]{1,0:T(8,128)(2,1)S(1)}, bf16[136,1024]{1,0:T(8,128)(2,1)S(1)}, u32[]{:S(2)}, u32[]{:S(2)}) collective-permute-start(bf16[136,1024]{1,0:T(8,128)(2,1)S(1)} %center.1.after.first), channel_id=1, source_target_pairs={{0,16},{8,120},{16,0},{24,40},{32,48},{40,24},{48,32},{56,72},{64,... | collective-permute-start | bytes 835592 | tf_op jit(solution)/shard_map/ppermute | solution.py:43
  13.1 4.5 %collective-permute-done.1.second = bf16[136,1024]{1,0:T(8,128)(2,1)S(1)} collective-permute-done((bf16[136,1024]{1,0:T(8,128)(2,1)S(1)}, bf16[136,1024]{1,0:T(8,128)(2,1)S(1)}, u32[]{:S(2)}, u32[]{:S(2)}) %collective-permute-start.1) | collective-permute-done | bytes 278560 | tf_op jit(solution)/shard_map/ppermute | solution.py:43
  17.7 10.6 %collective-permute-start.3 = (bf16[272,1024]{1,0:T(8,128)(2,1)S(1)}, bf16[272,1024]{1,0:T(8,128)(2,1)S(1)}, u32[]{:S(2)}, u32[]{:S(2)}) collective-permute-start(bf16[272,1024]{1,0:T(8,128)(2,1)S(1)} %join.1.refs_0_), channel_id=1, source_target_pairs={{0,112},{8,24},{16,32},{24,8},{32,16},{40,56},{48,64},{56,40},{64,... | collective-permute-start | bytes 1671176 | tf_op jit(solution)/shard_map/ppermute | solution.py:43
  31.4 4.3 %collective-permute-done.3.refs_1_ = bf16[272,1024]{1,0:T(8,128)(2,1)S(1)} collective-permute-done((bf16[272,1024]{1,0:T(8,128)(2,1)S(1)}, bf16[272,1024]{1,0:T(8,128)(2,1)S(1)}, u32[]{:S(2)}, u32[]{:S(2)}) %collective-permute-start.3) | collective-permute-done | bytes 557088 | tf_op jit(solution)/shard_map/ppermute | solution.py:43
  38.5 8.7 %collective-permute-done.4.after.refs_2_ = bf16[272,1024]{1,0:T(8,128)(2,1)S(1)} collective-permute-done((bf16[272,1024]{1,0:T(8,128)(2,1)S(1)}, bf16[272,1024]{1,0:T(8,128)(2,1)S(1)}, u32[]{:S(2)}, u32[]{:S(2)}) %collective-permute-start.4) | collective-permute-done | bytes 557088 | tf_op jit(solution)/shard_map/ppermute | solution.py:43
  52.7 5.1 %collective-permute-start.6 = (bf16[272,1024]{1,0:T(8,128)(2,1)S(1)}, bf16[272,1024]{1,0:T(8,128)(2,1)}, u32[]{:S(2)}, u32[]{:S(2)}) collective-permute-start(bf16[272,1024]{1,0:T(8,128)(2,1)S(1)} %collective-permute-done.4.after.refs_2_), channel_id=1, source_target_pairs={{0,112},{8,24},{16,32},{24,8},{32,16},{40,56},{48,64},{56,40},{64,... | collective-permute-start | bytes 1671176 | tf_op jit(solution)/shard_map/ppermute | solution.py:43
  59.0 3.9 %score.2 = (f32[96,128]{1,0:T(8,128)S(1)}, s32[96,128]{1,0:T(8,128)S(1)}) custom-call(s32[3]{0:T(128)S(1)} %pad_add_fusion.pos, bf16[512,1024]{1,0:T(8,128)(2,1)} %get-tuple-element.23.own, bf16[512,1024]{1,0:T(8,128)(2,1)} %collective-permute-done.5.other, bf16[272,1024]{1,0:T(8,128)(2,1)S(1)} %join.1.refs_0_, bf16[272,1024]{1,0:T(8,128)(2,1)S(1)} %copy-done.4, ...), custom_call_target="tpu_custom_call" | custom-call | tf_op jit(solution)/shard_map/score/pallas_call | solution.py:47
  69.5 7.1 %all-to-all-start = ((bf16[8,64,128]{2,1,0:T(8,128)(2,1)}), bf16[8,64,128]{2,1,0:T(8,128)(2,1)}, u32[]{:S(2)}, u32[]{:S(2)}) async-start(bf16[8,64,128]{2,1,0:T(8,128)(2,1)} %copy-done.26), calls=%async_computation | async-start | bytes 262144 | tf_op jit(solution)/shard_map/all_to_all | solution.py:461
  76.6 9.2 %all-to-all-done.got = bf16[8,64,128]{2,1,0:T(8,128)(2,1)} async-done(((bf16[8,64,128]{2,1,0:T(8,128)(2,1)}), bf16[8,64,128]{2,1,0:T(8,128)(2,1)}, u32[]{:S(2)}, u32[]{:S(2)}) %all-to-all-start) | async-done | bytes 131104 | tf_op jit(solution)/shard_map/all_to_all | solution.py:461
  88.5 5.1 %collective-permute-start.8 = (bf16[256,1024]{1,0:T(8,128)(2,1)S(1)}, bf16[256,1024]{1,0:T(8,128)(2,1)S(1)}, u32[]{:S(2)}, u32[]{:S(2)}) collective-permute-start(bf16[256,1024]{1,0:T(8,128)(2,1)S(1)} %get-tuple-element.35), channel_id=1, source_target_pairs={{0,112},{8,24},{16,32},{24,8},{32,16},{40,56},{48,64},{56,40},{64,... | collective-permute-start | bytes 1572872 | tf_op jit(solution)/shard_map/ppermute | solution.py:43
  95.6 5.2 %collective-permute-done.8 = bf16[256,1024]{1,0:T(8,128)(2,1)S(1)} collective-permute-done((bf16[256,1024]{1,0:T(8,128)(2,1)S(1)}, bf16[256,1024]{1,0:T(8,128)(2,1)S(1)}, u32[]{:S(2)}, u32[]{:S(2)}) %collective-permute-start.8) | collective-permute-done | bytes 524320 | tf_op jit(solution)/shard_map/ppermute | solution.py:43
  104.9 8.0 %collective-permute-done.9 = bf16[256,1024]{1,0:T(8,128)(2,1)S(1)} collective-permute-done((bf16[256,1024]{1,0:T(8,128)(2,1)S(1)}, bf16[256,1024]{1,0:T(8,128)(2,1)S(1)}, u32[]{:S(2)}, u32[]{:S(2)}) %collective-permute-start.9) | collective-permute-done | bytes 524320 | tf_op jit(solution)/shard_map/ppermute | solution.py:43
  113.1 5.6 %collective-permute-start.10 = (bf16[256,1024]{1,0:T(8,128)(2,1)S(1)}, bf16[256,1024]{1,0:T(8,128)(2,1)S(1)}, u32[]{:S(2)}, u32[]{:S(2)}) collective-permute-start(bf16[256,1024]{1,0:T(8,128)(2,1)S(1)} %add_convert_fusion.3), channel_id=1, source_target_pairs={{0,112},{8,24},{16,32},{24,8},{32,16},{40,56},{48,64},{56,40},{64,... | collective-permute-start | bytes 1572872 | tf_op jit(solution)/shard_map/ppermute | solution.py:43
  120.7 7.1 %collective-permute-done.10 = bf16[256,1024]{1,0:T(8,128)(2,1)S(1)} collective-permute-done((bf16[256,1024]{1,0:T(8,128)(2,1)S(1)}, bf16[256,1024]{1,0:T(8,128)(2,1)S(1)}, u32[]{:S(2)}, u32[]{:S(2)}) %collective-permute-start.10) | collective-permute-done | bytes 524320 | tf_op jit(solution)/shard_map/ppermute | solution.py:43
  129.8 6.3 %collective-permute-done.11 = bf16[128,1024]{1,0:T(8,128)(2,1)S(1)} collective-permute-done((bf16[128,1024]{1,0:T(8,128)(2,1)S(1)}, bf16[128,1024]{1,0:T(8,128)(2,1)S(1)}, u32[]{:S(2)}, u32[]{:S(2)}) %collective-permute-start.11) | collective-permute-done | bytes 262176 | tf_op jit(solution)/shard_map/ppermute | solution.py:43
  138.2 8.6 %collective-permute-done.12.second = bf16[128,1024]{1,0:T(8,128)(2,1)S(1)} collective-permute-done((bf16[128,1024]{1,0:T(8,128)(2,1)S(1)}, bf16[128,1024]{1,0:T(8,128)(2,1)S(1)}, u32[]{:S(2)}, u32[]{:S(2)}) %collective-permute-start.12) | collective-permute-done | bytes 262176 | tf_op jit(solution)/shard_map/ppermute | solution.py:43
  147.5 6.0 %collective-permute-start.13 = (bf16[256,1024]{1,0:T(8,128)(2,1)S(1)}, bf16[256,1024]{1,0:T(8,128)(2,1)S(1)}, u32[]{:S(2)}, u32[]{:S(2)}) collective-permute-start(bf16[256,1024]{1,0:T(8,128)(2,1)S(1)} %rjoin.1.refs_0_), channel_id=1, source_target_pairs={{0,112},{8,24},{16,32},{24,8},{32,16},{40,56},{48,64},{56,40},{64,... | collective-permute-start | bytes 1572872 | tf_op jit(solution)/shard_map/ppermute | solution.py:43
  153.5 11.6 %collective-permute-done.13.refs_1_ = bf16[256,1024]{1,0:T(8,128)(2,1)S(1)} collective-permute-done((bf16[256,1024]{1,0:T(8,128)(2,1)S(1)}, bf16[256,1024]{1,0:T(8,128)(2,1)S(1)}, u32[]{:S(2)}, u32[]{:S(2)}) %collective-permute-start.13) | collective-permute-done | bytes 524320 | tf_op jit(solution)/shard_map/ppermute | solution.py:43
  167.0 14.7 %collective-permute-done.14.refs_2_ = bf16[256,1024]{1,0:T(8,128)(2,1)S(1)} collective-permute-done((bf16[256,1024]{1,0:T(8,128)(2,1)S(1)}, bf16[256,1024]{1,0:T(8,128)(2,1)S(1)}, u32[]{:S(2)}, u32[]{:S(2)}) %collective-permute-start.14) | collective-permute-done | bytes 524320 | tf_op jit(solution)/shard_map/ppermute | solution.py:43
  181.7 5.2 %collective-permute-start.15 = (bf16[256,1024]{1,0:T(8,128)(2,1)S(1)}, bf16[256,1024]{1,0:T(8,128)(2,1)S(1)}, u32[]{:S(2)}, u32[]{:S(2)}) collective-permute-start(bf16[256,1024]{1,0:T(8,128)(2,1)S(1)} %collective-permute-done.14.refs_2_), channel_id=1, source_target_pairs={{0,112},{8,24},{16,32},{24,8},{32,16},{40,56},{48,64},{56,40},{64,... | collective-permute-start | bytes 1572872 | tf_op jit(solution)/shard_map/ppermute | solution.py:43
  189.3 4.7 %collective-permute-done.15.refs_0_.refs_3_ = bf16[256,1024]{1,0:T(8,128)(2,1)S(1)} collective-permute-done((bf16[256,1024]{1,0:T(8,128)(2,1)S(1)}, bf16[256,1024]{1,0:T(8,128)(2,1)S(1)}, u32[]{:S(2)}, u32[]{:S(2)}) %collective-permute-start.15) | collective-permute-done | bytes 524320 | tf_op jit(solution)/shard_map/ppermute | solution.py:43
  224.3 4.1 %collective-permute-start.17 = (bf16[272,1024]{1,0:T(8,128)(2,1)S(1)}, bf16[272,1024]{1,0:T(8,128)(2,1)S(1)}, u32[]{:S(2)}, u32[]{:S(2)}) collective-permute-start(bf16[272,1024]{1,0:T(8,128)(2,1)S(1)} %pad_maximum_fusion), channel_id=1, source_target_pairs={{0,384},{8,136},{16,400},{24,152},{32,416},{40,168},{48,432},{56,1... | collective-permute-start | bytes 1671176 | tf_op jit(solution)/shard_map/ppermute | solution.py:43
  228.4 4.7 %collective-permute-done.20 = bf16[256,1024]{1,0:T(8,128)(2,1)S(1)} collective-permute-done((bf16[256,1024]{1,0:T(8,128)(2,1)S(1)}, bf16[256,1024]{1,0:T(8,128)(2,1)S(1)}, u32[]{:S(2)}, u32[]{:S(2)}) %collective-permute-start.20) | collective-permute-done | bytes 524320 | tf_op jit(solution)/shard_map/ppermute | solution.py:43
  236.2 3.9 %collective-permute-done.17 = bf16[272,1024]{1,0:T(8,128)(2,1)S(1)} collective-permute-done((bf16[272,1024]{1,0:T(8,128)(2,1)S(1)}, bf16[272,1024]{1,0:T(8,128)(2,1)S(1)}, u32[]{:S(2)}, u32[]{:S(2)}) %collective-permute-start.17) | collective-permute-done | bytes 557088 | tf_op jit(solution)/shard_map/ppermute | solution.py:43
  (125 shorter events, 89.6 us)
Async XLA Ops:
  6.1 22.2 %collective-permute-start = (bf16[264,1024]{1,0:T(8,128)(2,1)S(1)}, bf16[264,1024]{1,0:T(8,128)(2,1)S(1)}, u32[]{:S(2)}, u32[]{:S(2)}) collective-permute-start(bf16[264,1024]{1,0:T(8,128)(2,1)S(1)} %get-tuple-element.22.first), channel_id=1, source_target_pairs={{0,128},{8,392},{16,144},{24,408},{32,160},{40,424},{48,176},{56,4... | collective-permute-start | bytes 1622024 | tf_op jit(solution)/shard_map/ppermute | solution.py:43
  8.8 8.8 %collective-permute-start.1 = (bf16[136,1024]{1,0:T(8,128)(2,1)S(1)}, bf16[136,1024]{1,0:T(8,128)(2,1)S(1)}, u32[]{:S(2)}, u32[]{:S(2)}) collective-permute-start(bf16[136,1024]{1,0:T(8,128)(2,1)S(1)} %center.1.after.first), channel_id=1, source_target_pairs={{0,16},{8,120},{16,0},{24,40},{32,48},{40,24},{48,32},{56,72},{64,... | collective-permute-start | bytes 835592 | tf_op jit(solution)/shard_map/ppermute | solution.py:43
  17.7 18.1 %collective-permute-start.3 = (bf16[272,1024]{1,0:T(8,128)(2,1)S(1)}, bf16[272,1024]{1,0:T(8,128)(2,1)S(1)}, u32[]{:S(2)}, u32[]{:S(2)}) collective-permute-start(bf16[272,1024]{1,0:T(8,128)(2,1)S(1)} %join.1.refs_0_), channel_id=1, source_target_pairs={{0,112},{8,24},{16,32},{24,8},{32,16},{40,56},{48,64},{56,40},{64,... | collective-permute-start | bytes 1671176 | tf_op jit(solution)/shard_map/ppermute | solution.py:43
  28.4 18.8 %collective-permute-start.2 = (bf16[528,1024]{1,0:T(8,128)(2,1)S(1)}, bf16[528,1024]{1,0:T(8,128)(2,1)S(1)}, u32[]{:S(2)}, u32[]{:S(2)}) collective-permute-start(bf16[528,1024]{1,0:T(8,128)(2,1)S(1)} %xjoin.1.near), channel_id=1, source_target_pairs={{0,384},{8,136},{16,400},{24,152},{32,416},{40,168},{48,432},{56,1... | collective-permute-start | bytes 3244040 | tf_op jit(solution)/shard_map/ppermute | solution.py:43
  35.8 11.4 %collective-permute-start.4 = (bf16[272,1024]{1,0:T(8,128)(2,1)S(1)}, bf16[272,1024]{1,0:T(8,128)(2,1)S(1)}, u32[]{:S(2)}, u32[]{:S(2)}) collective-permute-start(bf16[272,1024]{1,0:T(8,128)(2,1)S(1)} %collective-permute-done.3.refs_1_), channel_id=1, source_target_pairs={{0,16},{8,120},{16,0},{24,40},{32,48},{40,24},{48,32},{56,72},{64,... | collective-permute-start | bytes 1671176 | tf_op jit(solution)/shard_map/ppermute | solution.py:43
  48.3 9.6 %collective-permute-start.5 = (bf16[512,1024]{1,0:T(8,128)(2,1)}, bf16[512,1024]{1,0:T(8,128)(2,1)}, u32[]{:S(2)}, u32[]{:S(2)}) collective-permute-start(bf16[512,1024]{1,0:T(8,128)(2,1)} %get-tuple-element.23.own), channel_id=1, source_target_pairs={{0,8},{8,0},{16,24},{24,16},{32,40},{40,32},{48,56},{56,48},{64,72... | collective-permute-start | bytes 3145736 | tf_op jit(solution)/shard_map/ppermute | solution.py:43
  50.3 26.3 %collective-permute-start.7 = (bf16[544,1024]{1,0:T(8,128)(2,1)S(1)}, bf16[544,1024]{1,0:T(8,128)(2,1)S(1)}, u32[]{:S(2)}, u32[]{:S(2)}) collective-permute-start(bf16[544,1024]{1,0:T(8,128)(2,1)S(1)} %get-tuple-element.30.own), channel_id=1, source_target_pairs={{0,8},{8,0},{16,24},{24,16},{32,40},{40,32},{48,56},{56,48},{64,72... | collective-permute-start | bytes 3342344 | tf_op jit(solution)/shard_map/ppermute | solution.py:43
  52.7 12.7 %collective-permute-start.6 = (bf16[272,1024]{1,0:T(8,128)(2,1)S(1)}, bf16[272,1024]{1,0:T(8,128)(2,1)}, u32[]{:S(2)}, u32[]{:S(2)}) collective-permute-start(bf16[272,1024]{1,0:T(8,128)(2,1)S(1)} %collective-permute-done.4.after.refs_2_), channel_id=1, source_target_pairs={{0,112},{8,24},{16,32},{24,8},{32,16},{40,56},{48,64},{56,40},{64,... | collective-permute-start | bytes 1671176 | tf_op jit(solution)/shard_map/ppermute | solution.py:43
  69.5 16.3 %all-to-all-start = ((bf16[8,64,128]{2,1,0:T(8,128)(2,1)}), bf16[8,64,128]{2,1,0:T(8,128)(2,1)}, u32[]{:S(2)}, u32[]{:S(2)}) async-start(bf16[8,64,128]{2,1,0:T(8,128)(2,1)} %copy-done.26), calls=%async_computation | async-start | bytes 262144 | tf_op jit(solution)/shard_map/all_to_all | solution.py:461
  88.5 12.3 %collective-permute-start.8 = (bf16[256,1024]{1,0:T(8,128)(2,1)S(1)}, bf16[256,1024]{1,0:T(8,128)(2,1)S(1)}, u32[]{:S(2)}, u32[]{:S(2)}) collective-permute-start(bf16[256,1024]{1,0:T(8,128)(2,1)S(1)} %get-tuple-element.35), channel_id=1, source_target_pairs={{0,112},{8,24},{16,32},{24,8},{32,16},{40,56},{48,64},{56,40},{64,... | collective-permute-start | bytes 1572872 | tf_op jit(solution)/shard_map/ppermute | solution.py:43
  101.0 11.9 %collective-permute-start.9 = (bf16[256,1024]{1,0:T(8,128)(2,1)S(1)}, bf16[256,1024]{1,0:T(8,128)(2,1)S(1)}, u32[]{:S(2)}, u32[]{:S(2)}) collective-permute-start(bf16[256,1024]{1,0:T(8,128)(2,1)S(1)} %add_convert_fusion.4), channel_id=1, source_target_pairs={{0,16},{8,120},{16,0},{24,40},{32,48},{40,24},{48,32},{56,72},{64,... | collective-permute-start | bytes 1572872 | tf_op jit(solution)/shard_map/ppermute | solution.py:43
  113.1 14.7 %collective-permute-start.10 = (bf16[256,1024]{1,0:T(8,128)(2,1)S(1)}, bf16[256,1024]{1,0:T(8,128)(2,1)S(1)}, u32[]{:S(2)}, u32[]{:S(2)}) collective-permute-start(bf16[256,1024]{1,0:T(8,128)(2,1)S(1)} %add_convert_fusion.3), channel_id=1, source_target_pairs={{0,112},{8,24},{16,32},{24,8},{32,16},{40,56},{48,64},{56,40},{64,... | collective-permute-start | bytes 1572872 | tf_op jit(solution)/shard_map/ppermute | solution.py:43
  127.8 8.3 %collective-permute-start.11 = (bf16[128,1024]{1,0:T(8,128)(2,1)S(1)}, bf16[128,1024]{1,0:T(8,128)(2,1)S(1)}, u32[]{:S(2)}, u32[]{:S(2)}) collective-permute-start(bf16[128,1024]{1,0:T(8,128)(2,1)S(1)} %fusion), channel_id=1, source_target_pairs={{0,16},{8,120},{16,0},{24,40},{32,48},{40,24},{48,32},{56,72},{64,... | collective-permute-start | bytes 786440 | tf_op jit(solution)/shard_map/ppermute | solution.py:43
  136.3 10.5 %collective-permute-start.12 = (bf16[128,1024]{1,0:T(8,128)(2,1)S(1)}, bf16[128,1024]{1,0:T(8,128)(2,1)S(1)}, u32[]{:S(2)}, u32[]{:S(2)}) collective-permute-start(bf16[128,1024]{1,0:T(8,128)(2,1)S(1)} %fusion.4.first), channel_id=1, source_target_pairs={{0,16},{8,120},{16,0},{24,40},{32,48},{40,24},{48,32},{56,72},{64,... | collective-permute-start | bytes 786440 | tf_op jit(solution)/shard_map/ppermute | solution.py:43
  147.5 17.5 %collective-permute-start.13 = (bf16[256,1024]{1,0:T(8,128)(2,1)S(1)}, bf16[256,1024]{1,0:T(8,128)(2,1)S(1)}, u32[]{:S(2)}, u32[]{:S(2)}) collective-permute-start(bf16[256,1024]{1,0:T(8,128)(2,1)S(1)} %rjoin.1.refs_0_), channel_id=1, source_target_pairs={{0,112},{8,24},{16,32},{24,8},{32,16},{40,56},{48,64},{56,40},{64,... | collective-permute-start | bytes 1572872 | tf_op jit(solution)/shard_map/ppermute | solution.py:43
  165.0 16.6 %collective-permute-start.14 = (bf16[256,1024]{1,0:T(8,128)(2,1)S(1)}, bf16[256,1024]{1,0:T(8,128)(2,1)S(1)}, u32[]{:S(2)}, u32[]{:S(2)}) collective-permute-start(bf16[256,1024]{1,0:T(8,128)(2,1)S(1)} %collective-permute-done.13.refs_1_), channel_id=1, source_target_pairs={{0,16},{8,120},{16,0},{24,40},{32,48},{40,24},{48,32},{56,72},{64,... | collective-permute-start | bytes 1572872 | tf_op jit(solution)/shard_map/ppermute | solution.py:43
  181.7 12.4 %collective-permute-start.15 = (bf16[256,1024]{1,0:T(8,128)(2,1)S(1)}, bf16[256,1024]{1,0:T(8,128)(2,1)S(1)}, u32[]{:S(2)}, u32[]{:S(2)}) collective-permute-start(bf16[256,1024]{1,0:T(8,128)(2,1)S(1)} %collective-permute-done.14.refs_2_), channel_id=1, source_target_pairs={{0,112},{8,24},{16,32},{24,8},{32,16},{40,56},{48,64},{56,40},{64,... | collective-permute-start | bytes 1572872 | tf_op jit(solution)/shard_map/ppermute | solution.py:43
  196.3 12.8 %all-to-all-start.1 = ((bf16[8,64,128]{2,1,0:T(8,128)(2,1)}), bf16[8,64,128]{2,1,0:T(8,128)(2,1)S(1)}, u32[]{:S(2)}, u32[]{:S(2)}) async-start(bf16[8,64,128]{2,1,0:T(8,128)(2,1)} %resend.1.after), calls=%async_computation.1 | async-start | bytes 262144 | tf_op jit(solution)/shard_map/all_to_all | solution.py:495
  207.0 12.6 %collective-permute-start.19 = (bf16[512,1024]{1,0:T(8,128)(2,1)}, bf16[512,1024]{1,0:T(8,128)(2,1)}, u32[]{:S(2)}, u32[]{:S(2)}) collective-permute-start(bf16[512,1024]{1,0:T(8,128)(2,1)} %fitted.2.after), channel_id=1, source_target_pairs={{0,8},{8,0},{16,24},{24,16},{32,40},{40,32},{48,56},{56,48},{64,72... | collective-permute-start | bytes 3145736 | tf_op jit(solution)/shard_map/ppermute | solution.py:43
  212.4 11.4 %collective-permute-start.16 = (bf16[544,1024]{1,0:T(8,128)(2,1)S(1)}, bf16[544,1024]{1,0:T(8,128)(2,1)S(1)}, u32[]{:S(2)}, u32[]{:S(2)}) collective-permute-start(bf16[544,1024]{1,0:T(8,128)(2,1)S(1)} %encgrad.3), channel_id=1, source_target_pairs={{0,8},{8,0},{16,24},{24,16},{32,40},{40,32},{48,56},{56,48},{64,72... | collective-permute-start | bytes 3342344 | tf_op jit(solution)/shard_map/ppermute | solution.py:43
  220.8 12.3 %collective-permute-start.20 = (bf16[256,1024]{1,0:T(8,128)(2,1)S(1)}, bf16[256,1024]{1,0:T(8,128)(2,1)S(1)}, u32[]{:S(2)}, u32[]{:S(2)}) collective-permute-start(bf16[256,1024]{1,0:T(8,128)(2,1)S(1)} %add_convert_fusion), channel_id=1, source_target_pairs={{0,384},{8,136},{16,400},{24,152},{32,416},{40,168},{48,432},{56,1... | collective-permute-start | bytes 1572872 | tf_op jit(solution)/shard_map/ppermute | solution.py:43
  224.3 15.9 %collective-permute-start.17 = (bf16[272,1024]{1,0:T(8,128)(2,1)S(1)}, bf16[272,1024]{1,0:T(8,128)(2,1)S(1)}, u32[]{:S(2)}, u32[]{:S(2)}) collective-permute-start(bf16[272,1024]{1,0:T(8,128)(2,1)S(1)} %pad_maximum_fusion), channel_id=1, source_target_pairs={{0,384},{8,136},{16,400},{24,152},{32,416},{40,168},{48,432},{56,1... | collective-permute-start | bytes 1671176 | tf_op jit(solution)/shard_map/ppermute | solution.py:43
  234.2 9.1 %collective-permute-start.21 = (bf16[128,1024]{1,0:T(8,128)(2,1)S(1)}, bf16[128,1024]{1,0:T(8,128)(2,1)S(1)}, u32[]{:S(2)}, u32[]{:S(2)}) collective-permute-start(bf16[128,1024]{1,0:T(8,128)(2,1)S(1)} %add_convert_fusion.7), channel_id=1, source_target_pairs={{0,128},{8,392},{16,144},{24,408},{32,160},{40,424},{48,176},{56,4... | collective-permute-start | bytes 786440 | tf_op jit(solution)/shard_map/ppermute | solution.py:43
  240.3 8.4 %collective-permute-start.18 = (bf16[136,1024]{1,0:T(8,128)(2,1)S(1)}, bf16[136,1024]{1,0:T(8,128)(2,1)S(1)}, u32[]{:S(2)}, u32[]{:S(2)}) collective-permute-start(bf16[136,1024]{1,0:T(8,128)(2,1)S(1)} %add_convert_fusion.5), channel_id=1, source_target_pairs={{0,128},{8,392},{16,144},{24,408},{32,160},{40,424},{48,176},{56,4... | collective-permute-start | bytes 835592 | tf_op jit(solution)/shard_map/ppermute | solution.py:43
  (30 other events, 313.8 us)

commit v4 on v2

--- a/solution.py
+++ b/solution.py
@@ -4,6 +4,7 @@
 from jax.experimental import pallas as pl
 from jax.experimental.pallas import tpu as pltpu
 from jax.sharding import PartitionSpec as P
+
 
 NX, NZ, NC, NY = 4, 8, 2, 8
 BLOCK = 64
@@ -33,14 +34,13 @@
     return lax.ppermute(value, "atoms", _perm(**shift))
 
 
-def call(body, outs, *args, scratch=(), specs=None, name):
+def call(body, outs, *args, scratch=(), specs=None):
     return pl.pallas_call(
         body,
         out_shape=outs,
         in_specs=specs,
         scratch_shapes=scratch,
         compiler_params=pltpu.CompilerParams(vmem_limit_bytes=VMEM),
-        name=name,
     )(*args)
 
 
@@ -134,26 +134,33 @@
                     out[16 * i + 8 * s + b : 16 * i + 8 * s + b + 1, :] = got
 
 
-def score_body(pos, own, other, *refs):
-    chunks, (picks, where) = refs[:-2], refs[-2:]
-    places = [locate(c[R : R + 8, 0:384].astype(F32), pos) for c in chunks]
-    for i, (at_a, at_b) in enumerate(places):
-        where[16 * i : 16 * i + 8, :] = at_a
-        where[16 * i + 8 : 16 * i + 16, :] = at_b
-    toks = [c[0:R, :] for c in chunks]
-    tok = toks[0] if len(toks) == 1 else jnp.concatenate(toks, axis=0)
-    pick_into(picks, (own, other), tok, places)
-
-
-def back_body(first):
+def score_body(n):
+    def body(pos, own, other, *refs):
+        chunks, (picks, where, *rows) = refs[:n], refs[n:]
+        places = [locate(c[R : R + 8, 0:384].astype(F32), pos) for c in chunks]
+        for i, (at_a, at_b) in enumerate(places):
+            where[16 * i : 16 * i + 8, :] = at_a
+            where[16 * i + 8 : 16 * i + 16, :] = at_b
+        toks = [c[0:R, :] for c in chunks]
+        tok = toks[0] if n == 1 else jnp.concatenate(toks, axis=0)
+        for out in rows:
+            out[...] = tok
+        pick_into(picks, (own, other), tok, places)
+
+    return body
+
+
+def back_body(first, n):
     def body(own, other, where, *refs):
-        chunks, picks = refs[:-1], refs[-1]
+        chunks, (picks, *rows) = refs[:n], refs[n:]
         toks = [c[...] for c in chunks]
         places = []
-        for i in range(len(chunks)):
+        for i in range(n):
             at = 16 * (first + i)
             places.append((where[at : at + 8, :], where[at + 8 : at + 16, :]))
-        tok = toks[0] if len(toks) == 1 else jnp.concatenate(toks, axis=0)
+        tok = toks[0] if n == 1 else jnp.concatenate(toks, axis=0)
+        for out in rows:
+            out[...] = tok
         pick_into(picks, (own, other), tok, places)
 
     return body
@@ -300,19 +307,26 @@
     return parts
 
 
-def load_rows(refs, rows, sem):
+def load_rows(most, last, rows, sem):
     copies = [
-        pltpu.make_async_copy(ref.at[pl.ds(0, R)], rows.at[pl.ds(i * R, R)], sem.at[i]) for i, ref in enumerate(refs)
+        pltpu.make_async_copy(most, rows.at[pl.ds(0, 7 * R)], sem.at[0]),
+        pltpu.make_async_copy(last.at[pl.ds(0, R)], rows.at[pl.ds(7 * R, R)], sem.at[1]),
     ]
     for copy in copies:
         copy.start()
     return copies
 
 
+def tables_body(c0, c1, c2, c3, enc, dec):
+    for i, ref in enumerate((c0, c1, c2, c3)):
+        enc[R * i : R * (i + 1), :] = ref[0:R, :]
+        dec[R * i : R * (i + 1), :] = ref[R : 2 * R, :]
+        dec[4 * R + 8 * i : 4 * R + 8 * i + 8, :] = ref[2 * R : 2 * R + 8, :]
+
+
 def fitted_body(half):
-    def body(at, act, after, *refs):
-        chunks, (out, rows, sem) = refs[:8], refs[8:]
-        copies = load_rows(chunks, rows, sem)
+    def body(at, act, after, most, last, out, rows, sem):
+        copies = load_rows(most, last, rows, sem)
         parts = [jnp.concatenate(turned_table(at, act, 4 * half + q), axis=1).astype(BF) for q in range(4)]
         table = jnp.concatenate(parts, axis=0)
         for copy in copies:
@@ -323,10 +337,9 @@
 
 
 def encgrad_body(half):
-    def body(got, at, ranks, *refs):
-        chunks, rest = refs[:8], refs[8:]
+    def body(got, at, ranks, most, last, *rest):
         out, (rows, sem) = rest[0], rest[-2:]
-        copies = load_rows(chunks, rows, sem)
+        copies = load_rows(most, last, rows, sem)
         grad = jnp.where(at[...] >= 0, unsqueeze(total(got, 0, 32), ranks[...]) * LOSS_GRAD, 0.0)
         if half == 0:
             gram = rest[1]
@@ -370,6 +383,12 @@
     out[...] = dot(weights, decoder[...], NN)
 
 
+def finish_body(a, b, c, out, bias):
+    total_of = lambda lo, hi, n: a[lo:hi, 0:n].astype(F32) + b[lo:hi, 0:n].astype(F32) + c[lo:hi, 0:n].astype(F32)
+    out[...] = total_of(0, R, 1024).astype(BF)
+    bias[...] = total_of(R, R + 8, R)
+
+
 def add(a, b):
     return (a.astype(F32) + b.astype(F32)).astype(BF)
 
@@ -383,8 +402,9 @@
 
 def scatter_x(own, theirs):
     blocks = [add(own[i], theirs[i]) for i in range(4)]
-    to_next = add(blocks[2], move(blocks[3], dx=1))
-    return blocks[0], move(blocks[1], dx=-1), move(to_next, dx=1)
+    far = move(blocks[3], dx=1)
+    prev = move(blocks[1], dx=-1)
+    return blocks[0], prev, move(add(blocks[2], far), dx=1)
 
 
 def per_device(tokens, dec_bias, encoder, enc_bias, decoder, atom_ids, block_count):
@@ -392,50 +412,51 @@
     pos = jnp.stack([place >> 4, (place >> 1) & 7, place & 1]).astype(I32)
     bias_row = dec_bias.reshape(1, -1)
 
-    sent = call(center_body, sds((R + 8, 1024), BF), tokens, bias_row, atom_ids, specs=whole(3), name="center")
+    sent = call(center_body, sds((R + 8, 1024), BF), tokens, bias_row, atom_ids, specs=whole(3))
     packed, gram_part = call(
         pack_body,
         (sds((2 * R + 8, 1024), BF), sds((R, R), F32)),
-        encoder, decoder, enc_bias.reshape(1, -1), sent, specs=whole(3) + [ANY_SPEC], name="pack",
+        encoder, decoder, enc_bias.reshape(1, -1), sent, specs=whole(3) + [ANY_SPEC],
     )
     tok = gather_z(sent)
 
     x1, x2 = move(packed, dx=1), move(packed, dx=-1)
     x3 = move(x1, dx=1)
-    enc_own = jnp.concatenate([encoder, x1[:R], x2[:R], x3[:R]], axis=0)
-    dec_own = jnp.concatenate(
-        [decoder, x1[R : 2 * R], x2[R : 2 * R], x3[R : 2 * R], packed[2 * R :], x1[2 * R :], x2[2 * R :], x3[2 * R :]],
-        axis=0,
+    enc_own, dec_own = call(
+        tables_body, (sds((4 * R, 1024), BF), sds((4 * R + 32, 1024), BF)), packed, x1, x2, x3,
+        specs=whole(4),
     )
     enc_other = move(enc_own, dc=1)
     dec_other = move(dec_own, dc=1)
 
     def score(chunks):
         n = len(chunks)
+        rows = [sds((n * R, 1024), BF)] if n > 1 else []
         return call(
-            score_body,
-            (sds((16 * n, 128), F32), sds((16 * n, 128), I32)),
+            score_body(n),
+            (sds((16 * n, 128), F32), sds((16 * n, 128), I32), *rows),
             pos, enc_own, enc_other, *chunks,
-            specs=[SMEM_SPEC] + whole(2 + n), name="score",
+            specs=[SMEM_SPEC] + whole(2 + n),
         )
 
-    picks, wheres = zip(score(tok[0:7]), score(tok[7:8]))
+    pick_most, where_most, tok_most = score(tok[0:7])
+    pick_last, where_last = score(tok[7:8])
     out, where, ranks = call(
         send_body, (sds((NY, 64, 128), BF), sds((R, R), I32), sds((64, R), I32)),
-        *picks, *wheres, gram_part, specs=whole(5), name="send",
+        pick_most, pick_last, where_most, where_last, gram_part, specs=whole(5),
     )
     got = lax.all_to_all(out, "width", split_axis=0, concat_axis=0, tiled=True)
 
     act, at_t, act_t, gram_rows, d7 = call(
         act_body,
         (sds((R, R), F32), sds((R, R), I32), sds((R, R), F32), sds((32, 128), BF), sds((R, 1024), BF)),
-        got, dec_own, dec_other, where, ranks, specs=whole(5), name="act",
+        got, dec_own, dec_other, where, ranks, specs=whole(5),
     )
 
     def decoded(ms, dtype=BF):
         return call(
             decode_body(ms), tuple(sds((R, 1024), dtype) for _ in ms),
-            at_t, act_t, dec_own, dec_other, specs=whole(4), name="decode",
+            at_t, act_t, dec_own, dec_other, specs=whole(4),
         )
 
     d5, d6 = decoded((5, 6))
@@ -456,23 +477,23 @@
 
     def back(chunks, first):
         n = len(chunks)
+        rows = [sds((n * R, 1024), BF)] if n > 1 else []
         return call(
-            back_body(first), sds((16 * n, 128), F32),
-            dec_own, dec_other, where, *chunks, specs=whole(3 + n), name="back",
+            back_body(first, n), (sds((16 * n, 128), F32), *rows),
+            dec_own, dec_other, where, *chunks, specs=whole(3 + n),
         )
 
-    backs = (back(res[0:7], 0), back(res[7:8], 7))
-    out2 = call(
-        resend_body, sds((NY, 64, 128), BF), *backs, where, ranks, gram_rows, specs=whole(5), name="resend"
-    )
+    back_most, res_most = back(res[0:7], 0)
+    (back_last,) = back(res[7:8], 7)
+    out2 = call(resend_body, sds((NY, 64, 128), BF), back_most, back_last, where, ranks, gram_rows, specs=whole(5))
     got2 = lax.all_to_all(out2, "width", split_axis=0, concat_axis=0, tiled=True)
 
-    scratch = [pltpu.VMEM((8 * R, 1024), BF), pltpu.SemaphoreType.DMA((8,))]
+    scratch = [pltpu.VMEM((8 * R, 1024), BF), pltpu.SemaphoreType.DMA((2,))]
 
     def fitted(half, after):
         return call(
-            fitted_body(half), sds((4 * R, 1024), BF), where, act, after, *res,
-            specs=whole(2) + [ANY_SPEC] * 9, scratch=scratch, name="fitted",
+            fitted_body(half), sds((4 * R, 1024), BF), where, act, after, res_most, res[7],
+            specs=whole(2) + [ANY_SPEC] * 3, scratch=scratch,
         )
 
     fit_other = fitted(1, out2)
@@ -483,21 +504,18 @@
     def encgrad(half):
         outs = [sds((4, R + 8, 1024), BF)] + ([sds((R, R), F32)] if half == 0 else [])
         return call(
-            encgrad_body(half), tuple(outs), got2, where, ranks, *tok,
-            specs=whole(3) + [ANY_SPEC] * 8, scratch=scratch, name="encgrad",
+            encgrad_body(half), tuple(outs), got2, where, ranks, tok_most, tok[7],
+            specs=whole(3) + [ANY_SPEC] * 2, scratch=scratch,
         )
 
     (eg_other,) = encgrad(1)
     eg_theirs = move(eg_other, dc=1)
     eg_own, gram = encgrad(0)
     eg = scatter_x(eg_own, eg_theirs)
-    eg_sum = eg[0].astype(F32) + eg[1].astype(F32) + eg[2].astype(F32)
-    encoder_grad = eg_sum[:R].astype(BF)
-    bias_grad = eg_sum[R, 0:R]
-
-    penalty = call(
-        penalty_body, sds((R, 1024), F32), block_count, gram, decoder, specs=[SMEM_SPEC] + whole(2), name="penalty"
-    )
+    encoder_grad, bias_grad = call(finish_body, (sds((R, 1024), BF), sds((8, R), F32)), *eg, specs=whole(3))
+    bias_grad = bias_grad[0]
+
+    penalty = call(penalty_body, sds((R, 1024), F32), block_count, gram, decoder, specs=[SMEM_SPEC] + whole(2))
     decoder_grad = (fit[0].astype(F32) + fit[1].astype(F32) + fit[2].astype(F32) + penalty).astype(BF)
     return (residual, encoder_grad, decoder_grad, bias_grad)
 

time: 246 us -> 247 us (level)
  the two profiles are of different devices: /device:TPU:8 before, /device:TPU:6 now
where the time goes in v4:
time: 247 us; the launch traced here: 243 us
  starting transfers between devices  128 us (52%)
  waiting for transfers between devices  61.9 us (25%)
  Pallas kernels  32.3 us (13%)
  local copies, waits for them, and re-layouts  13.6 us (6%)
  other arithmetic  5.15 us (2%)
    ppermute x34, starting transfers between devices, move(): return lax.ppermute(value, 'atoms', _perm(**shift))  118 us
    ppermute x34, waiting for transfers between devices, move(): return lax.ppermute(value, 'atoms', _perm(**shift))  50.2 us
    pallas_call x20, Pallas kernels, call(): pl.pallas_call(body, out_shape=outs, in_specs=specs, scratch_shapes=scrat...  32.3 us
    unnamed x51, local copies, waits for them, and re-layouts  13.1 us
    all_to_all x1, waiting for transfers between devices, per_device(): got = lax.all_to_all(out, 'width', split_axis=0, concat_axis=0, tiled=True)  9.07 us
    all_to_all x1, starting transfers between devices, per_device(): got = lax.all_to_all(out, 'width', split_axis=0, concat_axis=0, tiled=True)  7.11 us
  transfers between devices with their start and end apart: 36, of which 21 were waited for; matrix products, arithmetic and copies ran while one was open for 2% of the time, Pallas kernels for 11%

profile of v4, /device:TPU:6, one launch (start us, length us, event | category | flops | bytes accessed | tf_op | source)
XLA Modules:
  0.0 243.1 jit_solution(1816456643607907461)
XLA Ops:
  6.7 7.7 %collective-permute-start = (bf16[264,1024]{1,0:T(8,128)(2,1)S(1)}, bf16[264,1024]{1,0:T(8,128)(2,1)S(1)}, u32[]{:S(2)}, u32[]{:S(2)}) collective-permute-start(bf16[264,1024]{1,0:T(8,128)(2,1)S(1)} %get-tuple-element.33.c0), channel_id=1, source_target_pairs={{0,128},{8,392},{16,144},{24,408},{32,160},{40,424},{48,176},{56,4... | collective-permute-start | bytes 1622024 | tf_op jit(solution)/shard_map/ppermute | solution.py:34
  16.4 8.6 %collective-permute-done.c1 = bf16[264,1024]{1,0:T(8,128)(2,1)S(1)} collective-permute-done((bf16[264,1024]{1,0:T(8,128)(2,1)S(1)}, bf16[264,1024]{1,0:T(8,128)(2,1)S(1)}, u32[]{:S(2)}, u32[]{:S(2)}) %collective-permute-start) | collective-permute-done | bytes 540704 | tf_op jit(solution)/shard_map/ppermute | solution.py:34
  25.0 5.6 %collective-permute-start.2 = (bf16[264,1024]{1,0:T(8,128)(2,1)S(1)}, bf16[264,1024]{1,0:T(8,128)(2,1)S(1)}, u32[]{:S(2)}, u32[]{:S(2)}) collective-permute-start(bf16[264,1024]{1,0:T(8,128)(2,1)S(1)} %collective-permute-done.c1), channel_id=1, source_target_pairs={{0,128},{8,392},{16,144},{24,408},{32,160},{40,424},{48,176},{56,4... | collective-permute-start | bytes 1622024 | tf_op jit(solution)/shard_map/ppermute | solution.py:34
  32.5 4.9 %collective-permute-done.2.c3 = bf16[264,1024]{1,0:T(8,128)(2,1)S(1)} collective-permute-done((bf16[264,1024]{1,0:T(8,128)(2,1)S(1)}, bf16[264,1024]{1,0:T(8,128)(2,1)S(1)}, u32[]{:S(2)}, u32[]{:S(2)}) %collective-permute-start.2) | collective-permute-done | bytes 540704 | tf_op jit(solution)/shard_map/ppermute | solution.py:34
  42.0 7.1 %collective-permute-start.5 = (bf16[136,1024]{1,0:T(8,128)(2,1)S(1)}, bf16[136,1024]{1,0:T(8,128)(2,1)S(1)}, u32[]{:S(2)}, u32[]{:S(2)}) collective-permute-start(bf16[136,1024]{1,0:T(8,128)(2,1)S(1)} %shard_map.102.after.refs_0_), channel_id=1, source_target_pairs={{0,112},{8,24},{16,0},{24,40},{32,16},{40,56},{48,32},{56,72},{64,... | collective-permute-start | bytes 835592 | tf_op jit(solution)/shard_map/ppermute | solution.py:34
  51.8 3.4 %collective-permute-done.5.refs_2_ = bf16[136,1024]{1,0:T(8,128)(2,1)S(1)} collective-permute-done((bf16[136,1024]{1,0:T(8,128)(2,1)S(1)}, bf16[136,1024]{1,0:T(8,128)(2,1)S(1)}, u32[]{:S(2)}, u32[]{:S(2)}) %collective-permute-start.5) | collective-permute-done | bytes 278560 | tf_op jit(solution)/shard_map/ppermute | solution.py:34
  55.2 5.6 %collective-permute-start.7 = (bf16[136,1024]{1,0:T(8,128)(2,1)S(1)}, bf16[136,1024]{1,0:T(8,128)(2,1)}, u32[]{:S(2)}, u32[]{:S(2)}) collective-permute-start(bf16[136,1024]{1,0:T(8,128)(2,1)S(1)} %collective-permute-done.5.refs_2_), channel_id=1, source_target_pairs={{0,112},{8,24},{16,0},{24,40},{32,16},{40,56},{48,32},{56,72},{64,... | collective-permute-start | bytes 835592 | tf_op jit(solution)/shard_map/ppermute | solution.py:34
  64.1 3.5 %collective-permute-done.7.refs_4_ = bf16[136,1024]{1,0:T(8,128)(2,1)} collective-permute-done((bf16[136,1024]{1,0:T(8,128)(2,1)S(1)}, bf16[136,1024]{1,0:T(8,128)(2,1)}, u32[]{:S(2)}, u32[]{:S(2)}) %collective-permute-start.7) | collective-permute-done | bytes 278560 | tf_op jit(solution)/shard_map/ppermute | solution.py:34
  67.6 5.7 %collective-permute-start.9 = (bf16[136,1024]{1,0:T(8,128)(2,1)}, bf16[136,1024]{1,0:T(8,128)(2,1)}, u32[]{:S(2)}, u32[]{:S(2)}) collective-permute-start(bf16[136,1024]{1,0:T(8,128)(2,1)} %collective-permute-done.7.refs_4_), channel_id=1, source_target_pairs={{0,112},{8,24},{16,0},{24,40},{32,16},{40,56},{48,32},{56,72},{64,... | collective-permute-start | bytes 835592 | tf_op jit(solution)/shard_map/ppermute | solution.py:34
  76.0 3.6 %collective-permute-done.9.refs_6_ = bf16[136,1024]{1,0:T(8,128)(2,1)} collective-permute-done((bf16[136,1024]{1,0:T(8,128)(2,1)}, bf16[136,1024]{1,0:T(8,128)(2,1)}, u32[]{:S(2)}, u32[]{:S(2)}) %collective-permute-start.9) | collective-permute-done | bytes 278560 | tf_op jit(solution)/shard_map/ppermute | solution.py:34
  82.5 4.5 %shard_map.105 = (f32[112,128]{1,0:T(8,128)S(1)}, s32[112,128]{1,0:T(8,128)S(1)}, bf16[896,1024]{1,0:T(8,128)(2,1)S(1)}) custom-call(s32[3]{0:T(128)S(1)} %pad_add_fusion.pos, bf16[512,1024]{1,0:T(8,128)(2,1)S(1)} %get-tuple-element.34.own, bf16[512,1024]{1,0:T(8,128)(2,1)} %collective-permute-done.3.other, bf16[136,1024]{1,0:T(8,128)(2,1)S(1)} %shard_map.102.after.refs_0_, ...), custom_call_target="tpu_custom_call" | custom-call | tf_op jit(solution)/shard_map/pallas_call | solution.py:38
  91.1 7.1 %all-to-all-start = ((bf16[8,64,128]{2,1,0:T(8,128)(2,1)}), bf16[8,64,128]{2,1,0:T(8,128)(2,1)S(1)}, u32[]{:S(2)}, u32[]{:S(2)}) async-start(bf16[8,64,128]{2,1,0:T(8,128)(2,1)} %get-tuple-element.40), calls=%async_computation | async-start | bytes 262144 | tf_op jit(solution)/shard_map/all_to_all | solution.py:448
  98.2 9.1 %all-to-all-done.got = bf16[8,64,128]{2,1,0:T(8,128)(2,1)S(1)} async-done(((bf16[8,64,128]{2,1,0:T(8,128)(2,1)}), bf16[8,64,128]{2,1,0:T(8,128)(2,1)S(1)}, u32[]{:S(2)}, u32[]{:S(2)}) %all-to-all-start) | async-done | bytes 131104 | tf_op jit(solution)/shard_map/all_to_all | solution.py:448
  112.4 5.6 %collective-permute-start.16 = (bf16[128,1024]{1,0:T(8,128)(2,1)S(1)}, bf16[128,1024]{1,0:T(8,128)(2,1)S(1)}, u32[]{:S(2)}, u32[]{:S(2)}) collective-permute-start(bf16[128,1024]{1,0:T(8,128)(2,1)S(1)} %get-tuple-element.52), channel_id=1, source_target_pairs={{0,112},{8,24},{16,0},{24,40},{32,16},{40,56},{48,32},{56,72},{64,... | collective-permute-start | bytes 786440 | tf_op jit(solution)/shard_map/ppermute | solution.py:34
  122.7 5.6 %collective-permute-start.17 = (bf16[128,1024]{1,0:T(8,128)(2,1)S(1)}, bf16[128,1024]{1,0:T(8,128)(2,1)S(1)}, u32[]{:S(2)}, u32[]{:S(2)}) collective-permute-start(bf16[128,1024]{1,0:T(8,128)(2,1)S(1)} %add_convert_fusion.11), channel_id=1, source_target_pairs={{0,112},{8,24},{16,0},{24,40},{32,16},{40,56},{48,32},{56,72},{64,... | collective-permute-start | bytes 786440 | tf_op jit(solution)/shard_map/ppermute | solution.py:34
  134.1 5.6 %collective-permute-start.18 = (bf16[128,1024]{1,0:T(8,128)(2,1)S(1)}, bf16[128,1024]{1,0:T(8,128)(2,1)S(1)}, u32[]{:S(2)}, u32[]{:S(2)}) collective-permute-start(bf16[128,1024]{1,0:T(8,128)(2,1)S(1)} %add_convert_fusion.10), channel_id=1, source_target_pairs={{0,112},{8,24},{16,0},{24,40},{32,16},{40,56},{48,32},{56,72},{64,... | collective-permute-start | bytes 786440 | tf_op jit(solution)/shard_map/ppermute | solution.py:34
  146.3 5.3 %collective-permute-done.15 = bf16[128,1024]{1,0:T(8,128)(2,1)S(1)} collective-permute-done((bf16[128,1024]{1,0:T(8,128)(2,1)S(1)}, bf16[128,1024]{1,0:T(8,128)(2,1)S(1)}, u32[]{:S(2)}, u32[]{:S(2)}) %collective-permute-start.15) | collective-permute-done | bytes 262176 | tf_op jit(solution)/shard_map/ppermute | solution.py:34
  153.8 5.1 %collective-permute-start.20 = (bf16[128,1024]{1,0:T(8,128)(2,1)S(1)}, bf16[128,1024]{1,0:T(8,128)(2,1)S(1)}, u32[]{:S(2)}, u32[]{:S(2)}) collective-permute-start(bf16[128,1024]{1,0:T(8,128)(2,1)S(1)} %subtract_convert_fusion.refs_0_), channel_id=1, source_target_pairs={{0,112},{8,24},{16,0},{24,40},{32,16},{40,56},{48,32},{56,72},{64,... | collective-permute-start | bytes 786440 | tf_op jit(solution)/shard_map/ppermute | solution.py:34
  158.9 4.1 %collective-permute-done.19.refs_1_ = bf16[128,1024]{1,0:T(8,128)(2,1)S(1)} collective-permute-done((bf16[128,1024]{1,0:T(8,128)(2,1)S(1)}, bf16[128,1024]{1,0:T(8,128)(2,1)S(1)}, u32[]{:S(2)}, u32[]{:S(2)}) %collective-permute-start.19) | collective-permute-done | bytes 262176 | tf_op jit(solution)/shard_map/ppermute | solution.py:34
  165.1 5.6 %collective-permute-start.22 = (bf16[128,1024]{1,0:T(8,128)(2,1)S(1)}, bf16[128,1024]{1,0:T(8,128)(2,1)S(1)}, u32[]{:S(2)}, u32[]{:S(2)}) collective-permute-start(bf16[128,1024]{1,0:T(8,128)(2,1)S(1)} %collective-permute-done.20.refs_2_), channel_id=1, source_target_pairs={{0,112},{8,24},{16,0},{24,40},{32,16},{40,56},{48,32},{56,72},{64,... | collective-permute-start | bytes 786440 | tf_op jit(solution)/shard_map/ppermute | solution.py:34
  176.7 5.6 %collective-permute-start.24 = (bf16[128,1024]{1,0:T(8,128)(2,1)S(1)}, bf16[128,1024]{1,0:T(8,128)(2,1)S(1)}, u32[]{:S(2)}, u32[]{:S(2)}) collective-permute-start(bf16[128,1024]{1,0:T(8,128)(2,1)S(1)} %collective-permute-done.22.refs_4_), channel_id=1, source_target_pairs={{0,112},{8,24},{16,0},{24,40},{32,16},{40,56},{48,32},{56,72},{64,... | collective-permute-start | bytes 786440 | tf_op jit(solution)/shard_map/ppermute | solution.py:34
  194.3 3.4 %all-to-all-start.1 = ((bf16[8,64,128]{2,1,0:T(8,128)(2,1)}), bf16[8,64,128]{2,1,0:T(8,128)(2,1)S(1)}, u32[]{:S(2)}, u32[]{:S(2)}) async-start(bf16[8,64,128]{2,1,0:T(8,128)(2,1)} %shard_map.115.after), calls=%async_computation.1 | async-start | bytes 262144 | tf_op jit(solution)/shard_map/all_to_all | solution.py:489
  222.4 3.9 %collective-permute-start.31 = (bf16[128,1024]{1,0:T(8,128)(2,1)S(1)}, bf16[128,1024]{1,0:T(8,128)(2,1)S(1)}, u32[]{:S(2)}, u32[]{:S(2)}) collective-permute-start(bf16[128,1024]{1,0:T(8,128)(2,1)S(1)} %get-tuple-element.65), channel_id=1, source_target_pairs={{0,384},{8,136},{16,400},{24,152},{32,416},{40,168},{48,432},{56,1... | collective-permute-start | bytes 786440 | tf_op jit(solution)/shard_map/ppermute | solution.py:34
  233.4 4.4 %collective-permute-start.29 = (bf16[136,1024]{1,0:T(8,128)(2,1)S(1)}, bf16[136,1024]{1,0:T(8,128)(2,1)S(1)}, u32[]{:S(2)}, u32[]{:S(2)}) collective-permute-start(bf16[136,1024]{1,0:T(8,128)(2,1)S(1)} %fusion), channel_id=1, source_target_pairs={{0,128},{8,392},{16,144},{24,408},{32,160},{40,424},{48,176},{56,4... | collective-permute-start | bytes 835592 | tf_op jit(solution)/shard_map/ppermute | solution.py:34
  (132 shorter events, 110.4 us)
Async XLA Ops:
  6.7 18.3 %collective-permute-start = (bf16[264,1024]{1,0:T(8,128)(2,1)S(1)}, bf16[264,1024]{1,0:T(8,128)(2,1)S(1)}, u32[]{:S(2)}, u32[]{:S(2)}) collective-permute-start(bf16[264,1024]{1,0:T(8,128)(2,1)S(1)} %get-tuple-element.33.c0), channel_id=1, source_target_pairs={{0,128},{8,392},{16,144},{24,408},{32,160},{40,424},{48,176},{56,4... | collective-permute-start | bytes 1622024 | tf_op jit(solution)/shard_map/ppermute | solution.py:34
  14.5 18.1 %collective-permute-start.1 = (bf16[264,1024]{1,0:T(8,128)(2,1)S(1)}, bf16[264,1024]{1,0:T(8,128)(2,1)S(1)}, u32[]{:S(2)}, u32[]{:S(2)}) collective-permute-start(bf16[264,1024]{1,0:T(8,128)(2,1)S(1)} %get-tuple-element.33.c0), channel_id=1, source_target_pairs={{0,384},{8,136},{16,400},{24,152},{32,416},{40,168},{48,432},{56,1... | collective-permute-start | bytes 1622024 | tf_op jit(solution)/shard_map/ppermute | solution.py:34
  25.0 12.4 %collective-permute-start.2 = (bf16[264,1024]{1,0:T(8,128)(2,1)S(1)}, bf16[264,1024]{1,0:T(8,128)(2,1)S(1)}, u32[]{:S(2)}, u32[]{:S(2)}) collective-permute-start(bf16[264,1024]{1,0:T(8,128)(2,1)S(1)} %collective-permute-done.c1), channel_id=1, source_target_pairs={{0,128},{8,392},{16,144},{24,408},{32,160},{40,424},{48,176},{56,4... | collective-permute-start | bytes 1622024 | tf_op jit(solution)/shard_map/ppermute | solution.py:34
  30.6 18.5 %collective-permute-start.4 = (bf16[136,1024]{1,0:T(8,128)(2,1)S(1)}, bf16[136,1024]{1,0:T(8,128)(2,1)S(1)}, u32[]{:S(2)}, u32[]{:S(2)}) collective-permute-start(bf16[136,1024]{1,0:T(8,128)(2,1)S(1)} %shard_map.102.after.refs_0_), channel_id=1, source_target_pairs={{0,16},{8,120},{16,32},{24,8},{32,48},{40,24},{48,64},{56,40},{64,... | collective-permute-start | bytes 835592 | tf_op jit(solution)/shard_map/ppermute | solution.py:34
  37.6 42.0 %collective-permute-start.3 = (bf16[512,1024]{1,0:T(8,128)(2,1)S(1)}, bf16[512,1024]{1,0:T(8,128)(2,1)}, u32[]{:S(2)}, u32[]{:S(2)}) collective-permute-start(bf16[512,1024]{1,0:T(8,128)(2,1)S(1)} %get-tuple-element.34.own), channel_id=1, source_target_pairs={{0,8},{8,0},{16,24},{24,16},{32,40},{40,32},{48,56},{56,48},{64,72... | collective-permute-start | bytes 3145736 | tf_op jit(solution)/shard_map/ppermute | solution.py:34
  39.5 58.7 %collective-permute-start.11 = (bf16[544,1024]{1,0:T(8,128)(2,1)S(1)}, bf16[544,1024]{1,0:T(8,128)(2,1)S(1)}, u32[]{:S(2)}, u32[]{:S(2)}) collective-permute-start(bf16[544,1024]{1,0:T(8,128)(2,1)S(1)} %get-tuple-element.41.own), channel_id=1, source_target_pairs={{0,8},{8,0},{16,24},{24,16},{32,40},{40,32},{48,56},{56,48},{64,72... | collective-permute-start | bytes 3342344 | tf_op jit(solution)/shard_map/ppermute | solution.py:34
  42.0 13.2 %collective-permute-start.5 = (bf16[136,1024]{1,0:T(8,128)(2,1)S(1)}, bf16[136,1024]{1,0:T(8,128)(2,1)S(1)}, u32[]{:S(2)}, u32[]{:S(2)}) collective-permute-start(bf16[136,1024]{1,0:T(8,128)(2,1)S(1)} %shard_map.102.after.refs_0_), channel_id=1, source_target_pairs={{0,112},{8,24},{16,0},{24,40},{32,16},{40,56},{48,32},{56,72},{64,... | collective-permute-start | bytes 835592 | tf_op jit(solution)/shard_map/ppermute | solution.py:34
  49.1 12.4 %collective-permute-start.6 = (bf16[136,1024]{1,0:T(8,128)(2,1)S(1)}, bf16[136,1024]{1,0:T(8,128)(2,1)S(1)}, u32[]{:S(2)}, u32[]{:S(2)}) collective-permute-start(bf16[136,1024]{1,0:T(8,128)(2,1)S(1)} %collective-permute-done.4.refs_1_), channel_id=1, source_target_pairs={{0,16},{8,120},{16,32},{24,8},{32,48},{40,24},{48,64},{56,40},{64,... | collective-permute-start | bytes 835592 | tf_op jit(solution)/shard_map/ppermute | solution.py:34
  55.2 12.5 %collective-permute-start.7 = (bf16[136,1024]{1,0:T(8,128)(2,1)S(1)}, bf16[136,1024]{1,0:T(8,128)(2,1)}, u32[]{:S(2)}, u32[]{:S(2)}) collective-permute-start(bf16[136,1024]{1,0:T(8,128)(2,1)S(1)} %collective-permute-done.5.refs_2_), channel_id=1, source_target_pairs={{0,112},{8,24},{16,0},{24,40},{32,16},{40,56},{48,32},{56,72},{64,... | collective-permute-start | bytes 835592 | tf_op jit(solution)/shard_map/ppermute | solution.py:34
  61.5 12.5 %collective-permute-start.8 = (bf16[136,1024]{1,0:T(8,128)(2,1)S(1)}, bf16[136,1024]{1,0:T(8,128)(2,1)}, u32[]{:S(2)}, u32[]{:S(2)}) collective-permute-start(bf16[136,1024]{1,0:T(8,128)(2,1)S(1)} %collective-permute-done.6.refs_3_), channel_id=1, source_target_pairs={{0,16},{8,120},{16,32},{24,8},{32,48},{40,24},{48,64},{56,40},{64,... | collective-permute-start | bytes 835592 | tf_op jit(solution)/shard_map/ppermute | solution.py:34
  67.6 12.0 %collective-permute-start.9 = (bf16[136,1024]{1,0:T(8,128)(2,1)}, bf16[136,1024]{1,0:T(8,128)(2,1)}, u32[]{:S(2)}, u32[]{:S(2)}) collective-permute-start(bf16[136,1024]{1,0:T(8,128)(2,1)} %collective-permute-done.7.refs_4_), channel_id=1, source_target_pairs={{0,112},{8,24},{16,0},{24,40},{32,16},{40,56},{48,32},{56,72},{64,... | collective-permute-start | bytes 835592 | tf_op jit(solution)/shard_map/ppermute | solution.py:34
  74.0 13.1 %collective-permute-start.10 = (bf16[136,1024]{1,0:T(8,128)(2,1)}, bf16[136,1024]{1,0:T(8,128)(2,1)}, u32[]{:S(2)}, u32[]{:S(2)}) collective-permute-start(bf16[136,1024]{1,0:T(8,128)(2,1)} %collective-permute-done.8.refs_5_), channel_id=1, source_target_pairs={{0,16},{8,120},{16,32},{24,8},{32,48},{40,24},{48,64},{56,40},{64,... | collective-permute-start | bytes 835592 | tf_op jit(solution)/shard_map/ppermute | solution.py:34
  91.1 16.2 %all-to-all-start = ((bf16[8,64,128]{2,1,0:T(8,128)(2,1)}), bf16[8,64,128]{2,1,0:T(8,128)(2,1)S(1)}, u32[]{:S(2)}, u32[]{:S(2)}) async-start(bf16[8,64,128]{2,1,0:T(8,128)(2,1)} %get-tuple-element.40), calls=%async_computation | async-start | bytes 262144 | tf_op jit(solution)/shard_map/all_to_all | solution.py:448
  122.7 11.3 %collective-permute-start.17 = (bf16[128,1024]{1,0:T(8,128)(2,1)S(1)}, bf16[128,1024]{1,0:T(8,128)(2,1)S(1)}, u32[]{:S(2)}, u32[]{:S(2)}) collective-permute-start(bf16[128,1024]{1,0:T(8,128)(2,1)S(1)} %add_convert_fusion.11), channel_id=1, source_target_pairs={{0,112},{8,24},{16,0},{24,40},{32,16},{40,56},{48,32},{56,72},{64,... | collective-permute-start | bytes 786440 | tf_op jit(solution)/shard_map/ppermute | solution.py:34
  128.4 11.3 %collective-permute-start.14 = (bf16[128,1024]{1,0:T(8,128)(2,1)S(1)}, bf16[128,1024]{1,0:T(8,128)(2,1)S(1)}, u32[]{:S(2)}, u32[]{:S(2)}) collective-permute-start(bf16[128,1024]{1,0:T(8,128)(2,1)S(1)} %add_convert_fusion.13), channel_id=1, source_target_pairs={{0,16},{8,120},{16,32},{24,8},{32,48},{40,24},{48,64},{56,40},{64,... | collective-permute-start | bytes 786440 | tf_op jit(solution)/shard_map/ppermute | solution.py:34
  134.1 12.3 %collective-permute-start.18 = (bf16[128,1024]{1,0:T(8,128)(2,1)S(1)}, bf16[128,1024]{1,0:T(8,128)(2,1)S(1)}, u32[]{:S(2)}, u32[]{:S(2)}) collective-permute-start(bf16[128,1024]{1,0:T(8,128)(2,1)S(1)} %add_convert_fusion.10), channel_id=1, source_target_pairs={{0,112},{8,24},{16,0},{24,40},{32,16},{40,56},{48,32},{56,72},{64,... | collective-permute-start | bytes 786440 | tf_op jit(solution)/shard_map/ppermute | solution.py:34
  139.8 11.9 %collective-permute-start.15 = (bf16[128,1024]{1,0:T(8,128)(2,1)S(1)}, bf16[128,1024]{1,0:T(8,128)(2,1)S(1)}, u32[]{:S(2)}, u32[]{:S(2)}) collective-permute-start(bf16[128,1024]{1,0:T(8,128)(2,1)S(1)} %add_convert_fusion.12), channel_id=1, source_target_pairs={{0,16},{8,120},{16,32},{24,8},{32,48},{40,24},{48,64},{56,40},{64,... | collective-permute-start | bytes 786440 | tf_op jit(solution)/shard_map/ppermute | solution.py:34
  153.8 11.4 %collective-permute-start.20 = (bf16[128,1024]{1,0:T(8,128)(2,1)S(1)}, bf16[128,1024]{1,0:T(8,128)(2,1)S(1)}, u32[]{:S(2)}, u32[]{:S(2)}) collective-permute-start(bf16[128,1024]{1,0:T(8,128)(2,1)S(1)} %subtract_convert_fusion.refs_0_), channel_id=1, source_target_pairs={{0,112},{8,24},{16,0},{24,40},{32,16},{40,56},{48,32},{56,72},{64,... | collective-permute-start | bytes 786440 | tf_op jit(solution)/shard_map/ppermute | solution.py:34
  165.1 11.6 %collective-permute-start.22 = (bf16[128,1024]{1,0:T(8,128)(2,1)S(1)}, bf16[128,1024]{1,0:T(8,128)(2,1)S(1)}, u32[]{:S(2)}, u32[]{:S(2)}) collective-permute-start(bf16[128,1024]{1,0:T(8,128)(2,1)S(1)} %collective-permute-done.20.refs_2_), channel_id=1, source_target_pairs={{0,112},{8,24},{16,0},{24,40},{32,16},{40,56},{48,32},{56,72},{64,... | collective-permute-start | bytes 786440 | tf_op jit(solution)/shard_map/ppermute | solution.py:34
  194.3 12.4 %all-to-all-start.1 = ((bf16[8,64,128]{2,1,0:T(8,128)(2,1)}), bf16[8,64,128]{2,1,0:T(8,128)(2,1)S(1)}, u32[]{:S(2)}, u32[]{:S(2)}) async-start(bf16[8,64,128]{2,1,0:T(8,128)(2,1)} %shard_map.115.after), calls=%async_computation.1 | async-start | bytes 262144 | tf_op jit(solution)/shard_map/all_to_all | solution.py:489
  202.1 13.5 %collective-permute-start.30 = (bf16[512,1024]{1,0:T(8,128)(2,1)S(1)}, bf16[512,1024]{1,0:T(8,128)(2,1)}, u32[]{:S(2)}, u32[]{:S(2)}) collective-permute-start(bf16[512,1024]{1,0:T(8,128)(2,1)S(1)} %shard_map.119.after), channel_id=1, source_target_pairs={{0,8},{8,0},{16,24},{24,16},{32,40},{40,32},{48,56},{56,48},{64,72... | collective-permute-start | bytes 3145736 | tf_op jit(solution)/shard_map/ppermute | solution.py:34
  220.3 12.9 %collective-permute-start.28 = (bf16[136,1024]{1,0:T(8,128)(2,1)S(1)}, bf16[136,1024]{1,0:T(8,128)(2,1)S(1)}, u32[]{:S(2)}, u32[]{:S(2)}) collective-permute-start(bf16[136,1024]{1,0:T(8,128)(2,1)S(1)} %get-tuple-element.62), channel_id=1, source_target_pairs={{0,128},{8,392},{16,144},{24,408},{32,160},{40,424},{48,176},{56,4... | collective-permute-start | bytes 835592 | tf_op jit(solution)/shard_map/ppermute | solution.py:34
  222.4 16.4 %collective-permute-start.31 = (bf16[128,1024]{1,0:T(8,128)(2,1)S(1)}, bf16[128,1024]{1,0:T(8,128)(2,1)S(1)}, u32[]{:S(2)}, u32[]{:S(2)}) collective-permute-start(bf16[128,1024]{1,0:T(8,128)(2,1)S(1)} %get-tuple-element.65), channel_id=1, source_target_pairs={{0,384},{8,136},{16,400},{24,152},{32,416},{40,168},{48,432},{56,1... | collective-permute-start | bytes 786440 | tf_op jit(solution)/shard_map/ppermute | solution.py:34
  227.4 11.5 %collective-permute-start.33 = (bf16[128,1024]{1,0:T(8,128)(2,1)S(1)}, bf16[128,1024]{1,0:T(8,128)(2,1)S(1)}, u32[]{:S(2)}, u32[]{:S(2)}) collective-permute-start(bf16[128,1024]{1,0:T(8,128)(2,1)S(1)} %add_convert_fusion.5), channel_id=1, source_target_pairs={{0,128},{8,392},{16,144},{24,408},{32,160},{40,424},{48,176},{56,4... | collective-permute-start | bytes 786440 | tf_op jit(solution)/shard_map/ppermute | solution.py:34
  (37 other events, 235.8 us)

commit v5 on v4

--- a/solution.py
+++ b/solution.py
@@ -134,20 +134,21 @@
                     out[16 * i + 8 * s + b : 16 * i + 8 * s + b + 1, :] = got
 
 
-def score_body(n):
-    def body(pos, own, other, *refs):
-        chunks, (picks, where, *rows) = refs[:n], refs[n:]
-        places = [locate(c[R : R + 8, 0:384].astype(F32), pos) for c in chunks]
-        for i, (at_a, at_b) in enumerate(places):
-            where[16 * i : 16 * i + 8, :] = at_a
-            where[16 * i + 8 : 16 * i + 16, :] = at_b
-        toks = [c[0:R, :] for c in chunks]
-        tok = toks[0] if n == 1 else jnp.concatenate(toks, axis=0)
-        for out in rows:
-            out[...] = tok
-        pick_into(picks, (own, other), tok, places)
-
-    return body
+def score_some(pos, own, other, toks, exts, picks, where):
+    places = [locate(ext, pos) for ext in exts]
+    for i, (at_a, at_b) in enumerate(places):
+        where[16 * i : 16 * i + 8, :] = at_a
+        where[16 * i + 8 : 16 * i + 16, :] = at_b
+    tok = toks[0] if len(toks) == 1 else jnp.concatenate(toks, axis=0)
+    pick_into(picks, (own, other), tok, places)
+    return tok
+
+
+def score_body(pos, own, other, first, exts, t4, t5, t6, picks, where, rows):
+    some = [exts[8 * i : 8 * i + 8, :] for i in range(4)] + [t[R : R + 8, 0:384].astype(F32) for t in (t4, t5, t6)]
+    rows[...] = score_some(
+        pos, own, other, [first[...]] + [t[0:R, :] for t in (t4, t5, t6)], some, picks, where
+    )
 
 
 def back_body(first, n):
@@ -207,7 +208,8 @@
     return jnp.concatenate(out, axis=0)
 
 
-def send_body(p0, p1, w0, w1, gram, out, where, ranks):
+def send_body(pos, own, other, t7, p0, w0, gram, out, where, ranks, p1, w1):
+    score_some(pos, own, other, [t7[0:R, :]], [t7[R : R + 8, 0:384].astype(F32)], p1, w1)
     picks = jnp.concatenate([p0[...], p1[...]], axis=0)
     at = jnp.concatenate([w0[...], w1[...]], axis=0)
     where[...] = at
@@ -317,11 +319,14 @@
     return copies
 
 
-def tables_body(c0, c1, c2, c3, enc, dec):
+def tables_body(c0, c1, c2, c3, t0, t1, t2, t3, enc, dec, rows, exts):
     for i, ref in enumerate((c0, c1, c2, c3)):
         enc[R * i : R * (i + 1), :] = ref[0:R, :]
         dec[R * i : R * (i + 1), :] = ref[R : 2 * R, :]
         dec[4 * R + 8 * i : 4 * R + 8 * i + 8, :] = ref[2 * R : 2 * R + 8, :]
+    for i, ref in enumerate((t0, t1, t2, t3)):
+        rows[R * i : R * (i + 1), :] = ref[0:R, :]
+        exts[8 * i : 8 * i + 8, :] = ref[R : R + 8, 0:384].astype(F32)
 
 
 def fitted_body(half):
@@ -422,28 +427,22 @@
 
     x1, x2 = move(packed, dx=1), move(packed, dx=-1)
     x3 = move(x1, dx=1)
-    enc_own, dec_own = call(
-        tables_body, (sds((4 * R, 1024), BF), sds((4 * R + 32, 1024), BF)), packed, x1, x2, x3,
-        specs=whole(4),
+    enc_own, dec_own, tok_first, tok_exts = call(
+        tables_body,
+        (sds((4 * R, 1024), BF), sds((4 * R + 32, 1024), BF), sds((4 * R, 1024), BF), sds((32, 384), F32)),
+        packed, x1, x2, x3, *tok[0:4], specs=whole(8),
     )
     enc_other = move(enc_own, dc=1)
     dec_other = move(dec_own, dc=1)
 
-    def score(chunks):
-        n = len(chunks)
-        rows = [sds((n * R, 1024), BF)] if n > 1 else []
-        return call(
-            score_body(n),
-            (sds((16 * n, 128), F32), sds((16 * n, 128), I32), *rows),
-            pos, enc_own, enc_other, *chunks,
-            specs=[SMEM_SPEC] + whole(2 + n),
-        )
-
-    pick_most, where_most, tok_most = score(tok[0:7])
-    pick_last, where_last = score(tok[7:8])
+    pick_most, where_most, tok_most = call(
+        score_body, (sds((112, 128), F32), sds((112, 128), I32), sds((7 * R, 1024), BF)),
+        pos, enc_own, enc_other, tok_first, tok_exts, *tok[4:7], specs=[SMEM_SPEC] + whole(7),
+    )
     out, where, ranks = call(
         send_body, (sds((NY, 64, 128), BF), sds((R, R), I32), sds((64, R), I32)),
-        pick_most, pick_last, where_most, where_last, gram_part, specs=whole(5),
+        pos, enc_own, enc_other, tok[7], pick_most, where_most, gram_part, specs=[SMEM_SPEC] + whole(6),
+        scratch=[pltpu.VMEM((16, 128), F32), pltpu.VMEM((16, 128), I32)],
     )
     got = lax.all_to_all(out, "width", split_axis=0, concat_axis=0, tiled=True)
 

time: 247 us -> 236 us (0.955)
  waiting for transfers between devices: 61.9 us -> 58 us
  local copies, waits for them, and re-layouts: 13.6 us -> 10.2 us
  starting transfers between devices: 128 us -> 125 us
    ppermute x34, waiting for transfers between devices: 50.2 us -> 46.3 us  [move(): return lax.ppermute(value, 'atoms', _perm(**shift))]
    ppermute x34, starting transfers between devices: 118 us -> 114 us  [move(): return lax.ppermute(value, 'atoms', _perm(**shift))]
    unnamed x51 -> x39, local copies, waits for them, and re-layouts: 13.1 us -> 9.72 us
    pallas_call x20 -> x19, Pallas kernels: 32.3 us -> 32.2 us  [call(): pl.pallas_call(body, out_shape=outs, in_specs=specs, scratch_shapes=scrat...]
  transfers between devices with their start and end apart: 36 -> 36, of which waited for: 21 -> 19; matrix products, arithmetic and copies ran while one was open for 2% -> 2% of each run, Pallas kernels for 11% -> 12%
where the time goes in v5:
time: 236 us; the launch traced here: 232 us
  starting transfers between devices  125 us (53%)
  waiting for transfers between devices  58 us (25%)
  Pallas kernels  32.2 us (14%)
  local copies, waits for them, and re-layouts  10.2 us (4%)
  other arithmetic  5.15 us (2%)
    ppermute x34, starting transfers between devices, move(): return lax.ppermute(value, 'atoms', _perm(**shift))  114 us
    ppermute x34, waiting for transfers between devices, move(): return lax.ppermute(value, 'atoms', _perm(**shift))  46.3 us
    pallas_call x19, Pallas kernels, call(): pl.pallas_call(body, out_shape=outs, in_specs=specs, scratch_shapes=scrat...  32.2 us
    unnamed x39, local copies, waits for them, and re-layouts  9.72 us
    all_to_all x1, waiting for transfers between devices, per_device(): got = lax.all_to_all(out, 'width', split_axis=0, concat_axis=0, tiled=True)  9.07 us
    all_to_all x1, starting transfers between devices, per_device(): got = lax.all_to_all(out, 'width', split_axis=0, concat_axis=0, tiled=True)  7.11 us
  transfers between devices with their start and end apart: 36, of which 19 were waited for; matrix products, arithmetic and copies ran while one was open for 2% of the time, Pallas kernels for 12%

profile of v5, /device:TPU:6, one launch (start us, length us, event | category | flops | bytes accessed | tf_op | source)
XLA Modules:
  0.0 232.3 jit_solution(15660779312504070361)
XLA Ops:
  6.1 7.7 %collective-permute-start = (bf16[264,1024]{1,0:T(8,128)(2,1)S(1)}, bf16[264,1024]{1,0:T(8,128)(2,1)S(1)}, u32[]{:S(2)}, u32[]{:S(2)}) collective-permute-start(bf16[264,1024]{1,0:T(8,128)(2,1)S(1)} %get-tuple-element.33.c0), channel_id=1, source_target_pairs={{0,128},{8,392},{16,144},{24,408},{32,160},{40,424},{48,176},{56,4... | collective-permute-start | bytes 1622024 | tf_op jit(solution)/shard_map/ppermute | solution.py:34
  20.7 5.6 %collective-permute-start.2 = (bf16[264,1024]{1,0:T(8,128)(2,1)S(1)}, bf16[264,1024]{1,0:T(8,128)(2,1)S(1)}, u32[]{:S(2)}, u32[]{:S(2)}) collective-permute-start(bf16[264,1024]{1,0:T(8,128)(2,1)S(1)} %collective-permute-done.c1), channel_id=1, source_target_pairs={{0,128},{8,392},{16,144},{24,408},{32,160},{40,424},{48,176},{56,4... | collective-permute-start | bytes 1622024 | tf_op jit(solution)/shard_map/ppermute | solution.py:34
  26.3 6.2 %collective-permute-start.4 = (bf16[136,1024]{1,0:T(8,128)(2,1)S(1)}, bf16[136,1024]{1,0:T(8,128)(2,1)S(1)}, u32[]{:S(2)}, u32[]{:S(2)}) collective-permute-start(bf16[136,1024]{1,0:T(8,128)(2,1)S(1)} %shard_map.102.after.t0), channel_id=1, source_target_pairs={{0,112},{8,24},{16,0},{24,40},{32,16},{40,56},{48,32},{56,72},{64,... | collective-permute-start | bytes 835592 | tf_op jit(solution)/shard_map/ppermute | solution.py:34
  34.4 4.3 %collective-permute-done.4.t2 = bf16[136,1024]{1,0:T(8,128)(2,1)S(1)} collective-permute-done((bf16[136,1024]{1,0:T(8,128)(2,1)S(1)}, bf16[136,1024]{1,0:T(8,128)(2,1)S(1)}, u32[]{:S(2)}, u32[]{:S(2)}) %collective-permute-start.4) | collective-permute-done | bytes 278560 | tf_op jit(solution)/shard_map/ppermute | solution.py:34
  53.6 4.7 %collective-permute-done.9.t4 = bf16[136,1024]{1,0:T(8,128)(2,1)} collective-permute-done((bf16[136,1024]{1,0:T(8,128)(2,1)S(1)}, bf16[136,1024]{1,0:T(8,128)(2,1)}, u32[]{:S(2)}, u32[]{:S(2)}) %collective-permute-start.9) | collective-permute-done | bytes 278560 | tf_op jit(solution)/shard_map/ppermute | solution.py:34
  60.2 3.9 %collective-permute-start.8 = (bf16[136,1024]{1,0:T(8,128)(2,1)}, bf16[136,1024]{1,0:T(8,128)(2,1)}, u32[]{:S(2)}, u32[]{:S(2)}) collective-permute-start(bf16[136,1024]{1,0:T(8,128)(2,1)} %collective-permute-done.7.t5), channel_id=1, source_target_pairs={{0,16},{8,120},{16,32},{24,8},{32,48},{40,24},{48,64},{56,40},{64,... | collective-permute-start | bytes 835592 | tf_op jit(solution)/shard_map/ppermute | solution.py:34
  64.2 5.7 %collective-permute-done.10.t6 = bf16[136,1024]{1,0:T(8,128)(2,1)} collective-permute-done((bf16[136,1024]{1,0:T(8,128)(2,1)}, bf16[136,1024]{1,0:T(8,128)(2,1)}, u32[]{:S(2)}, u32[]{:S(2)}) %collective-permute-start.10) | collective-permute-done | bytes 278560 | tf_op jit(solution)/shard_map/ppermute | solution.py:34
  71.1 4.5 %shard_map.105 = (f32[112,128]{1,0:T(8,128)S(1)}, s32[112,128]{1,0:T(8,128)S(1)}, bf16[896,1024]{1,0:T(8,128)(2,1)S(1)}) custom-call(s32[3]{0:T(128)S(1)} %pad_add_fusion.pos, bf16[512,1024]{1,0:T(8,128)(2,1)S(1)} %get-tuple-element.34.own, bf16[512,1024]{1,0:T(8,128)(2,1)} %collective-permute-done.6.other, bf16[512,1024]{1,0:T(8,128)(2,1)S(1)} %copy-done.14, ...), custom_call_target="tpu_custom_call" | custom-call | tf_op jit(solution)/shard_map/pallas_call | solution.py:38
  75.6 3.9 %shard_map.106 = (bf16[8,64,128]{2,1,0:T(8,128)(2,1)}, s32[128,128]{1,0:T(8,128)S(1)}, s32[64,128]{1,0:T(8,128)S(1)}) custom-call(s32[3]{0:T(128)S(1)} %pad_add_fusion.pos, bf16[512,1024]{1,0:T(8,128)(2,1)S(1)} %get-tuple-element.34.own, bf16[512,1024]{1,0:T(8,128)(2,1)} %collective-permute-done.6.other, bf16[136,1024]{1,0:T(8,128)(2,1)} %collective-permute-done.8.t7.last, ...), custom_call_target="tpu_custom_call" | custom-call | tf_op jit(solution)/shard_map/pallas_call | solution.py:38
  79.5 7.1 %all-to-all-start = ((bf16[8,64,128]{2,1,0:T(8,128)(2,1)}), bf16[8,64,128]{2,1,0:T(8,128)(2,1)S(1)}, u32[]{:S(2)}, u32[]{:S(2)}) async-start(bf16[8,64,128]{2,1,0:T(8,128)(2,1)} %get-tuple-element.40), calls=%async_computation | async-start | bytes 262144 | tf_op jit(solution)/shard_map/all_to_all | solution.py:447
  86.7 9.1 %all-to-all-done.got = bf16[8,64,128]{2,1,0:T(8,128)(2,1)S(1)} async-done(((bf16[8,64,128]{2,1,0:T(8,128)(2,1)}), bf16[8,64,128]{2,1,0:T(8,128)(2,1)S(1)}, u32[]{:S(2)}, u32[]{:S(2)}) %all-to-all-start) | async-done | bytes 131104 | tf_op jit(solution)/shard_map/all_to_all | solution.py:447
  100.8 5.1 %collective-permute-start.16 = (bf16[128,1024]{1,0:T(8,128)(2,1)S(1)}, bf16[128,1024]{1,0:T(8,128)(2,1)S(1)}, u32[]{:S(2)}, u32[]{:S(2)}) collective-permute-start(bf16[128,1024]{1,0:T(8,128)(2,1)S(1)} %get-tuple-element.52), channel_id=1, source_target_pairs={{0,112},{8,24},{16,0},{24,40},{32,16},{40,56},{48,32},{56,72},{64,... | collective-permute-start | bytes 786440 | tf_op jit(solution)/shard_map/ppermute | solution.py:34
  110.5 5.1 %collective-permute-start.17 = (bf16[128,1024]{1,0:T(8,128)(2,1)S(1)}, bf16[128,1024]{1,0:T(8,128)(2,1)S(1)}, u32[]{:S(2)}, u32[]{:S(2)}) collective-permute-start(bf16[128,1024]{1,0:T(8,128)(2,1)S(1)} %add_convert_fusion.11), channel_id=1, source_target_pairs={{0,112},{8,24},{16,0},{24,40},{32,16},{40,56},{48,32},{56,72},{64,... | collective-permute-start | bytes 786440 | tf_op jit(solution)/shard_map/ppermute | solution.py:34
  120.0 5.5 %collective-permute-start.18 = (bf16[128,1024]{1,0:T(8,128)(2,1)S(1)}, bf16[128,1024]{1,0:T(8,128)(2,1)S(1)}, u32[]{:S(2)}, u32[]{:S(2)}) collective-permute-start(bf16[128,1024]{1,0:T(8,128)(2,1)S(1)} %add_convert_fusion.10), channel_id=1, source_target_pairs={{0,112},{8,24},{16,0},{24,40},{32,16},{40,56},{48,32},{56,72},{64,... | collective-permute-start | bytes 786440 | tf_op jit(solution)/shard_map/ppermute | solution.py:34
  130.9 6.4 %collective-permute-done.15 = bf16[128,1024]{1,0:T(8,128)(2,1)S(1)} collective-permute-done((bf16[128,1024]{1,0:T(8,128)(2,1)S(1)}, bf16[128,1024]{1,0:T(8,128)(2,1)S(1)}, u32[]{:S(2)}, u32[]{:S(2)}) %collective-permute-start.15) | collective-permute-done | bytes 262176 | tf_op jit(solution)/shard_map/ppermute | solution.py:34
  139.3 5.1 %collective-permute-start.20 = (bf16[128,1024]{1,0:T(8,128)(2,1)S(1)}, bf16[128,1024]{1,0:T(8,128)(2,1)S(1)}, u32[]{:S(2)}, u32[]{:S(2)}) collective-permute-start(bf16[128,1024]{1,0:T(8,128)(2,1)S(1)} %subtract_convert_fusion.refs_0_), channel_id=1, source_target_pairs={{0,112},{8,24},{16,0},{24,40},{32,16},{40,56},{48,32},{56,72},{64,... | collective-permute-start | bytes 786440 | tf_op jit(solution)/shard_map/ppermute | solution.py:34
  144.5 4.7 %collective-permute-done.19.refs_1_ = bf16[128,1024]{1,0:T(8,128)(2,1)S(1)} collective-permute-done((bf16[128,1024]{1,0:T(8,128)(2,1)S(1)}, bf16[128,1024]{1,0:T(8,128)(2,1)S(1)}, u32[]{:S(2)}, u32[]{:S(2)}) %collective-permute-start.19) | collective-permute-done | bytes 262176 | tf_op jit(solution)/shard_map/ppermute | solution.py:34
  151.1 5.2 %collective-permute-start.22 = (bf16[128,1024]{1,0:T(8,128)(2,1)S(1)}, bf16[128,1024]{1,0:T(8,128)(2,1)S(1)}, u32[]{:S(2)}, u32[]{:S(2)}) collective-permute-start(bf16[128,1024]{1,0:T(8,128)(2,1)S(1)} %collective-permute-done.20.refs_2_), channel_id=1, source_target_pairs={{0,112},{8,24},{16,0},{24,40},{32,16},{40,56},{48,32},{56,72},{64,... | collective-permute-start | bytes 786440 | tf_op jit(solution)/shard_map/ppermute | solution.py:34
  156.3 3.8 %collective-permute-done.21.refs_3_ = bf16[128,1024]{1,0:T(8,128)(2,1)S(1)} collective-permute-done((bf16[128,1024]{1,0:T(8,128)(2,1)S(1)}, bf16[128,1024]{1,0:T(8,128)(2,1)S(1)}, u32[]{:S(2)}, u32[]{:S(2)}) %collective-permute-start.21) | collective-permute-done | bytes 262176 | tf_op jit(solution)/shard_map/ppermute | solution.py:34
  162.3 5.6 %collective-permute-start.24 = (bf16[128,1024]{1,0:T(8,128)(2,1)S(1)}, bf16[128,1024]{1,0:T(8,128)(2,1)S(1)}, u32[]{:S(2)}, u32[]{:S(2)}) collective-permute-start(bf16[128,1024]{1,0:T(8,128)(2,1)S(1)} %collective-permute-done.22.refs_4_), channel_id=1, source_target_pairs={{0,112},{8,24},{16,0},{24,40},{32,16},{40,56},{48,32},{56,72},{64,... | collective-permute-start | bytes 786440 | tf_op jit(solution)/shard_map/ppermute | solution.py:34
  174.8 4.2 %collective-permute-done.25.refs_0_.last = bf16[128,1024]{1,0:T(8,128)(2,1)S(1)} collective-permute-done((bf16[128,1024]{1,0:T(8,128)(2,1)S(1)}, bf16[128,1024]{1,0:T(8,128)(2,1)S(1)}, u32[]{:S(2)}, u32[]{:S(2)}) %collective-permute-start.25) | collective-permute-done | bytes 262176 | tf_op jit(solution)/shard_map/ppermute | solution.py:34
  207.0 4.5 %collective-permute-start.28 = (bf16[136,1024]{1,0:T(8,128)(2,1)S(1)}, bf16[136,1024]{1,0:T(8,128)(2,1)S(1)}, u32[]{:S(2)}, u32[]{:S(2)}) collective-permute-start(bf16[136,1024]{1,0:T(8,128)(2,1)S(1)} %get-tuple-element.62), channel_id=1, source_target_pairs={{0,128},{8,392},{16,144},{24,408},{32,160},{40,424},{48,176},{56,4... | collective-permute-start | bytes 835592 | tf_op jit(solution)/shard_map/ppermute | solution.py:34
  214.6 5.1 %collective-permute-start.33 = (bf16[128,1024]{1,0:T(8,128)(2,1)S(1)}, bf16[128,1024]{1,0:T(8,128)(2,1)S(1)}, u32[]{:S(2)}, u32[]{:S(2)}) collective-permute-start(bf16[128,1024]{1,0:T(8,128)(2,1)S(1)} %add_convert_fusion.5), channel_id=1, source_target_pairs={{0,128},{8,392},{16,144},{24,408},{32,160},{40,424},{48,176},{56,4... | collective-permute-start | bytes 786440 | tf_op jit(solution)/shard_map/ppermute | solution.py:34
  221.8 5.1 %collective-permute-start.29 = (bf16[136,1024]{1,0:T(8,128)(2,1)S(1)}, bf16[136,1024]{1,0:T(8,128)(2,1)S(1)}, u32[]{:S(2)}, u32[]{:S(2)}) collective-permute-start(bf16[136,1024]{1,0:T(8,128)(2,1)S(1)} %fusion), channel_id=1, source_target_pairs={{0,128},{8,392},{16,144},{24,408},{32,160},{40,424},{48,176},{56,4... | collective-permute-start | bytes 835592 | tf_op jit(solution)/shard_map/ppermute | solution.py:34
  (119 shorter events, 102.1 us)
Async XLA Ops:
  6.1 14.6 %collective-permute-start = (bf16[264,1024]{1,0:T(8,128)(2,1)S(1)}, bf16[264,1024]{1,0:T(8,128)(2,1)S(1)}, u32[]{:S(2)}, u32[]{:S(2)}) collective-permute-start(bf16[264,1024]{1,0:T(8,128)(2,1)S(1)} %get-tuple-element.33.c0), channel_id=1, source_target_pairs={{0,128},{8,392},{16,144},{24,408},{32,160},{40,424},{48,176},{56,4... | collective-permute-start | bytes 1622024 | tf_op jit(solution)/shard_map/ppermute | solution.py:34
  13.8 18.7 %collective-permute-start.3 = (bf16[136,1024]{1,0:T(8,128)(2,1)S(1)}, bf16[136,1024]{1,0:T(8,128)(2,1)S(1)}, u32[]{:S(2)}, u32[]{:S(2)}) collective-permute-start(bf16[136,1024]{1,0:T(8,128)(2,1)S(1)} %shard_map.102.after.t0), channel_id=1, source_target_pairs={{0,16},{8,120},{16,32},{24,8},{32,48},{40,24},{48,64},{56,40},{64,... | collective-permute-start | bytes 835592 | tf_op jit(solution)/shard_map/ppermute | solution.py:34
  15.8 23.0 %collective-permute-start.1 = (bf16[264,1024]{1,0:T(8,128)(2,1)S(1)}, bf16[264,1024]{1,0:T(8,128)(2,1)S(1)}, u32[]{:S(2)}, u32[]{:S(2)}) collective-permute-start(bf16[264,1024]{1,0:T(8,128)(2,1)S(1)} %get-tuple-element.33.c0), channel_id=1, source_target_pairs={{0,384},{8,136},{16,400},{24,152},{32,416},{40,168},{48,432},{56,1... | collective-permute-start | bytes 1622024 | tf_op jit(solution)/shard_map/ppermute | solution.py:34
  20.7 21.5 %collective-permute-start.2 = (bf16[264,1024]{1,0:T(8,128)(2,1)S(1)}, bf16[264,1024]{1,0:T(8,128)(2,1)S(1)}, u32[]{:S(2)}, u32[]{:S(2)}) collective-permute-start(bf16[264,1024]{1,0:T(8,128)(2,1)S(1)} %collective-permute-done.c1), channel_id=1, source_target_pairs={{0,128},{8,392},{16,144},{24,408},{32,160},{40,424},{48,176},{56,4... | collective-permute-start | bytes 1622024 | tf_op jit(solution)/shard_map/ppermute | solution.py:34
  26.3 12.5 %collective-permute-start.4 = (bf16[136,1024]{1,0:T(8,128)(2,1)S(1)}, bf16[136,1024]{1,0:T(8,128)(2,1)S(1)}, u32[]{:S(2)}, u32[]{:S(2)}) collective-permute-start(bf16[136,1024]{1,0:T(8,128)(2,1)S(1)} %shard_map.102.after.t0), channel_id=1, source_target_pairs={{0,112},{8,24},{16,0},{24,40},{32,16},{40,56},{48,32},{56,72},{64,... | collective-permute-start | bytes 835592 | tf_op jit(solution)/shard_map/ppermute | solution.py:34
  43.4 26.5 %collective-permute-start.6 = (bf16[512,1024]{1,0:T(8,128)(2,1)S(1)}, bf16[512,1024]{1,0:T(8,128)(2,1)}, u32[]{:S(2)}, u32[]{:S(2)}) collective-permute-start(bf16[512,1024]{1,0:T(8,128)(2,1)S(1)} %get-tuple-element.34.own), channel_id=1, source_target_pairs={{0,8},{8,0},{16,24},{24,16},{32,40},{40,32},{48,56},{56,48},{64,72... | collective-permute-start | bytes 3145736 | tf_op jit(solution)/shard_map/ppermute | solution.py:34
  45.3 41.3 %collective-permute-start.11 = (bf16[544,1024]{1,0:T(8,128)(2,1)S(1)}, bf16[544,1024]{1,0:T(8,128)(2,1)S(1)}, u32[]{:S(2)}, u32[]{:S(2)}) collective-permute-start(bf16[544,1024]{1,0:T(8,128)(2,1)S(1)} %get-tuple-element.41.own), channel_id=1, source_target_pairs={{0,8},{8,0},{16,24},{24,16},{32,40},{40,32},{48,56},{56,48},{64,72... | collective-permute-start | bytes 3342344 | tf_op jit(solution)/shard_map/ppermute | solution.py:34
  47.7 10.6 %collective-permute-start.9 = (bf16[136,1024]{1,0:T(8,128)(2,1)S(1)}, bf16[136,1024]{1,0:T(8,128)(2,1)}, u32[]{:S(2)}, u32[]{:S(2)}) collective-permute-start(bf16[136,1024]{1,0:T(8,128)(2,1)S(1)} %collective-permute-done.4.t2), channel_id=1, source_target_pairs={{0,112},{8,24},{16,0},{24,40},{32,16},{40,56},{48,32},{56,72},{64,... | collective-permute-start | bytes 835592 | tf_op jit(solution)/shard_map/ppermute | solution.py:34
  58.3 11.6 %collective-permute-start.10 = (bf16[136,1024]{1,0:T(8,128)(2,1)}, bf16[136,1024]{1,0:T(8,128)(2,1)}, u32[]{:S(2)}, u32[]{:S(2)}) collective-permute-start(bf16[136,1024]{1,0:T(8,128)(2,1)} %collective-permute-done.9.t4), channel_id=1, source_target_pairs={{0,112},{8,24},{16,0},{24,40},{32,16},{40,56},{48,32},{56,72},{64,... | collective-permute-start | bytes 835592 | tf_op jit(solution)/shard_map/ppermute | solution.py:34
  60.2 15.4 %collective-permute-start.8 = (bf16[136,1024]{1,0:T(8,128)(2,1)}, bf16[136,1024]{1,0:T(8,128)(2,1)}, u32[]{:S(2)}, u32[]{:S(2)}) collective-permute-start(bf16[136,1024]{1,0:T(8,128)(2,1)} %collective-permute-done.7.t5), channel_id=1, source_target_pairs={{0,16},{8,120},{16,32},{24,8},{32,48},{40,24},{48,64},{56,40},{64,... | collective-permute-start | bytes 835592 | tf_op jit(solution)/shard_map/ppermute | solution.py:34
  79.5 16.2 %all-to-all-start = ((bf16[8,64,128]{2,1,0:T(8,128)(2,1)}), bf16[8,64,128]{2,1,0:T(8,128)(2,1)S(1)}, u32[]{:S(2)}, u32[]{:S(2)}) async-start(bf16[8,64,128]{2,1,0:T(8,128)(2,1)} %get-tuple-element.40), calls=%async_computation | async-start | bytes 262144 | tf_op jit(solution)/shard_map/all_to_all | solution.py:447
  120.0 10.9 %collective-permute-start.18 = (bf16[128,1024]{1,0:T(8,128)(2,1)S(1)}, bf16[128,1024]{1,0:T(8,128)(2,1)S(1)}, u32[]{:S(2)}, u32[]{:S(2)}) collective-permute-start(bf16[128,1024]{1,0:T(8,128)(2,1)S(1)} %add_convert_fusion.10), channel_id=1, source_target_pairs={{0,112},{8,24},{16,0},{24,40},{32,16},{40,56},{48,32},{56,72},{64,... | collective-permute-start | bytes 786440 | tf_op jit(solution)/shard_map/ppermute | solution.py:34
  125.6 11.6 %collective-permute-start.15 = (bf16[128,1024]{1,0:T(8,128)(2,1)S(1)}, bf16[128,1024]{1,0:T(8,128)(2,1)S(1)}, u32[]{:S(2)}, u32[]{:S(2)}) collective-permute-start(bf16[128,1024]{1,0:T(8,128)(2,1)S(1)} %add_convert_fusion.12), channel_id=1, source_target_pairs={{0,16},{8,120},{16,32},{24,8},{32,48},{40,24},{48,64},{56,40},{64,... | collective-permute-start | bytes 786440 | tf_op jit(solution)/shard_map/ppermute | solution.py:34
  137.4 11.8 %collective-permute-start.19 = (bf16[128,1024]{1,0:T(8,128)(2,1)S(1)}, bf16[128,1024]{1,0:T(8,128)(2,1)S(1)}, u32[]{:S(2)}, u32[]{:S(2)}) collective-permute-start(bf16[128,1024]{1,0:T(8,128)(2,1)S(1)} %subtract_convert_fusion.refs_0_), channel_id=1, source_target_pairs={{0,16},{8,120},{16,32},{24,8},{32,48},{40,24},{48,64},{56,40},{64,... | collective-permute-start | bytes 786440 | tf_op jit(solution)/shard_map/ppermute | solution.py:34
  139.3 11.8 %collective-permute-start.20 = (bf16[128,1024]{1,0:T(8,128)(2,1)S(1)}, bf16[128,1024]{1,0:T(8,128)(2,1)S(1)}, u32[]{:S(2)}, u32[]{:S(2)}) collective-permute-start(bf16[128,1024]{1,0:T(8,128)(2,1)S(1)} %subtract_convert_fusion.refs_0_), channel_id=1, source_target_pairs={{0,112},{8,24},{16,0},{24,40},{32,16},{40,56},{48,32},{56,72},{64,... | collective-permute-start | bytes 786440 | tf_op jit(solution)/shard_map/ppermute | solution.py:34
  149.2 10.9 %collective-permute-start.21 = (bf16[128,1024]{1,0:T(8,128)(2,1)S(1)}, bf16[128,1024]{1,0:T(8,128)(2,1)S(1)}, u32[]{:S(2)}, u32[]{:S(2)}) collective-permute-start(bf16[128,1024]{1,0:T(8,128)(2,1)S(1)} %collective-permute-done.19.refs_1_), channel_id=1, source_target_pairs={{0,16},{8,120},{16,32},{24,8},{32,48},{40,24},{48,64},{56,40},{64,... | collective-permute-start | bytes 786440 | tf_op jit(solution)/shard_map/ppermute | solution.py:34
  151.1 11.2 %collective-permute-start.22 = (bf16[128,1024]{1,0:T(8,128)(2,1)S(1)}, bf16[128,1024]{1,0:T(8,128)(2,1)S(1)}, u32[]{:S(2)}, u32[]{:S(2)}) collective-permute-start(bf16[128,1024]{1,0:T(8,128)(2,1)S(1)} %collective-permute-done.20.refs_2_), channel_id=1, source_target_pairs={{0,112},{8,24},{16,0},{24,40},{32,16},{40,56},{48,32},{56,72},{64,... | collective-permute-start | bytes 786440 | tf_op jit(solution)/shard_map/ppermute | solution.py:34
  181.0 12.4 %all-to-all-start.1 = ((bf16[8,64,128]{2,1,0:T(8,128)(2,1)}), bf16[8,64,128]{2,1,0:T(8,128)(2,1)S(1)}, u32[]{:S(2)}, u32[]{:S(2)}) async-start(bf16[8,64,128]{2,1,0:T(8,128)(2,1)} %shard_map.114.after), calls=%async_computation.1 | async-start | bytes 262144 | tf_op jit(solution)/shard_map/all_to_all | solution.py:488
  188.8 13.5 %collective-permute-start.30 = (bf16[512,1024]{1,0:T(8,128)(2,1)S(1)}, bf16[512,1024]{1,0:T(8,128)(2,1)}, u32[]{:S(2)}, u32[]{:S(2)}) collective-permute-start(bf16[512,1024]{1,0:T(8,128)(2,1)S(1)} %shard_map.118.after), channel_id=1, source_target_pairs={{0,8},{8,0},{16,24},{24,16},{32,40},{40,32},{48,56},{56,48},{64,72... | collective-permute-start | bytes 3145736 | tf_op jit(solution)/shard_map/ppermute | solution.py:34
  195.9 10.8 %collective-permute-start.26 = (bf16[4,136,1024]{2,1,0:T(8,128)(2,1)S(1)}, bf16[4,136,1024]{2,1,0:T(8,128)(2,1)S(1)}, u32[]{:S(2)}, u32[]{:S(2)}) collective-permute-start(bf16[4,136,1024]{2,1,0:T(8,128)(2,1)S(1)} %shard_map.116), channel_id=1, source_target_pairs={{0,8},{8,0},{16,24},{24,16},{32,40},{40,32},{48,56},{56,48},{64,72... | collective-permute-start | bytes 3342344 | tf_op jit(solution)/shard_map/ppermute | solution.py:34
  207.0 14.6 %collective-permute-start.28 = (bf16[136,1024]{1,0:T(8,128)(2,1)S(1)}, bf16[136,1024]{1,0:T(8,128)(2,1)S(1)}, u32[]{:S(2)}, u32[]{:S(2)}) collective-permute-start(bf16[136,1024]{1,0:T(8,128)(2,1)S(1)} %get-tuple-element.62), channel_id=1, source_target_pairs={{0,128},{8,392},{16,144},{24,408},{32,160},{40,424},{48,176},{56,4... | collective-permute-start | bytes 835592 | tf_op jit(solution)/shard_map/ppermute | solution.py:34
  211.5 16.4 %collective-permute-start.31 = (bf16[128,1024]{1,0:T(8,128)(2,1)S(1)}, bf16[128,1024]{1,0:T(8,128)(2,1)S(1)}, u32[]{:S(2)}, u32[]{:S(2)}) collective-permute-start(bf16[128,1024]{1,0:T(8,128)(2,1)S(1)} %get-tuple-element.65), channel_id=1, source_target_pairs={{0,384},{8,136},{16,400},{24,152},{32,416},{40,168},{48,432},{56,1... | collective-permute-start | bytes 786440 | tf_op jit(solution)/shard_map/ppermute | solution.py:34
  214.6 13.4 %collective-permute-start.33 = (bf16[128,1024]{1,0:T(8,128)(2,1)S(1)}, bf16[128,1024]{1,0:T(8,128)(2,1)S(1)}, u32[]{:S(2)}, u32[]{:S(2)}) collective-permute-start(bf16[128,1024]{1,0:T(8,128)(2,1)S(1)} %add_convert_fusion.5), channel_id=1, source_target_pairs={{0,128},{8,392},{16,144},{24,408},{32,160},{40,424},{48,176},{56,4... | collective-permute-start | bytes 786440 | tf_op jit(solution)/shard_map/ppermute | solution.py:34
  219.7 10.9 %collective-permute-start.27 = (bf16[136,1024]{1,0:T(8,128)(2,1)S(1)}, bf16[136,1024]{1,0:T(8,128)(2,1)S(1)}, u32[]{:S(2)}, u32[]{:S(2)}) collective-permute-start(bf16[136,1024]{1,0:T(8,128)(2,1)S(1)} %get-tuple-element.63), channel_id=1, source_target_pairs={{0,384},{8,136},{16,400},{24,152},{32,416},{40,168},{48,432},{56,1... | collective-permute-start | bytes 835592 | tf_op jit(solution)/shard_map/ppermute | solution.py:34
  (31 other events, 230.0 us)

commit v6 on v5

--- a/solution.py
+++ b/solution.py
@@ -151,20 +151,12 @@
     )
 
 
-def back_body(first, n):
-    def body(own, other, where, *refs):
-        chunks, (picks, *rows) = refs[:n], refs[n:]
-        toks = [c[...] for c in chunks]
-        places = []
-        for i in range(n):
-            at = 16 * (first + i)
-            places.append((where[at : at + 8, :], where[at + 8 : at + 16, :]))
-        tok = toks[0] if n == 1 else jnp.concatenate(toks, axis=0)
-        for out in rows:
-            out[...] = tok
-        pick_into(picks, (own, other), tok, places)
-
-    return body
+def back_body(own, other, where, *refs):
+    chunks, (picks, rows) = refs[:7], refs[7:]
+    places = [(where[16 * i : 16 * i + 8, :], where[16 * i + 8 : 16 * i + 16, :]) for i in range(7)]
+    tok = jnp.concatenate([c[...] for c in chunks], axis=0)
+    rows[...] = tok
+    pick_into(picks, (own, other), tok, places)
 
 
 def halves_of(packed):
@@ -226,7 +218,8 @@
         out[d, 48:64, :] = low[16 * d : 16 * d + 16, :]
 
 
-def resend_body(p0, p1, where, ranks, rows, out):
+def resend_body(own, other, where, t7, p0, ranks, rows, out, p1):
+    pick_into(p1, (own, other), t7[...], [(where[112:120, :], where[120:128, :])])
     picks = jnp.concatenate([p0[...], p1[...]], axis=0)
     live = halves_of(where[...])[0] >= 0
     sent = squeeze(picks, live, ranks[...]).astype(BF)
@@ -329,6 +322,11 @@
         exts[8 * i : 8 * i + 8, :] = ref[R : R + 8, 0:384].astype(F32)
 
 
+def x_slot(pos, q, half):
+    side = 1 - 2 * pos[2] if half == 0 else 2 * pos[2] - 1
+    return (pos[0] + (0, -side, side, 2)[q] + NX) & 3
+
+
 def fitted_body(half):
     def body(at, act, after, most, last, out, rows, sem):
         copies = load_rows(most, last, rows, sem)
@@ -336,13 +334,15 @@
         table = jnp.concatenate(parts, axis=0)
         for copy in copies:
             copy.wait()
-        out[...] = (dot(table, rows[...], NN) * LOSS_GRAD).astype(BF)
+        part = (dot(table, rows[...], NN) * LOSS_GRAD).astype(BF)
+        for q in range(4):
+            out[q] = part[q * R : (q + 1) * R, :]
 
     return body
 
 
 def encgrad_body(half):
-    def body(got, at, ranks, most, last, *rest):
+    def body(pos, got, at, ranks, most, last, *rest):
         out, (rows, sem) = rest[0], rest[-2:]
         copies = load_rows(most, last, rows, sem)
         grad = jnp.where(at[...] >= 0, unsqueeze(total(got, 0, 32), ranks[...]) * LOSS_GRAD, 0.0)
@@ -357,20 +357,21 @@
             for piece in pieces[1:]:
                 acc = acc + piece
             sums = lax.dot_general(ones, acc, NT, precision=lax.Precision.HIGHEST, preferred_element_type=F32)
-            out[q, R : R + 8, 0:128] = sums.astype(BF)
-            out[q, R : R + 8, 128:1024] = jnp.zeros((8, 896), BF)
+            slot = x_slot(pos, q, half)
+            out[slot, R : R + 8, 0:128] = sums.astype(BF)
+            out[slot, R : R + 8, 128:1024] = jnp.zeros((8, 896), BF)
             parts.append(jnp.concatenate(pieces, axis=1).astype(BF))
         table = jnp.concatenate(parts, axis=0)
         for copy in copies:
             copy.wait()
         part = dot(table, rows[...], NN).astype(BF)
         for q in range(4):
-            out[q, 0:R, :] = part[q * R : (q + 1) * R, :]
+            out[x_slot(pos, q, half), 0:R, :] = part[q * R : (q + 1) * R, :]
 
     return body
 
 
-def penalty_body(count, gram_ref, decoder, out):
+def penalty_body(count, gram_ref, decoder, a, b, c, out):
     gram = gram_ref[...]
     row, col = rows_iota((R, R)), lanes_iota((R, R))
     diagonal = row == col
@@ -385,13 +386,20 @@
     spread = jnp.sum(coupled * cosine, axis=1, keepdims=True)
     diag_term = jnp.where(diagonal, spread / (norm_c * norm_c), 0.0)
     weights = (4.0 * COHERENCE * (coupled / pair - diag_term)).astype(BF)
-    out[...] = dot(weights, decoder[...], NN)
-
-
-def finish_body(a, b, c, out, bias):
-    total_of = lambda lo, hi, n: a[lo:hi, 0:n].astype(F32) + b[lo:hi, 0:n].astype(F32) + c[lo:hi, 0:n].astype(F32)
-    out[...] = total_of(0, R, 1024).astype(BF)
-    bias[...] = total_of(R, R + 8, R)
+    fit = (a[...].astype(F32) + b[...].astype(F32)) + c[...].astype(F32)
+    out[...] = (fit + dot(weights, decoder[...], NN)).astype(BF)
+
+
+def sum_of(got, lo, hi, n):
+    acc = got[0, lo:hi, 0:n].astype(F32)
+    for i in range(1, NX):
+        acc = acc + got[i, lo:hi, 0:n].astype(F32)
+    return acc
+
+
+def finish_body(got, out, bias):
+    out[...] = sum_of(got, 0, R, 1024).astype(BF)
+    bias[...] = sum_of(got, R, R + 8, R)
 
 
 def add(a, b):
@@ -405,11 +413,16 @@
     return [own, f1, b1, f2, b2, f3, b3, move(f3, dz=1)]
 
 
-def scatter_x(own, theirs):
+def ring_x(own, theirs):
     blocks = [add(own[i], theirs[i]) for i in range(4)]
     far = move(blocks[3], dx=1)
     prev = move(blocks[1], dx=-1)
     return blocks[0], prev, move(add(blocks[2], far), dx=1)
+
+
+def scatter_x(own, theirs):
+    groups = [[_place(x, z, c) for x in range(NX)] for z in range(NZ) for c in range(NC)]
+    return lax.all_to_all(add(own, theirs), "atoms", split_axis=0, concat_axis=0, tiled=True, axis_index_groups=groups)
 
 
 def per_device(tokens, dec_bias, encoder, enc_bias, decoder, atom_ids, block_count):
@@ -474,48 +487,46 @@
 
     res = gather_z(residual)
 
-    def back(chunks, first):
-        n = len(chunks)
-        rows = [sds((n * R, 1024), BF)] if n > 1 else []
-        return call(
-            back_body(first, n), (sds((16 * n, 128), F32), *rows),
-            dec_own, dec_other, where, *chunks, specs=whole(3 + n),
-        )
-
-    back_most, res_most = back(res[0:7], 0)
-    (back_last,) = back(res[7:8], 7)
-    out2 = call(resend_body, sds((NY, 64, 128), BF), back_most, back_last, where, ranks, gram_rows, specs=whole(5))
+    back_most, res_most = call(
+        back_body, (sds((112, 128), F32), sds((7 * R, 1024), BF)), dec_own, dec_other, where, *res[0:7],
+        specs=whole(10),
+    )
+    out2 = call(
+        resend_body, sds((NY, 64, 128), BF), dec_own, dec_other, where, res[7], back_most, ranks, gram_rows,
+        specs=whole(7), scratch=[pltpu.VMEM((16, 128), F32)],
+    )
     got2 = lax.all_to_all(out2, "width", split_axis=0, concat_axis=0, tiled=True)
 
     scratch = [pltpu.VMEM((8 * R, 1024), BF), pltpu.SemaphoreType.DMA((2,))]
 
     def fitted(half, after):
         return call(
-            fitted_body(half), sds((4 * R, 1024), BF), where, act, after, res_most, res[7],
+            fitted_body(half), sds((4, R, 1024), BF), where, act, after, res_most, res[7],
             specs=whole(2) + [ANY_SPEC] * 3, scratch=scratch,
         )
 
     fit_other = fitted(1, out2)
     fit_theirs = move(fit_other, dc=1)
     fit_own = fitted(0, fit_other)
-    fit = scatter_x(fit_own.reshape(4, R, 1024), fit_theirs.reshape(4, R, 1024))
+    fit = ring_x(fit_own, fit_theirs)
 
     def encgrad(half):
         outs = [sds((4, R + 8, 1024), BF)] + ([sds((R, R), F32)] if half == 0 else [])
         return call(
-            encgrad_body(half), tuple(outs), got2, where, ranks, tok_most, tok[7],
-            specs=whole(3) + [ANY_SPEC] * 2, scratch=scratch,
+            encgrad_body(half), tuple(outs), pos, got2, where, ranks, tok_most, tok[7],
+            specs=[SMEM_SPEC] + whole(3) + [ANY_SPEC] * 2, scratch=scratch,
         )
 
     (eg_other,) = encgrad(1)
     eg_theirs = move(eg_other, dc=1)
     eg_own, gram = encgrad(0)
     eg = scatter_x(eg_own, eg_theirs)
-    encoder_grad, bias_grad = call(finish_body, (sds((R, 1024), BF), sds((8, R), F32)), *eg, specs=whole(3))
+    encoder_grad, bias_grad = call(finish_body, (sds((R, 1024), BF), sds((8, R), F32)), eg, specs=whole(1))
     bias_grad = bias_grad[0]
 
-    penalty = call(penalty_body, sds((R, 1024), F32), block_count, gram, decoder, specs=[SMEM_SPEC] + whole(2))
-    decoder_grad = (fit[0].astype(F32) + fit[1].astype(F32) + fit[2].astype(F32) + penalty).astype(BF)
+    decoder_grad = call(
+        penalty_body, sds((R, 1024), BF), block_count, gram, decoder, *fit, specs=[SMEM_SPEC] + whole(5)
+    )
     return (residual, encoder_grad, decoder_grad, bias_grad)
 
 

time: 236 us -> 251 us (1.064)
  blocking collectives: 0 us -> 11.5 us
  waiting for transfers between devices: 58 us -> 69.5 us
  starting transfers between devices: 125 us -> 116 us
    ppermute x34 -> x31, waiting for transfers between devices: 46.3 us -> 60.4 us  [move(): return lax.ppermute(value, 'atoms', _perm(**shift))]
    all_to_all x0 -> x1, blocking collectives: none -> 11.5 us  [per_device(): lax.all_to_all(out2, 'width', split_axis=0, concat_axis=0, tiled=True)]
    ppermute x34 -> x31, starting transfers between devices: 114 us -> 103 us  [move(): return lax.ppermute(value, 'atoms', _perm(**shift))]
    all_to_all x1, waiting for transfers between devices: 2.65 us -> 0.01 us  [scatter_x(): lax.all_to_all(add(own, theirs), 'atoms', split_axis=0, concat_axis=0, ti...]
    all_to_all x1, starting transfers between devices: 3.37 us -> 5.95 us  [scatter_x(): lax.all_to_all(add(own, theirs), 'atoms', split_axis=0, concat_axis=0, ti...]
    unnamed x39 -> x45, local copies, waits for them, and re-layouts: 9.72 us -> 11 us
    pallas_call x19 -> x18, Pallas kernels: 32.2 us -> 32.7 us  [call(): pl.pallas_call(body, out_shape=outs, in_specs=specs, scratch_shapes=scrat...]
  transfers between devices with their start and end apart: 36 -> 33, of which waited for: 19 -> 18; matrix products, arithmetic and copies ran while one was open for 2% -> 2% of each run, Pallas kernels for 12% -> 10%
where the time goes in v6:
time: 251 us; the launch traced here: 247 us
  starting transfers between devices  116 us (46%)
  waiting for transfers between devices  69.5 us (28%)
  Pallas kernels  32.7 us (13%)
  local copies, waits for them, and re-layouts  11.5 us (5%)
  blocking collectives  11.5 us (5%)
  other arithmetic  4.52 us (2%)
    ppermute x31, starting transfers between devices, move(): return lax.ppermute(value, 'atoms', _perm(**shift))  103 us
    ppermute x31, waiting for transfers between devices, move(): return lax.ppermute(value, 'atoms', _perm(**shift))  60.4 us
    pallas_call x18, Pallas kernels, call(): pl.pallas_call(body, out_shape=outs, in_specs=specs, scratch_shapes=scrat...  32.7 us
    all_to_all x1, blocking collectives, per_device(): lax.all_to_all(out2, 'width', split_axis=0, concat_axis=0, tiled=True)  11.5 us
    unnamed x45, local copies, waits for them, and re-layouts  11 us
    all_to_all x1, waiting for transfers between devices, per_device(): got = lax.all_to_all(out, 'width', split_axis=0, concat_axis=0, tiled=True)  9.07 us
    all_to_all x1, starting transfers between devices, per_device(): got = lax.all_to_all(out, 'width', split_axis=0, concat_axis=0, tiled=True)  7.12 us
    all_to_all x1, starting transfers between devices, scatter_x(): lax.all_to_all(add(own, theirs), 'atoms', split_axis=0, concat_axis=0, ti...  5.95 us
  transfers between devices with their start and end apart: 33, of which 18 were waited for; matrix products, arithmetic and copies ran while one was open for 2% of the time, Pallas kernels for 10%

profile of v6, /device:TPU:6, one launch (start us, length us, event | category | flops | bytes accessed | tf_op | source)
XLA Modules:
  0.0 247.4 jit_solution(4944827698701746135)
XLA Ops:
  6.7 7.7 %collective-permute-start = (bf16[264,1024]{1,0:T(8,128)(2,1)S(1)}, bf16[264,1024]{1,0:T(8,128)(2,1)S(1)}, u32[]{:S(2)}, u32[]{:S(2)}) collective-permute-start(bf16[264,1024]{1,0:T(8,128)(2,1)S(1)} %get-tuple-element.33.c0), channel_id=1, source_target_pairs={{0,128},{8,392},{16,144},{24,408},{32,160},{40,424},{48,176},{56,4... | collective-permute-start | bytes 1622024 | tf_op jit(solution)/shard_map/ppermute | solution.py:34
  21.3 5.6 %collective-permute-start.2 = (bf16[264,1024]{1,0:T(8,128)(2,1)S(1)}, bf16[264,1024]{1,0:T(8,128)(2,1)S(1)}, u32[]{:S(2)}, u32[]{:S(2)}) collective-permute-start(bf16[264,1024]{1,0:T(8,128)(2,1)S(1)} %collective-permute-done.c1), channel_id=1, source_target_pairs={{0,128},{8,392},{16,144},{24,408},{32,160},{40,424},{48,176},{56,4... | collective-permute-start | bytes 1622024 | tf_op jit(solution)/shard_map/ppermute | solution.py:34
  26.9 6.2 %collective-permute-start.4 = (bf16[136,1024]{1,0:T(8,128)(2,1)S(1)}, bf16[136,1024]{1,0:T(8,128)(2,1)S(1)}, u32[]{:S(2)}, u32[]{:S(2)}) collective-permute-start(bf16[136,1024]{1,0:T(8,128)(2,1)S(1)} %shard_map.102.after.t0), channel_id=1, source_target_pairs={{0,112},{8,24},{16,0},{24,40},{32,16},{40,56},{48,32},{56,72},{64,... | collective-permute-start | bytes 835592 | tf_op jit(solution)/shard_map/ppermute | solution.py:34
  35.0 4.3 %collective-permute-done.4.t2 = bf16[136,1024]{1,0:T(8,128)(2,1)S(1)} collective-permute-done((bf16[136,1024]{1,0:T(8,128)(2,1)S(1)}, bf16[136,1024]{1,0:T(8,128)(2,1)S(1)}, u32[]{:S(2)}, u32[]{:S(2)}) %collective-permute-start.4) | collective-permute-done | bytes 278560 | tf_op jit(solution)/shard_map/ppermute | solution.py:34
  54.8 4.7 %collective-permute-done.9.t4 = bf16[136,1024]{1,0:T(8,128)(2,1)} collective-permute-done((bf16[136,1024]{1,0:T(8,128)(2,1)S(1)}, bf16[136,1024]{1,0:T(8,128)(2,1)}, u32[]{:S(2)}, u32[]{:S(2)}) %collective-permute-start.9) | collective-permute-done | bytes 278560 | tf_op jit(solution)/shard_map/ppermute | solution.py:34
  61.4 3.9 %collective-permute-start.8 = (bf16[136,1024]{1,0:T(8,128)(2,1)}, bf16[136,1024]{1,0:T(8,128)(2,1)S(1)}, u32[]{:S(2)}, u32[]{:S(2)}) collective-permute-start(bf16[136,1024]{1,0:T(8,128)(2,1)} %collective-permute-done.7.t5), channel_id=1, source_target_pairs={{0,16},{8,120},{16,32},{24,8},{32,48},{40,24},{48,64},{56,40},{64,... | collective-permute-start | bytes 835592 | tf_op jit(solution)/shard_map/ppermute | solution.py:34
  65.5 5.7 %collective-permute-done.10.t6 = bf16[136,1024]{1,0:T(8,128)(2,1)} collective-permute-done((bf16[136,1024]{1,0:T(8,128)(2,1)}, bf16[136,1024]{1,0:T(8,128)(2,1)}, u32[]{:S(2)}, u32[]{:S(2)}) %collective-permute-start.10) | collective-permute-done | bytes 278560 | tf_op jit(solution)/shard_map/ppermute | solution.py:34
  73.2 4.5 %shard_map.105 = (f32[112,128]{1,0:T(8,128)S(1)}, s32[112,128]{1,0:T(8,128)S(1)}, bf16[896,1024]{1,0:T(8,128)(2,1)S(1)}) custom-call(s32[3]{0:T(128)S(1)} %pad_add_fusion.pos, bf16[512,1024]{1,0:T(8,128)(2,1)S(1)} %get-tuple-element.34.own, bf16[512,1024]{1,0:T(8,128)(2,1)} %collective-permute-done.6.other, bf16[512,1024]{1,0:T(8,128)(2,1)S(1)} %copy-done.11, ...), custom_call_target="tpu_custom_call" | custom-call | tf_op jit(solution)/shard_map/pallas_call | solution.py:38
  82.6 7.1 %all-to-all-start = ((bf16[8,64,128]{2,1,0:T(8,128)(2,1)}), bf16[8,64,128]{2,1,0:T(8,128)(2,1)S(1)}, u32[]{:S(2)}, u32[]{:S(2)}) async-start(bf16[8,64,128]{2,1,0:T(8,128)(2,1)} %get-tuple-element.40), calls=%async_computation | async-start | bytes 262144 | tf_op jit(solution)/shard_map/all_to_all | solution.py:460
  89.7 9.1 %all-to-all-done.got = bf16[8,64,128]{2,1,0:T(8,128)(2,1)S(1)} async-done(((bf16[8,64,128]{2,1,0:T(8,128)(2,1)}), bf16[8,64,128]{2,1,0:T(8,128)(2,1)S(1)}, u32[]{:S(2)}, u32[]{:S(2)}) %all-to-all-start) | async-done | bytes 131104 | tf_op jit(solution)/shard_map/all_to_all | solution.py:460
  103.9 5.1 %collective-permute-start.16 = (bf16[128,1024]{1,0:T(8,128)(2,1)S(1)}, bf16[128,1024]{1,0:T(8,128)(2,1)S(1)}, u32[]{:S(2)}, u32[]{:S(2)}) collective-permute-start(bf16[128,1024]{1,0:T(8,128)(2,1)S(1)} %get-tuple-element.52), channel_id=1, source_target_pairs={{0,112},{8,24},{16,0},{24,40},{32,16},{40,56},{48,32},{56,72},{64,... | collective-permute-start | bytes 786440 | tf_op jit(solution)/shard_map/ppermute | solution.py:34
  113.6 5.1 %collective-permute-start.17 = (bf16[128,1024]{1,0:T(8,128)(2,1)S(1)}, bf16[128,1024]{1,0:T(8,128)(2,1)S(1)}, u32[]{:S(2)}, u32[]{:S(2)}) collective-permute-start(bf16[128,1024]{1,0:T(8,128)(2,1)S(1)} %add_convert_fusion.6), channel_id=1, source_target_pairs={{0,112},{8,24},{16,0},{24,40},{32,16},{40,56},{48,32},{56,72},{64,... | collective-permute-start | bytes 786440 | tf_op jit(solution)/shard_map/ppermute | solution.py:34
  123.0 5.6 %collective-permute-start.18 = (bf16[128,1024]{1,0:T(8,128)(2,1)S(1)}, bf16[128,1024]{1,0:T(8,128)(2,1)S(1)}, u32[]{:S(2)}, u32[]{:S(2)}) collective-permute-start(bf16[128,1024]{1,0:T(8,128)(2,1)S(1)} %add_convert_fusion.5), channel_id=1, source_target_pairs={{0,112},{8,24},{16,0},{24,40},{32,16},{40,56},{48,32},{56,72},{64,... | collective-permute-start | bytes 786440 | tf_op jit(solution)/shard_map/ppermute | solution.py:34
  134.0 6.4 %collective-permute-done.15 = bf16[128,1024]{1,0:T(8,128)(2,1)S(1)} collective-permute-done((bf16[128,1024]{1,0:T(8,128)(2,1)S(1)}, bf16[128,1024]{1,0:T(8,128)(2,1)S(1)}, u32[]{:S(2)}, u32[]{:S(2)}) %collective-permute-start.15) | collective-permute-done | bytes 262176 | tf_op jit(solution)/shard_map/ppermute | solution.py:34
  142.4 5.1 %collective-permute-start.23 = (bf16[128,1024]{1,0:T(8,128)(2,1)S(1)}, bf16[128,1024]{1,0:T(8,128)(2,1)S(1)}, u32[]{:S(2)}, u32[]{:S(2)}) collective-permute-start(bf16[128,1024]{1,0:T(8,128)(2,1)S(1)} %subtract_convert_fusion.refs_0_), channel_id=1, source_target_pairs={{0,112},{8,24},{16,0},{24,40},{32,16},{40,56},{48,32},{56,72},{64,... | collective-permute-start | bytes 786440 | tf_op jit(solution)/shard_map/ppermute | solution.py:34
  147.6 4.7 %collective-permute-done.19.refs_1_ = bf16[128,1024]{1,0:T(8,128)(2,1)S(1)} collective-permute-done((bf16[128,1024]{1,0:T(8,128)(2,1)S(1)}, bf16[128,1024]{1,0:T(8,128)(2,1)S(1)}, u32[]{:S(2)}, u32[]{:S(2)}) %collective-permute-start.19) | collective-permute-done | bytes 262176 | tf_op jit(solution)/shard_map/ppermute | solution.py:34
  154.2 5.2 %collective-permute-start.24 = (bf16[128,1024]{1,0:T(8,128)(2,1)S(1)}, bf16[128,1024]{1,0:T(8,128)(2,1)S(1)}, u32[]{:S(2)}, u32[]{:S(2)}) collective-permute-start(bf16[128,1024]{1,0:T(8,128)(2,1)S(1)} %collective-permute-done.23.refs_2_), channel_id=1, source_target_pairs={{0,112},{8,24},{16,0},{24,40},{32,16},{40,56},{48,32},{56,72},{64,... | collective-permute-start | bytes 786440 | tf_op jit(solution)/shard_map/ppermute | solution.py:34
  165.4 5.6 %collective-permute-start.25 = (bf16[128,1024]{1,0:T(8,128)(2,1)S(1)}, bf16[128,1024]{1,0:T(8,128)(2,1)S(1)}, u32[]{:S(2)}, u32[]{:S(2)}) collective-permute-start(bf16[128,1024]{1,0:T(8,128)(2,1)S(1)} %collective-permute-done.24.refs_4_), channel_id=1, source_target_pairs={{0,112},{8,24},{16,0},{24,40},{32,16},{40,56},{48,32},{56,72},{64,... | collective-permute-start | bytes 786440 | tf_op jit(solution)/shard_map/ppermute | solution.py:34
  177.9 4.2 %collective-permute-done.22.t7.last = bf16[128,1024]{1,0:T(8,128)(2,1)S(1)} collective-permute-done((bf16[128,1024]{1,0:T(8,128)(2,1)S(1)}, bf16[128,1024]{1,0:T(8,128)(2,1)S(1)}, u32[]{:S(2)}, u32[]{:S(2)}) %collective-permute-start.22) | collective-permute-done | bytes 262176 | tf_op jit(solution)/shard_map/ppermute | solution.py:34
  183.4 11.5 %all_to_all.15.got = bf16[8,64,128]{2,1,0:T(8,128)(2,1)S(1)} all-to-all(bf16[8,64,128]{2,1,0:T(8,128)(2,1)S(1)} %shard_map.113.after), channel_id=1, replica_groups=mesh['atoms'=64,'width'=8] {'width'}, dimensions={0} | all-to-all | bytes 262144 | tf_op jit(solution)/shard_map/all_to_all | solution.py:498
  210.7 6.0 %all-to-all-start.2 = ((bf16[4,136,1024]{2,1,0:T(8,128)(2,1)}), bf16[4,136,1024]{2,1,0:T(8,128)(2,1)S(1)}, u32[]{:S(2)}, u32[]{:S(2)}) async-start(bf16[4,136,1024]{2,1,0:T(8,128)(2,1)} %add_convert_fusion), calls=%async_computation.2 | async-start | bytes 2228224 | tf_op jit(solution)/shard_map/all_to_all | solution.py:425
  220.1 3.9 %collective-permute-start.28 = (bf16[128,1024]{1,0:T(8,128)(2,1)S(1)}, bf16[128,1024]{1,0:T(8,128)(2,1)S(1)}, u32[]{:S(2)}, u32[]{:S(2)}) collective-permute-start(bf16[128,1024]{1,0:T(8,128)(2,1)S(1)} %get-tuple-element.63), channel_id=1, source_target_pairs={{0,384},{8,136},{16,400},{24,152},{32,416},{40,168},{48,432},{56,1... | collective-permute-start | bytes 786440 | tf_op jit(solution)/shard_map/ppermute | solution.py:34
  224.0 11.6 %collective-permute-done.29 = bf16[128,1024]{1,0:T(8,128)(2,1)S(1)} collective-permute-done((bf16[128,1024]{1,0:T(8,128)(2,1)S(1)}, bf16[128,1024]{1,0:T(8,128)(2,1)S(1)}, u32[]{:S(2)}, u32[]{:S(2)}) %collective-permute-start.29) | collective-permute-done | bytes 262176 | tf_op jit(solution)/shard_map/ppermute | solution.py:34
  236.7 3.8 %collective-permute-start.30 = (bf16[128,1024]{1,0:T(8,128)(2,1)S(1)}, bf16[128,1024]{1,0:T(8,128)(2,1)S(1)}, u32[]{:S(2)}, u32[]{:S(2)}) collective-permute-start(bf16[128,1024]{1,0:T(8,128)(2,1)S(1)} %fusion), channel_id=1, source_target_pairs={{0,128},{8,392},{16,144},{24,408},{32,160},{40,424},{48,176},{56,4... | collective-permute-start | bytes 786440 | tf_op jit(solution)/shard_map/ppermute | solution.py:34
  (117 shorter events, 103.1 us)
Async XLA Ops:
  6.7 14.6 %collective-permute-start = (bf16[264,1024]{1,0:T(8,128)(2,1)S(1)}, bf16[264,1024]{1,0:T(8,128)(2,1)S(1)}, u32[]{:S(2)}, u32[]{:S(2)}) collective-permute-start(bf16[264,1024]{1,0:T(8,128)(2,1)S(1)} %get-tuple-element.33.c0), channel_id=1, source_target_pairs={{0,128},{8,392},{16,144},{24,408},{32,160},{40,424},{48,176},{56,4... | collective-permute-start | bytes 1622024 | tf_op jit(solution)/shard_map/ppermute | solution.py:34
  14.5 18.7 %collective-permute-start.3 = (bf16[136,1024]{1,0:T(8,128)(2,1)S(1)}, bf16[136,1024]{1,0:T(8,128)(2,1)S(1)}, u32[]{:S(2)}, u32[]{:S(2)}) collective-permute-start(bf16[136,1024]{1,0:T(8,128)(2,1)S(1)} %shard_map.102.after.t0), channel_id=1, source_target_pairs={{0,16},{8,120},{16,32},{24,8},{32,48},{40,24},{48,64},{56,40},{64,... | collective-permute-start | bytes 835592 | tf_op jit(solution)/shard_map/ppermute | solution.py:34
  16.4 23.0 %collective-permute-start.1 = (bf16[264,1024]{1,0:T(8,128)(2,1)S(1)}, bf16[264,1024]{1,0:T(8,128)(2,1)S(1)}, u32[]{:S(2)}, u32[]{:S(2)}) collective-permute-start(bf16[264,1024]{1,0:T(8,128)(2,1)S(1)} %get-tuple-element.33.c0), channel_id=1, source_target_pairs={{0,384},{8,136},{16,400},{24,152},{32,416},{40,168},{48,432},{56,1... | collective-permute-start | bytes 1622024 | tf_op jit(solution)/shard_map/ppermute | solution.py:34
  21.3 21.5 %collective-permute-start.2 = (bf16[264,1024]{1,0:T(8,128)(2,1)S(1)}, bf16[264,1024]{1,0:T(8,128)(2,1)S(1)}, u32[]{:S(2)}, u32[]{:S(2)}) collective-permute-start(bf16[264,1024]{1,0:T(8,128)(2,1)S(1)} %collective-permute-done.c1), channel_id=1, source_target_pairs={{0,128},{8,392},{16,144},{24,408},{32,160},{40,424},{48,176},{56,4... | collective-permute-start | bytes 1622024 | tf_op jit(solution)/shard_map/ppermute | solution.py:34
  26.9 12.5 %collective-permute-start.4 = (bf16[136,1024]{1,0:T(8,128)(2,1)S(1)}, bf16[136,1024]{1,0:T(8,128)(2,1)S(1)}, u32[]{:S(2)}, u32[]{:S(2)}) collective-permute-start(bf16[136,1024]{1,0:T(8,128)(2,1)S(1)} %shard_map.102.after.t0), channel_id=1, source_target_pairs={{0,112},{8,24},{16,0},{24,40},{32,16},{40,56},{48,32},{56,72},{64,... | collective-permute-start | bytes 835592 | tf_op jit(solution)/shard_map/ppermute | solution.py:34
  33.1 9.7 %collective-permute-start.5 = (bf16[136,1024]{1,0:T(8,128)(2,1)S(1)}, bf16[136,1024]{1,0:T(8,128)(2,1)S(1)}, u32[]{:S(2)}, u32[]{:S(2)}) collective-permute-start(bf16[136,1024]{1,0:T(8,128)(2,1)S(1)} %collective-permute-done.3.t1), channel_id=1, source_target_pairs={{0,16},{8,120},{16,32},{24,8},{32,48},{40,24},{48,64},{56,40},{64,... | collective-permute-start | bytes 835592 | tf_op jit(solution)/shard_map/ppermute | solution.py:34
  44.6 26.5 %collective-permute-start.6 = (bf16[512,1024]{1,0:T(8,128)(2,1)S(1)}, bf16[512,1024]{1,0:T(8,128)(2,1)}, u32[]{:S(2)}, u32[]{:S(2)}) collective-permute-start(bf16[512,1024]{1,0:T(8,128)(2,1)S(1)} %get-tuple-element.34.own), channel_id=1, source_target_pairs={{0,8},{8,0},{16,24},{24,16},{32,40},{40,32},{48,56},{56,48},{64,72... | collective-permute-start | bytes 3145736 | tf_op jit(solution)/shard_map/ppermute | solution.py:34
  46.5 43.2 %collective-permute-start.11 = (bf16[544,1024]{1,0:T(8,128)(2,1)S(1)}, bf16[544,1024]{1,0:T(8,128)(2,1)S(1)}, u32[]{:S(2)}, u32[]{:S(2)}) collective-permute-start(bf16[544,1024]{1,0:T(8,128)(2,1)S(1)} %get-tuple-element.41.own), channel_id=1, source_target_pairs={{0,8},{8,0},{16,24},{24,16},{32,40},{40,32},{48,56},{56,48},{64,72... | collective-permute-start | bytes 3342344 | tf_op jit(solution)/shard_map/ppermute | solution.py:34
  49.0 10.6 %collective-permute-start.9 = (bf16[136,1024]{1,0:T(8,128)(2,1)S(1)}, bf16[136,1024]{1,0:T(8,128)(2,1)}, u32[]{:S(2)}, u32[]{:S(2)}) collective-permute-start(bf16[136,1024]{1,0:T(8,128)(2,1)S(1)} %collective-permute-done.4.t2), channel_id=1, source_target_pairs={{0,112},{8,24},{16,0},{24,40},{32,16},{40,56},{48,32},{56,72},{64,... | collective-permute-start | bytes 835592 | tf_op jit(solution)/shard_map/ppermute | solution.py:34
  51.2 10.3 %collective-permute-start.7 = (bf16[136,1024]{1,0:T(8,128)(2,1)S(1)}, bf16[136,1024]{1,0:T(8,128)(2,1)}, u32[]{:S(2)}, u32[]{:S(2)}) collective-permute-start(bf16[136,1024]{1,0:T(8,128)(2,1)S(1)} %collective-permute-done.5.t3), channel_id=1, source_target_pairs={{0,16},{8,120},{16,32},{24,8},{32,48},{40,24},{48,64},{56,40},{64,... | collective-permute-start | bytes 835592 | tf_op jit(solution)/shard_map/ppermute | solution.py:34
  59.5 11.6 %collective-permute-start.10 = (bf16[136,1024]{1,0:T(8,128)(2,1)}, bf16[136,1024]{1,0:T(8,128)(2,1)}, u32[]{:S(2)}, u32[]{:S(2)}) collective-permute-start(bf16[136,1024]{1,0:T(8,128)(2,1)} %collective-permute-done.9.t4), channel_id=1, source_target_pairs={{0,112},{8,24},{16,0},{24,40},{32,16},{40,56},{48,32},{56,72},{64,... | collective-permute-start | bytes 835592 | tf_op jit(solution)/shard_map/ppermute | solution.py:34
  61.4 16.3 %collective-permute-start.8 = (bf16[136,1024]{1,0:T(8,128)(2,1)}, bf16[136,1024]{1,0:T(8,128)(2,1)S(1)}, u32[]{:S(2)}, u32[]{:S(2)}) collective-permute-start(bf16[136,1024]{1,0:T(8,128)(2,1)} %collective-permute-done.7.t5), channel_id=1, source_target_pairs={{0,16},{8,120},{16,32},{24,8},{32,48},{40,24},{48,64},{56,40},{64,... | collective-permute-start | bytes 835592 | tf_op jit(solution)/shard_map/ppermute | solution.py:34
  82.6 16.2 %all-to-all-start = ((bf16[8,64,128]{2,1,0:T(8,128)(2,1)}), bf16[8,64,128]{2,1,0:T(8,128)(2,1)S(1)}, u32[]{:S(2)}, u32[]{:S(2)}) async-start(bf16[8,64,128]{2,1,0:T(8,128)(2,1)} %get-tuple-element.40), calls=%async_computation | async-start | bytes 262144 | tf_op jit(solution)/shard_map/all_to_all | solution.py:460
  123.0 10.9 %collective-permute-start.18 = (bf16[128,1024]{1,0:T(8,128)(2,1)S(1)}, bf16[128,1024]{1,0:T(8,128)(2,1)S(1)}, u32[]{:S(2)}, u32[]{:S(2)}) collective-permute-start(bf16[128,1024]{1,0:T(8,128)(2,1)S(1)} %add_convert_fusion.5), channel_id=1, source_target_pairs={{0,112},{8,24},{16,0},{24,40},{32,16},{40,56},{48,32},{56,72},{64,... | collective-permute-start | bytes 786440 | tf_op jit(solution)/shard_map/ppermute | solution.py:34
  128.7 11.6 %collective-permute-start.15 = (bf16[128,1024]{1,0:T(8,128)(2,1)S(1)}, bf16[128,1024]{1,0:T(8,128)(2,1)S(1)}, u32[]{:S(2)}, u32[]{:S(2)}) collective-permute-start(bf16[128,1024]{1,0:T(8,128)(2,1)S(1)} %add_convert_fusion.7), channel_id=1, source_target_pairs={{0,16},{8,120},{16,32},{24,8},{32,48},{40,24},{48,64},{56,40},{64,... | collective-permute-start | bytes 786440 | tf_op jit(solution)/shard_map/ppermute | solution.py:34
  140.5 11.8 %collective-permute-start.19 = (bf16[128,1024]{1,0:T(8,128)(2,1)S(1)}, bf16[128,1024]{1,0:T(8,128)(2,1)S(1)}, u32[]{:S(2)}, u32[]{:S(2)}) collective-permute-start(bf16[128,1024]{1,0:T(8,128)(2,1)S(1)} %subtract_convert_fusion.refs_0_), channel_id=1, source_target_pairs={{0,16},{8,120},{16,32},{24,8},{32,48},{40,24},{48,64},{56,40},{64,... | collective-permute-start | bytes 786440 | tf_op jit(solution)/shard_map/ppermute | solution.py:34
  142.4 11.8 %collective-permute-start.23 = (bf16[128,1024]{1,0:T(8,128)(2,1)S(1)}, bf16[128,1024]{1,0:T(8,128)(2,1)S(1)}, u32[]{:S(2)}, u32[]{:S(2)}) collective-permute-start(bf16[128,1024]{1,0:T(8,128)(2,1)S(1)} %subtract_convert_fusion.refs_0_), channel_id=1, source_target_pairs={{0,112},{8,24},{16,0},{24,40},{32,16},{40,56},{48,32},{56,72},{64,... | collective-permute-start | bytes 786440 | tf_op jit(solution)/shard_map/ppermute | solution.py:34
  152.3 10.9 %collective-permute-start.20 = (bf16[128,1024]{1,0:T(8,128)(2,1)S(1)}, bf16[128,1024]{1,0:T(8,128)(2,1)S(1)}, u32[]{:S(2)}, u32[]{:S(2)}) collective-permute-start(bf16[128,1024]{1,0:T(8,128)(2,1)S(1)} %collective-permute-done.19.refs_1_), channel_id=1, source_target_pairs={{0,16},{8,120},{16,32},{24,8},{32,48},{40,24},{48,64},{56,40},{64,... | collective-permute-start | bytes 786440 | tf_op jit(solution)/shard_map/ppermute | solution.py:34
  154.2 11.2 %collective-permute-start.24 = (bf16[128,1024]{1,0:T(8,128)(2,1)S(1)}, bf16[128,1024]{1,0:T(8,128)(2,1)S(1)}, u32[]{:S(2)}, u32[]{:S(2)}) collective-permute-start(bf16[128,1024]{1,0:T(8,128)(2,1)S(1)} %collective-permute-done.23.refs_2_), channel_id=1, source_target_pairs={{0,112},{8,24},{16,0},{24,40},{32,16},{40,56},{48,32},{56,72},{64,... | collective-permute-start | bytes 786440 | tf_op jit(solution)/shard_map/ppermute | solution.py:34
  197.9 11.3 %collective-permute-start.26 = (bf16[4,136,1024]{2,1,0:T(8,128)(2,1)S(1)}, bf16[4,136,1024]{2,1,0:T(8,128)(2,1)S(1)}, u32[]{:S(2)}, u32[]{:S(2)}) collective-permute-start(bf16[4,136,1024]{2,1,0:T(8,128)(2,1)S(1)} %shard_map.115), channel_id=1, source_target_pairs={{0,8},{8,0},{16,24},{24,16},{32,40},{40,32},{48,56},{56,48},{64,72... | collective-permute-start | bytes 3342344 | tf_op jit(solution)/shard_map/ppermute | solution.py:34
  201.8 14.9 %collective-permute-start.27 = (bf16[4,128,1024]{2,1,0:T(8,128)(2,1)S(1)}, bf16[4,128,1024]{2,1,0:T(8,128)(2,1)}, u32[]{:S(2)}, u32[]{:S(2)}) collective-permute-start(bf16[4,128,1024]{2,1,0:T(8,128)(2,1)S(1)} %shard_map.117.after), channel_id=1, source_target_pairs={{0,8},{8,0},{16,24},{24,16},{32,40},{40,32},{48,56},{56,48},{64,72... | collective-permute-start | bytes 3145736 | tf_op jit(solution)/shard_map/ppermute | solution.py:34
  210.7 35.4 %all-to-all-start.2 = ((bf16[4,136,1024]{2,1,0:T(8,128)(2,1)}), bf16[4,136,1024]{2,1,0:T(8,128)(2,1)S(1)}, u32[]{:S(2)}, u32[]{:S(2)}) async-start(bf16[4,136,1024]{2,1,0:T(8,128)(2,1)} %add_convert_fusion), calls=%async_computation.2 | async-start | bytes 2228224 | tf_op jit(solution)/shard_map/all_to_all | solution.py:425
  218.1 17.5 %collective-permute-start.29 = (bf16[128,1024]{1,0:T(8,128)(2,1)S(1)}, bf16[128,1024]{1,0:T(8,128)(2,1)S(1)}, u32[]{:S(2)}, u32[]{:S(2)}) collective-permute-start(bf16[128,1024]{1,0:T(8,128)(2,1)S(1)} %get-tuple-element.62), channel_id=1, source_target_pairs={{0,128},{8,392},{16,144},{24,408},{32,160},{40,424},{48,176},{56,4... | collective-permute-start | bytes 786440 | tf_op jit(solution)/shard_map/ppermute | solution.py:34
  220.1 21.1 %collective-permute-start.28 = (bf16[128,1024]{1,0:T(8,128)(2,1)S(1)}, bf16[128,1024]{1,0:T(8,128)(2,1)S(1)}, u32[]{:S(2)}, u32[]{:S(2)}) collective-permute-start(bf16[128,1024]{1,0:T(8,128)(2,1)S(1)} %get-tuple-element.63), channel_id=1, source_target_pairs={{0,384},{8,136},{16,400},{24,152},{32,416},{40,168},{48,432},{56,1... | collective-permute-start | bytes 786440 | tf_op jit(solution)/shard_map/ppermute | solution.py:34
  (31 other events, 243.4 us)

commit v7 on v5

--- a/solution.py
+++ b/solution.py
@@ -144,10 +144,10 @@
     return tok
 
 
-def score_body(pos, own, other, first, exts, t4, t5, t6, picks, where, rows):
-    some = [exts[8 * i : 8 * i + 8, :] for i in range(4)] + [t[R : R + 8, 0:384].astype(F32) for t in (t4, t5, t6)]
+def score_body(pos, own, other, first, exts, t4, t5, picks, where, rows):
+    some = [exts[8 * i : 8 * i + 8, :] for i in range(4)] + [t[R : R + 8, 0:384].astype(F32) for t in (t4, t5)]
     rows[...] = score_some(
-        pos, own, other, [first[...]] + [t[0:R, :] for t in (t4, t5, t6)], some, picks, where
+        pos, own, other, [first[...]] + [t[0:R, :] for t in (t4, t5)], some, picks, where
     )
 
 
@@ -208,8 +208,9 @@
     return jnp.concatenate(out, axis=0)
 
 
-def send_body(pos, own, other, t7, p0, w0, gram, out, where, ranks, p1, w1):
-    score_some(pos, own, other, [t7[0:R, :]], [t7[R : R + 8, 0:384].astype(F32)], p1, w1)
+def send_body(pos, own, other, t6, t7, p0, w0, gram, out, where, ranks, p1, w1):
+    late = (t6, t7)
+    score_some(pos, own, other, [t[0:R, :] for t in late], [t[R : R + 8, 0:384].astype(F32) for t in late], p1, w1)
     picks = jnp.concatenate([p0[...], p1[...]], axis=0)
     at = jnp.concatenate([w0[...], w1[...]], axis=0)
     where[...] = at
@@ -262,7 +263,7 @@
     return halves[0] + halves[1]
 
 
-def act_body(got, own, other, where, ranks, act, at_t, act_t, gram_rows, out):
+def act_body(got, own, other, where, ranks, act, at_t, act_t, gram_rows, out7, out5):
     pre = unsqueeze(total(got, 0, 32), ranks[...])
     bias = []
     for table in (own, other):
@@ -286,7 +287,9 @@
     high = rows.astype(BF)
     gram_rows[0:16, :] = high
     gram_rows[16:32, :] = (rows - high.astype(F32)).astype(BF)
-    out[...] = decode(turned, value_t, own, other, (7,)).astype(BF)
+    sums = decode(turned, value_t, own, other, (7, 5)).astype(BF)
+    out7[...] = sums[:R, :]
+    out5[...] = sums[R:, :]
 
 
 def decode_body(ms):
@@ -309,11 +312,12 @@
     return parts
 
 
-def load_rows(most, last, rows, sem):
-    copies = [
-        pltpu.make_async_copy(most, rows.at[pl.ds(0, 7 * R)], sem.at[0]),
-        pltpu.make_async_copy(last.at[pl.ds(0, R)], rows.at[pl.ds(7 * R, R)], sem.at[1]),
-    ]
+def load_rows(most, late, rows, sem):
+    first = 8 - len(late)
+    copies = [pltpu.make_async_copy(most, rows.at[pl.ds(0, first * R)], sem.at[0])]
+    for i, ref in enumerate(late):
+        to = rows.at[pl.ds((first + i) * R, R)]
+        copies.append(pltpu.make_async_copy(ref.at[pl.ds(0, R)], to, sem.at[1 + i]))
     for copy in copies:
         copy.start()
     return copies
@@ -331,7 +335,7 @@
 
 def fitted_body(half):
     def body(at, act, after, most, last, out, rows, sem):
-        copies = load_rows(most, last, rows, sem)
+        copies = load_rows(most, (last,), rows, sem)
         parts = [jnp.concatenate(turned_table(at, act, 4 * half + q), axis=1).astype(BF) for q in range(4)]
         table = jnp.concatenate(parts, axis=0)
         for copy in copies:
@@ -342,9 +346,9 @@
 
 
 def encgrad_body(half):
-    def body(got, at, ranks, most, last, *rest):
+    def body(got, at, ranks, most, t6, t7, *rest):
         out, (rows, sem) = rest[0], rest[-2:]
-        copies = load_rows(most, last, rows, sem)
+        copies = load_rows(most, (t6, t7), rows, sem)
         grad = jnp.where(at[...] >= 0, unsqueeze(total(got, 0, 32), ranks[...]) * LOSS_GRAD, 0.0)
         if half == 0:
             gram = rest[1]
@@ -436,32 +440,31 @@
     dec_other = move(dec_own, dc=1)
 
     pick_most, where_most, tok_most = call(
-        score_body, (sds((112, 128), F32), sds((112, 128), I32), sds((7 * R, 1024), BF)),
-        pos, enc_own, enc_other, tok_first, tok_exts, *tok[4:7], specs=[SMEM_SPEC] + whole(7),
+        score_body, (sds((96, 128), F32), sds((96, 128), I32), sds((6 * R, 1024), BF)),
+        pos, enc_own, enc_other, tok_first, tok_exts, *tok[4:6], specs=[SMEM_SPEC] + whole(6),
     )
     out, where, ranks = call(
         send_body, (sds((NY, 64, 128), BF), sds((R, R), I32), sds((64, R), I32)),
-        pos, enc_own, enc_other, tok[7], pick_most, where_most, gram_part, specs=[SMEM_SPEC] + whole(6),
-        scratch=[pltpu.VMEM((16, 128), F32), pltpu.VMEM((16, 128), I32)],
+        pos, enc_own, enc_other, *tok[6:8], pick_most, where_most, gram_part, specs=[SMEM_SPEC] + whole(7),
+        scratch=[pltpu.VMEM((32, 128), F32), pltpu.VMEM((32, 128), I32)],
     )
     got = lax.all_to_all(out, "width", split_axis=0, concat_axis=0, tiled=True)
 
-    act, at_t, act_t, gram_rows, d7 = call(
+    act, at_t, act_t, gram_rows, d7, d5 = call(
         act_body,
-        (sds((R, R), F32), sds((R, R), I32), sds((R, R), F32), sds((32, 128), BF), sds((R, 1024), BF)),
+        (sds((R, R), F32), sds((R, R), I32), sds((R, R), F32), sds((32, 128), BF), sds((R, 1024), BF), sds((R, 1024), BF)),
         got, dec_own, dec_other, where, ranks, specs=whole(5),
     )
 
-    def decoded(ms, dtype=BF):
+    def decoded(ms, last=BF):
         return call(
-            decode_body(ms), tuple(sds((R, 1024), dtype) for _ in ms),
+            decode_body(ms), (sds((R, 1024), BF), sds((R, 1024), last)),
             at_t, act_t, dec_own, dec_other, specs=whole(4),
         )
 
-    d5, d6 = decoded((5, 6))
-    d3, d4 = decoded((3, 4))
-    d1, d2 = decoded((1, 2))
-    (d0,) = decoded((0,), F32)
+    d6, d3 = decoded((6, 3))
+    d4, d1 = decoded((4, 1))
+    d2, d0 = decoded((2, 0), F32)
     f = move(d7, dz=1)
     b = move(d5, dz=-1)
     f = move(add(d6, f), dz=1)
@@ -487,7 +490,7 @@
     out2 = call(resend_body, sds((NY, 64, 128), BF), back_most, back_last, where, ranks, gram_rows, specs=whole(5))
     got2 = lax.all_to_all(out2, "width", split_axis=0, concat_axis=0, tiled=True)
 
-    scratch = [pltpu.VMEM((8 * R, 1024), BF), pltpu.SemaphoreType.DMA((2,))]
+    scratch = [pltpu.VMEM((8 * R, 1024), BF), pltpu.SemaphoreType.DMA((3,))]
 
     def fitted(half, after):
         return call(
@@ -503,8 +506,8 @@
     def encgrad(half):
         outs = [sds((4, R + 8, 1024), BF)] + ([sds((R, R), F32)] if half == 0 else [])
         return call(
-            encgrad_body(half), tuple(outs), got2, where, ranks, tok_most, tok[7],
-            specs=whole(3) + [ANY_SPEC] * 2, scratch=scratch,
+            encgrad_body(half), tuple(outs), got2, where, ranks, tok_most, *tok[6:8],
+            specs=whole(3) + [ANY_SPEC] * 3, scratch=scratch,
         )
 
     (eg_other,) = encgrad(1)

time: 236 us -> 235 us (level)
    pallas_call x19 -> x18, Pallas kernels: 32.2 us -> 30.8 us  [call(): pl.pallas_call(body, out_shape=outs, in_specs=specs, scratch_shapes=scrat...]
  transfers between devices with their start and end apart: 36 -> 36, of which waited for: 19 -> 19; matrix products, arithmetic and copies ran while one was open for 2% -> 2% of each run, Pallas kernels for 12% -> 11%
where the time goes in v7:
time: 235 us; the launch traced here: 231 us
  starting transfers between devices  124 us (53%)
  waiting for transfers between devices  58.9 us (25%)
  Pallas kernels  30.8 us (13%)
  local copies, waits for them, and re-layouts  10.2 us (4%)
  other arithmetic  5.15 us (2%)
    ppermute x34, starting transfers between devices, move(): return lax.ppermute(value, 'atoms', _perm(**shift))  113 us
    ppermute x34, waiting for transfers between devices, move(): return lax.ppermute(value, 'atoms', _perm(**shift))  47 us
    pallas_call x18, Pallas kernels, call(): pl.pallas_call(body, out_shape=outs, in_specs=specs, scratch_shapes=scrat...  30.8 us
    unnamed x39, local copies, waits for them, and re-layouts  9.69 us
    all_to_all x1, waiting for transfers between devices, per_device(): got = lax.all_to_all(out, 'width', split_axis=0, concat_axis=0, tiled=True)  9.21 us
    all_to_all x1, starting transfers between devices, per_device(): got = lax.all_to_all(out, 'width', split_axis=0, concat_axis=0, tiled=True)  7.11 us
  transfers between devices with their start and end apart: 36, of which 19 were waited for; matrix products, arithmetic and copies ran while one was open for 2% of the time, Pallas kernels for 11%

profile of v7, /device:TPU:6, one launch (start us, length us, event | category | flops | bytes accessed | tf_op | source)
XLA Modules:
  0.0 230.9 jit_solution(17649619530707389417)
XLA Ops:
  6.1 7.7 %collective-permute-start = (bf16[264,1024]{1,0:T(8,128)(2,1)S(1)}, bf16[264,1024]{1,0:T(8,128)(2,1)S(1)}, u32[]{:S(2)}, u32[]{:S(2)}) collective-permute-start(bf16[264,1024]{1,0:T(8,128)(2,1)S(1)} %get-tuple-element.34.c0), channel_id=1, source_target_pairs={{0,128},{8,392},{16,144},{24,408},{32,160},{40,424},{48,176},{56,4... | collective-permute-start | bytes 1622024 | tf_op jit(solution)/shard_map/ppermute | solution.py:34
  20.7 5.6 %collective-permute-start.2 = (bf16[264,1024]{1,0:T(8,128)(2,1)S(1)}, bf16[264,1024]{1,0:T(8,128)(2,1)S(1)}, u32[]{:S(2)}, u32[]{:S(2)}) collective-permute-start(bf16[264,1024]{1,0:T(8,128)(2,1)S(1)} %collective-permute-done.c1), channel_id=1, source_target_pairs={{0,128},{8,392},{16,144},{24,408},{32,160},{40,424},{48,176},{56,4... | collective-permute-start | bytes 1622024 | tf_op jit(solution)/shard_map/ppermute | solution.py:34
  26.3 6.2 %collective-permute-start.4 = (bf16[136,1024]{1,0:T(8,128)(2,1)S(1)}, bf16[136,1024]{1,0:T(8,128)(2,1)S(1)}, u32[]{:S(2)}, u32[]{:S(2)}) collective-permute-start(bf16[136,1024]{1,0:T(8,128)(2,1)S(1)} %shard_map.102.after.t0), channel_id=1, source_target_pairs={{0,112},{8,24},{16,0},{24,40},{32,16},{40,56},{48,32},{56,72},{64,... | collective-permute-start | bytes 835592 | tf_op jit(solution)/shard_map/ppermute | solution.py:34
  34.4 4.3 %collective-permute-done.4.t2 = bf16[136,1024]{1,0:T(8,128)(2,1)S(1)} collective-permute-done((bf16[136,1024]{1,0:T(8,128)(2,1)S(1)}, bf16[136,1024]{1,0:T(8,128)(2,1)S(1)}, u32[]{:S(2)}, u32[]{:S(2)}) %collective-permute-start.4) | collective-permute-done | bytes 278560 | tf_op jit(solution)/shard_map/ppermute | solution.py:34
  49.9 3.6 %collective-permute-start.9 = (bf16[136,1024]{1,0:T(8,128)(2,1)S(1)}, bf16[136,1024]{1,0:T(8,128)(2,1)}, u32[]{:S(2)}, u32[]{:S(2)}) collective-permute-start(bf16[136,1024]{1,0:T(8,128)(2,1)S(1)} %collective-permute-done.5.t3), channel_id=1, source_target_pairs={{0,16},{8,120},{16,32},{24,8},{32,48},{40,24},{48,64},{56,40},{64,... | collective-permute-start | bytes 835592 | tf_op jit(solution)/shard_map/ppermute | solution.py:34
  53.6 4.7 %collective-permute-done.7.t4 = bf16[136,1024]{1,0:T(8,128)(2,1)} collective-permute-done((bf16[136,1024]{1,0:T(8,128)(2,1)S(1)}, bf16[136,1024]{1,0:T(8,128)(2,1)}, u32[]{:S(2)}, u32[]{:S(2)}) %collective-permute-start.7) | collective-permute-done | bytes 278560 | tf_op jit(solution)/shard_map/ppermute | solution.py:34
  60.2 3.9 %collective-permute-start.10 = (bf16[136,1024]{1,0:T(8,128)(2,1)}, bf16[136,1024]{1,0:T(8,128)(2,1)}, u32[]{:S(2)}, u32[]{:S(2)}) collective-permute-start(bf16[136,1024]{1,0:T(8,128)(2,1)} %collective-permute-done.9.t5), channel_id=1, source_target_pairs={{0,16},{8,120},{16,32},{24,8},{32,48},{40,24},{48,64},{56,40},{64,... | collective-permute-start | bytes 835592 | tf_op jit(solution)/shard_map/ppermute | solution.py:34
  65.4 3.8 %shard_map.105 = (f32[96,128]{1,0:T(8,128)S(1)}, s32[96,128]{1,0:T(8,128)S(1)}, bf16[768,1024]{1,0:T(8,128)(2,1)S(1)}) custom-call(s32[3]{0:T(128)S(1)} %pad_add_fusion.pos, bf16[512,1024]{1,0:T(8,128)(2,1)S(1)} %get-tuple-element.35.own, bf16[512,1024]{1,0:T(8,128)(2,1)} %collective-permute-done.6.other, bf16[512,1024]{1,0:T(8,128)(2,1)S(1)} %copy-done.14, ...), custom_call_target="tpu_custom_call" | custom-call | tf_op jit(solution)/shard_map/pallas_call | solution.py:38
  70.1 3.6 %shard_map.106 = (bf16[8,64,128]{2,1,0:T(8,128)(2,1)}, s32[128,128]{1,0:T(8,128)S(1)}, s32[64,128]{1,0:T(8,128)S(1)}) custom-call(s32[3]{0:T(128)S(1)} %pad_add_fusion.pos, bf16[512,1024]{1,0:T(8,128)(2,1)S(1)} %get-tuple-element.35.own, bf16[512,1024]{1,0:T(8,128)(2,1)} %collective-permute-done.6.other, bf16[136,1024]{1,0:T(8,128)(2,1)} %collective-permute-done.8.t6, ...), custom_call_target="tpu_custom_call" | custom-call | tf_op jit(solution)/shard_map/pallas_call | solution.py:38
  73.7 7.1 %all-to-all-start = ((bf16[8,64,128]{2,1,0:T(8,128)(2,1)}), bf16[8,64,128]{2,1,0:T(8,128)(2,1)S(1)}, u32[]{:S(2)}, u32[]{:S(2)}) async-start(bf16[8,64,128]{2,1,0:T(8,128)(2,1)} %get-tuple-element.41), calls=%async_computation | async-start | bytes 262144 | tf_op jit(solution)/shard_map/all_to_all | solution.py:451
  80.8 9.2 %all-to-all-done.got = bf16[8,64,128]{2,1,0:T(8,128)(2,1)S(1)} async-done(((bf16[8,64,128]{2,1,0:T(8,128)(2,1)}), bf16[8,64,128]{2,1,0:T(8,128)(2,1)S(1)}, u32[]{:S(2)}, u32[]{:S(2)}) %all-to-all-start) | async-done | bytes 131104 | tf_op jit(solution)/shard_map/all_to_all | solution.py:451
  94.5 4.5 %collective-permute-start.16 = (bf16[128,1024]{1,0:T(8,128)(2,1)S(1)}, bf16[128,1024]{1,0:T(8,128)(2,1)S(1)}, u32[]{:S(2)}, u32[]{:S(2)}) collective-permute-start(bf16[128,1024]{1,0:T(8,128)(2,1)S(1)} %get-tuple-element.54), channel_id=1, source_target_pairs={{0,112},{8,24},{16,0},{24,40},{32,16},{40,56},{48,32},{56,72},{64,... | collective-permute-start | bytes 786440 | tf_op jit(solution)/shard_map/ppermute | solution.py:34
  108.0 5.1 %collective-permute-start.17 = (bf16[128,1024]{1,0:T(8,128)(2,1)S(1)}, bf16[128,1024]{1,0:T(8,128)(2,1)S(1)}, u32[]{:S(2)}, u32[]{:S(2)}) collective-permute-start(bf16[128,1024]{1,0:T(8,128)(2,1)S(1)} %add_convert_fusion.11), channel_id=1, source_target_pairs={{0,112},{8,24},{16,0},{24,40},{32,16},{40,56},{48,32},{56,72},{64,... | collective-permute-start | bytes 786440 | tf_op jit(solution)/shard_map/ppermute | solution.py:34
  119.5 5.1 %collective-permute-start.18 = (bf16[128,1024]{1,0:T(8,128)(2,1)S(1)}, bf16[128,1024]{1,0:T(8,128)(2,1)S(1)}, u32[]{:S(2)}, u32[]{:S(2)}) collective-permute-start(bf16[128,1024]{1,0:T(8,128)(2,1)S(1)} %add_convert_fusion.10), channel_id=1, source_target_pairs={{0,112},{8,24},{16,0},{24,40},{32,16},{40,56},{48,32},{56,72},{64,... | collective-permute-start | bytes 786440 | tf_op jit(solution)/shard_map/ppermute | solution.py:34
  128.5 6.8 %collective-permute-done.15 = bf16[128,1024]{1,0:T(8,128)(2,1)S(1)} collective-permute-done((bf16[128,1024]{1,0:T(8,128)(2,1)S(1)}, bf16[128,1024]{1,0:T(8,128)(2,1)S(1)}, u32[]{:S(2)}, u32[]{:S(2)}) %collective-permute-start.15) | collective-permute-done | bytes 262176 | tf_op jit(solution)/shard_map/ppermute | solution.py:34
  137.5 5.1 %collective-permute-start.20 = (bf16[128,1024]{1,0:T(8,128)(2,1)S(1)}, bf16[128,1024]{1,0:T(8,128)(2,1)S(1)}, u32[]{:S(2)}, u32[]{:S(2)}) collective-permute-start(bf16[128,1024]{1,0:T(8,128)(2,1)S(1)} %subtract_convert_fusion.refs_0_), channel_id=1, source_target_pairs={{0,112},{8,24},{16,0},{24,40},{32,16},{40,56},{48,32},{56,72},{64,... | collective-permute-start | bytes 786440 | tf_op jit(solution)/shard_map/ppermute | solution.py:34
  142.6 3.8 %collective-permute-done.19.refs_1_ = bf16[128,1024]{1,0:T(8,128)(2,1)S(1)} collective-permute-done((bf16[128,1024]{1,0:T(8,128)(2,1)S(1)}, bf16[128,1024]{1,0:T(8,128)(2,1)S(1)}, u32[]{:S(2)}, u32[]{:S(2)}) %collective-permute-start.19) | collective-permute-done | bytes 262176 | tf_op jit(solution)/shard_map/ppermute | solution.py:34
  148.3 5.1 %collective-permute-start.22 = (bf16[128,1024]{1,0:T(8,128)(2,1)S(1)}, bf16[128,1024]{1,0:T(8,128)(2,1)S(1)}, u32[]{:S(2)}, u32[]{:S(2)}) collective-permute-start(bf16[128,1024]{1,0:T(8,128)(2,1)S(1)} %collective-permute-done.20.refs_2_), channel_id=1, source_target_pairs={{0,112},{8,24},{16,0},{24,40},{32,16},{40,56},{48,32},{56,72},{64,... | collective-permute-start | bytes 786440 | tf_op jit(solution)/shard_map/ppermute | solution.py:34
  153.5 4.9 %collective-permute-done.21.refs_3_ = bf16[128,1024]{1,0:T(8,128)(2,1)S(1)} collective-permute-done((bf16[128,1024]{1,0:T(8,128)(2,1)S(1)}, bf16[128,1024]{1,0:T(8,128)(2,1)S(1)}, u32[]{:S(2)}, u32[]{:S(2)}) %collective-permute-start.21) | collective-permute-done | bytes 262176 | tf_op jit(solution)/shard_map/ppermute | solution.py:34
  160.3 5.1 %collective-permute-start.24 = (bf16[128,1024]{1,0:T(8,128)(2,1)S(1)}, bf16[128,1024]{1,0:T(8,128)(2,1)S(1)}, u32[]{:S(2)}, u32[]{:S(2)}) collective-permute-start(bf16[128,1024]{1,0:T(8,128)(2,1)S(1)} %collective-permute-done.22.refs_4_), channel_id=1, source_target_pairs={{0,112},{8,24},{16,0},{24,40},{32,16},{40,56},{48,32},{56,72},{64,... | collective-permute-start | bytes 786440 | tf_op jit(solution)/shard_map/ppermute | solution.py:34
  172.9 4.5 %collective-permute-done.25.refs_0_.last = bf16[128,1024]{1,0:T(8,128)(2,1)S(1)} collective-permute-done((bf16[128,1024]{1,0:T(8,128)(2,1)S(1)}, bf16[128,1024]{1,0:T(8,128)(2,1)S(1)}, u32[]{:S(2)}, u32[]{:S(2)}) %collective-permute-start.25) | collective-permute-done | bytes 262176 | tf_op jit(solution)/shard_map/ppermute | solution.py:34
  205.7 4.5 %collective-permute-start.28 = (bf16[136,1024]{1,0:T(8,128)(2,1)S(1)}, bf16[136,1024]{1,0:T(8,128)(2,1)S(1)}, u32[]{:S(2)}, u32[]{:S(2)}) collective-permute-start(bf16[136,1024]{1,0:T(8,128)(2,1)S(1)} %get-tuple-element.64), channel_id=1, source_target_pairs={{0,128},{8,392},{16,144},{24,408},{32,160},{40,424},{48,176},{56,4... | collective-permute-start | bytes 835592 | tf_op jit(solution)/shard_map/ppermute | solution.py:34
  213.2 5.1 %collective-permute-start.33 = (bf16[128,1024]{1,0:T(8,128)(2,1)S(1)}, bf16[128,1024]{1,0:T(8,128)(2,1)S(1)}, u32[]{:S(2)}, u32[]{:S(2)}) collective-permute-start(bf16[128,1024]{1,0:T(8,128)(2,1)S(1)} %add_convert_fusion.5), channel_id=1, source_target_pairs={{0,128},{8,392},{16,144},{24,408},{32,160},{40,424},{48,176},{56,4... | collective-permute-start | bytes 786440 | tf_op jit(solution)/shard_map/ppermute | solution.py:34
  220.4 5.1 %collective-permute-start.29 = (bf16[136,1024]{1,0:T(8,128)(2,1)S(1)}, bf16[136,1024]{1,0:T(8,128)(2,1)S(1)}, u32[]{:S(2)}, u32[]{:S(2)}) collective-permute-start(bf16[136,1024]{1,0:T(8,128)(2,1)S(1)} %fusion), channel_id=1, source_target_pairs={{0,128},{8,392},{16,144},{24,408},{32,160},{40,424},{48,176},{56,4... | collective-permute-start | bytes 835592 | tf_op jit(solution)/shard_map/ppermute | solution.py:34
  (118 shorter events, 104.2 us)
Async XLA Ops:
  6.1 14.6 %collective-permute-start = (bf16[264,1024]{1,0:T(8,128)(2,1)S(1)}, bf16[264,1024]{1,0:T(8,128)(2,1)S(1)}, u32[]{:S(2)}, u32[]{:S(2)}) collective-permute-start(bf16[264,1024]{1,0:T(8,128)(2,1)S(1)} %get-tuple-element.34.c0), channel_id=1, source_target_pairs={{0,128},{8,392},{16,144},{24,408},{32,160},{40,424},{48,176},{56,4... | collective-permute-start | bytes 1622024 | tf_op jit(solution)/shard_map/ppermute | solution.py:34
  13.8 18.7 %collective-permute-start.3 = (bf16[136,1024]{1,0:T(8,128)(2,1)S(1)}, bf16[136,1024]{1,0:T(8,128)(2,1)S(1)}, u32[]{:S(2)}, u32[]{:S(2)}) collective-permute-start(bf16[136,1024]{1,0:T(8,128)(2,1)S(1)} %shard_map.102.after.t0), channel_id=1, source_target_pairs={{0,16},{8,120},{16,32},{24,8},{32,48},{40,24},{48,64},{56,40},{64,... | collective-permute-start | bytes 835592 | tf_op jit(solution)/shard_map/ppermute | solution.py:34
  15.8 23.0 %collective-permute-start.1 = (bf16[264,1024]{1,0:T(8,128)(2,1)S(1)}, bf16[264,1024]{1,0:T(8,128)(2,1)S(1)}, u32[]{:S(2)}, u32[]{:S(2)}) collective-permute-start(bf16[264,1024]{1,0:T(8,128)(2,1)S(1)} %get-tuple-element.34.c0), channel_id=1, source_target_pairs={{0,384},{8,136},{16,400},{24,152},{32,416},{40,168},{48,432},{56,1... | collective-permute-start | bytes 1622024 | tf_op jit(solution)/shard_map/ppermute | solution.py:34
  20.7 21.5 %collective-permute-start.2 = (bf16[264,1024]{1,0:T(8,128)(2,1)S(1)}, bf16[264,1024]{1,0:T(8,128)(2,1)S(1)}, u32[]{:S(2)}, u32[]{:S(2)}) collective-permute-start(bf16[264,1024]{1,0:T(8,128)(2,1)S(1)} %collective-permute-done.c1), channel_id=1, source_target_pairs={{0,128},{8,392},{16,144},{24,408},{32,160},{40,424},{48,176},{56,4... | collective-permute-start | bytes 1622024 | tf_op jit(solution)/shard_map/ppermute | solution.py:34
  26.3 12.5 %collective-permute-start.4 = (bf16[136,1024]{1,0:T(8,128)(2,1)S(1)}, bf16[136,1024]{1,0:T(8,128)(2,1)S(1)}, u32[]{:S(2)}, u32[]{:S(2)}) collective-permute-start(bf16[136,1024]{1,0:T(8,128)(2,1)S(1)} %shard_map.102.after.t0), channel_id=1, source_target_pairs={{0,112},{8,24},{16,0},{24,40},{32,16},{40,56},{48,32},{56,72},{64,... | collective-permute-start | bytes 835592 | tf_op jit(solution)/shard_map/ppermute | solution.py:34
  43.4 20.8 %collective-permute-start.6 = (bf16[512,1024]{1,0:T(8,128)(2,1)S(1)}, bf16[512,1024]{1,0:T(8,128)(2,1)}, u32[]{:S(2)}, u32[]{:S(2)}) collective-permute-start(bf16[512,1024]{1,0:T(8,128)(2,1)S(1)} %get-tuple-element.35.own), channel_id=1, source_target_pairs={{0,8},{8,0},{16,24},{24,16},{32,40},{40,32},{48,56},{56,48},{64,72... | collective-permute-start | bytes 3145736 | tf_op jit(solution)/shard_map/ppermute | solution.py:34
  45.3 35.6 %collective-permute-start.11 = (bf16[544,1024]{1,0:T(8,128)(2,1)S(1)}, bf16[544,1024]{1,0:T(8,128)(2,1)S(1)}, u32[]{:S(2)}, u32[]{:S(2)}) collective-permute-start(bf16[544,1024]{1,0:T(8,128)(2,1)S(1)} %get-tuple-element.42.own), channel_id=1, source_target_pairs={{0,8},{8,0},{16,24},{24,16},{32,40},{40,32},{48,56},{56,48},{64,72... | collective-permute-start | bytes 3342344 | tf_op jit(solution)/shard_map/ppermute | solution.py:34
  58.2 11.6 %collective-permute-start.8 = (bf16[136,1024]{1,0:T(8,128)(2,1)}, bf16[136,1024]{1,0:T(8,128)(2,1)}, u32[]{:S(2)}, u32[]{:S(2)}) collective-permute-start(bf16[136,1024]{1,0:T(8,128)(2,1)} %collective-permute-done.7.t4), channel_id=1, source_target_pairs={{0,112},{8,24},{16,0},{24,40},{32,16},{40,56},{48,32},{56,72},{64,... | collective-permute-start | bytes 835592 | tf_op jit(solution)/shard_map/ppermute | solution.py:34
  73.7 16.3 %all-to-all-start = ((bf16[8,64,128]{2,1,0:T(8,128)(2,1)}), bf16[8,64,128]{2,1,0:T(8,128)(2,1)S(1)}, u32[]{:S(2)}, u32[]{:S(2)}) async-start(bf16[8,64,128]{2,1,0:T(8,128)(2,1)} %get-tuple-element.41), calls=%async_computation | async-start | bytes 262144 | tf_op jit(solution)/shard_map/all_to_all | solution.py:451
  91.9 12.1 %collective-permute-start.12 = (bf16[128,1024]{1,0:T(8,128)(2,1)S(1)}, bf16[128,1024]{1,0:T(8,128)(2,1)S(1)}, u32[]{:S(2)}, u32[]{:S(2)}) collective-permute-start(bf16[128,1024]{1,0:T(8,128)(2,1)S(1)} %get-tuple-element.51), channel_id=1, source_target_pairs={{0,16},{8,120},{16,32},{24,8},{32,48},{40,24},{48,64},{56,40},{64,... | collective-permute-start | bytes 786440 | tf_op jit(solution)/shard_map/ppermute | solution.py:34
  94.5 13.4 %collective-permute-start.16 = (bf16[128,1024]{1,0:T(8,128)(2,1)S(1)}, bf16[128,1024]{1,0:T(8,128)(2,1)S(1)}, u32[]{:S(2)}, u32[]{:S(2)}) collective-permute-start(bf16[128,1024]{1,0:T(8,128)(2,1)S(1)} %get-tuple-element.54), channel_id=1, source_target_pairs={{0,112},{8,24},{16,0},{24,40},{32,16},{40,56},{48,32},{56,72},{64,... | collective-permute-start | bytes 786440 | tf_op jit(solution)/shard_map/ppermute | solution.py:34
  104.1 11.2 %collective-permute-start.13 = (bf16[128,1024]{1,0:T(8,128)(2,1)S(1)}, bf16[128,1024]{1,0:T(8,128)(2,1)S(1)}, u32[]{:S(2)}, u32[]{:S(2)}) collective-permute-start(bf16[128,1024]{1,0:T(8,128)(2,1)S(1)} %add_convert_fusion.14), channel_id=1, source_target_pairs={{0,16},{8,120},{16,32},{24,8},{32,48},{40,24},{48,64},{56,40},{64,... | collective-permute-start | bytes 786440 | tf_op jit(solution)/shard_map/ppermute | solution.py:34
  108.0 11.4 %collective-permute-start.17 = (bf16[128,1024]{1,0:T(8,128)(2,1)S(1)}, bf16[128,1024]{1,0:T(8,128)(2,1)S(1)}, u32[]{:S(2)}, u32[]{:S(2)}) collective-permute-start(bf16[128,1024]{1,0:T(8,128)(2,1)S(1)} %add_convert_fusion.11), channel_id=1, source_target_pairs={{0,112},{8,24},{16,0},{24,40},{32,16},{40,56},{48,32},{56,72},{64,... | collective-permute-start | bytes 786440 | tf_op jit(solution)/shard_map/ppermute | solution.py:34
  135.5 10.9 %collective-permute-start.19 = (bf16[128,1024]{1,0:T(8,128)(2,1)S(1)}, bf16[128,1024]{1,0:T(8,128)(2,1)S(1)}, u32[]{:S(2)}, u32[]{:S(2)}) collective-permute-start(bf16[128,1024]{1,0:T(8,128)(2,1)S(1)} %subtract_convert_fusion.refs_0_), channel_id=1, source_target_pairs={{0,16},{8,120},{16,32},{24,8},{32,48},{40,24},{48,64},{56,40},{64,... | collective-permute-start | bytes 786440 | tf_op jit(solution)/shard_map/ppermute | solution.py:34
  137.5 10.9 %collective-permute-start.20 = (bf16[128,1024]{1,0:T(8,128)(2,1)S(1)}, bf16[128,1024]{1,0:T(8,128)(2,1)S(1)}, u32[]{:S(2)}, u32[]{:S(2)}) collective-permute-start(bf16[128,1024]{1,0:T(8,128)(2,1)S(1)} %subtract_convert_fusion.refs_0_), channel_id=1, source_target_pairs={{0,112},{8,24},{16,0},{24,40},{32,16},{40,56},{48,32},{56,72},{64,... | collective-permute-start | bytes 786440 | tf_op jit(solution)/shard_map/ppermute | solution.py:34
  146.4 12.0 %collective-permute-start.21 = (bf16[128,1024]{1,0:T(8,128)(2,1)S(1)}, bf16[128,1024]{1,0:T(8,128)(2,1)S(1)}, u32[]{:S(2)}, u32[]{:S(2)}) collective-permute-start(bf16[128,1024]{1,0:T(8,128)(2,1)S(1)} %collective-permute-done.19.refs_1_), channel_id=1, source_target_pairs={{0,16},{8,120},{16,32},{24,8},{32,48},{40,24},{48,64},{56,40},{64,... | collective-permute-start | bytes 786440 | tf_op jit(solution)/shard_map/ppermute | solution.py:34
  148.3 12.0 %collective-permute-start.22 = (bf16[128,1024]{1,0:T(8,128)(2,1)S(1)}, bf16[128,1024]{1,0:T(8,128)(2,1)S(1)}, u32[]{:S(2)}, u32[]{:S(2)}) collective-permute-start(bf16[128,1024]{1,0:T(8,128)(2,1)S(1)} %collective-permute-done.20.refs_2_), channel_id=1, source_target_pairs={{0,112},{8,24},{16,0},{24,40},{32,16},{40,56},{48,32},{56,72},{64,... | collective-permute-start | bytes 786440 | tf_op jit(solution)/shard_map/ppermute | solution.py:34
  179.3 12.4 %all-to-all-start.1 = ((bf16[8,64,128]{2,1,0:T(8,128)(2,1)}), bf16[8,64,128]{2,1,0:T(8,128)(2,1)S(1)}, u32[]{:S(2)}, u32[]{:S(2)}) async-start(bf16[8,64,128]{2,1,0:T(8,128)(2,1)} %shard_map.113.after), calls=%async_computation.1 | async-start | bytes 262144 | tf_op jit(solution)/shard_map/all_to_all | solution.py:491
  187.1 13.8 %collective-permute-start.30 = (bf16[512,1024]{1,0:T(8,128)(2,1)S(1)}, bf16[512,1024]{1,0:T(8,128)(2,1)}, u32[]{:S(2)}, u32[]{:S(2)}) collective-permute-start(bf16[512,1024]{1,0:T(8,128)(2,1)S(1)} %shard_map.117.after), channel_id=1, source_target_pairs={{0,8},{8,0},{16,24},{24,16},{32,40},{40,32},{48,56},{56,48},{64,72... | collective-permute-start | bytes 3145736 | tf_op jit(solution)/shard_map/ppermute | solution.py:34
  194.3 11.0 %collective-permute-start.26 = (bf16[4,136,1024]{2,1,0:T(8,128)(2,1)S(1)}, bf16[4,136,1024]{2,1,0:T(8,128)(2,1)S(1)}, u32[]{:S(2)}, u32[]{:S(2)}) collective-permute-start(bf16[4,136,1024]{2,1,0:T(8,128)(2,1)S(1)} %shard_map.115), channel_id=1, source_target_pairs={{0,8},{8,0},{16,24},{24,16},{32,40},{40,32},{48,56},{56,48},{64,72... | collective-permute-start | bytes 3342344 | tf_op jit(solution)/shard_map/ppermute | solution.py:34
  205.7 14.6 %collective-permute-start.28 = (bf16[136,1024]{1,0:T(8,128)(2,1)S(1)}, bf16[136,1024]{1,0:T(8,128)(2,1)S(1)}, u32[]{:S(2)}, u32[]{:S(2)}) collective-permute-start(bf16[136,1024]{1,0:T(8,128)(2,1)S(1)} %get-tuple-element.64), channel_id=1, source_target_pairs={{0,128},{8,392},{16,144},{24,408},{32,160},{40,424},{48,176},{56,4... | collective-permute-start | bytes 835592 | tf_op jit(solution)/shard_map/ppermute | solution.py:34
  210.2 16.4 %collective-permute-start.31 = (bf16[128,1024]{1,0:T(8,128)(2,1)S(1)}, bf16[128,1024]{1,0:T(8,128)(2,1)S(1)}, u32[]{:S(2)}, u32[]{:S(2)}) collective-permute-start(bf16[128,1024]{1,0:T(8,128)(2,1)S(1)} %get-tuple-element.67), channel_id=1, source_target_pairs={{0,384},{8,136},{16,400},{24,152},{32,416},{40,168},{48,432},{56,1... | collective-permute-start | bytes 786440 | tf_op jit(solution)/shard_map/ppermute | solution.py:34
  213.2 13.4 %collective-permute-start.33 = (bf16[128,1024]{1,0:T(8,128)(2,1)S(1)}, bf16[128,1024]{1,0:T(8,128)(2,1)S(1)}, u32[]{:S(2)}, u32[]{:S(2)}) collective-permute-start(bf16[128,1024]{1,0:T(8,128)(2,1)S(1)} %add_convert_fusion.5), channel_id=1, source_target_pairs={{0,128},{8,392},{16,144},{24,408},{32,160},{40,424},{48,176},{56,4... | collective-permute-start | bytes 786440 | tf_op jit(solution)/shard_map/ppermute | solution.py:34
  218.3 10.9 %collective-permute-start.27 = (bf16[136,1024]{1,0:T(8,128)(2,1)S(1)}, bf16[136,1024]{1,0:T(8,128)(2,1)S(1)}, u32[]{:S(2)}, u32[]{:S(2)}) collective-permute-start(bf16[136,1024]{1,0:T(8,128)(2,1)S(1)} %get-tuple-element.65), channel_id=1, source_target_pairs={{0,384},{8,136},{16,400},{24,152},{32,416},{40,168},{48,432},{56,1... | collective-permute-start | bytes 835592 | tf_op jit(solution)/shard_map/ppermute | solution.py:34
  (31 other events, 241.9 us)
